TPU v7x, 32 devices: a whole 2x2x4 slice. The times are simulated.
32 devices in a mesh: ctx: 8 (over z, x), wa: 4 (over y, core).
Axes of the slice: x: 2, y: 2, z: 4, core: 2. Of those that a mesh axis runs over, the one named last changes fastest.
Arguments:
- tokens: bfloat16 [4, 1024, 768], P('wa', 'ctx'), may hold values from -6 to 6
- lengths: int32 [4], P('wa'), may hold values from 513 to 1024, as said below
- qkv_weight: bfloat16 [768, 2304], P('wa'), may hold values from -0.21875 to 0.21875
- out_weight: bfloat16 [768, 768], P('wa'), may hold values from -6 to 6
- up_weight: bfloat16 [768, 3072], P('wa'), may hold values from -0.21875 to 0.21875
- down_weight: bfloat16 [3072, 768], P('wa'), may hold values from -0.109375 to 0.109375
- qv_bias: bfloat16 [1536], P('wa'), may hold values from -3 to 3
- out_bias: bfloat16 [768], P('wa'), may hold values from -3 to 3
- up_bias: bfloat16 [3072], P('wa'), may hold values from -3 to 3
- down_bias: bfloat16 [768], P('wa'), may hold values from -3 to 3
- gain_one: bfloat16 [768], P('wa'), may hold values from 0.25 to 1.75
- shift_one: bfloat16 [768], P('wa'), may hold values from -3 to 3
- gain_two: bfloat16 [768], P('wa'), may hold values from 0.25 to 1.75
- shift_two: bfloat16 [768], P('wa'), may hold values from -3 to 3
- cotangent: bfloat16 [4, 1024, 768], P('wa', 'ctx'), may hold values from -6 to 6
Outputs:
- output: bfloat16 [4, 1024, 768], P('wa', 'ctx')
- grad_tokens: bfloat16 [4, 1024, 768], P('wa', 'ctx')
- grad_qkv_weight: float32 [768, 2304], P('wa')
- grad_out_weight: float32 [768, 768], P('wa')
- grad_up_weight: float32 [768, 3072], P('wa')
- grad_down_weight: float32 [3072, 768], P('wa')
- grad_qv_bias: float32 [1536], P('wa')
- grad_out_bias: float32 [768], P('wa')
- grad_up_bias: float32 [3072], P('wa')
- grad_down_bias: float32 [768], P('wa')
- grad_gain_one: float32 [768], P('wa')
- grad_shift_one: float32 [768], P('wa')
- grad_gain_two: float32 [768], P('wa')
- grad_shift_two: float32 [768], P('wa')
Inputs may be any that keep to these rules, and one draw needn't show every extreme that they name: `lengths`: each sequence's count of valid tokens is more than half of its 1024 slots; in every draw some sequence has all 1024 valid.
All inputs are finite; a program needn't handle non-finite values.
Results may differ from a plain program's by a relative error of at most 0.015.
Values may be sent and summed in bfloat16 or wider, within the bound.
A program may use at most 192 MiB of HBM per device.

v0:
```python
from functools import partial
import math

import jax
import jax.numpy as jnp
from jax import lax
from jax.sharding import PartitionSpec as P

HEADS = 12
HEAD = 64


eps_norm = 1e-12
floor_score = -1e30


def layer_norm(summed, gain_vec, shift_vec):
    center = summed - jnp.mean(summed, -1, keepdims=True)
    spread = jnp.mean(center * center, -1, keepdims=True)
    return center * lax.rsqrt(spread + eps_norm) * gain_vec + shift_vec


def heads_of(block):
    return block.reshape(block.shape[0], block.shape[1], HEADS, HEAD)


def cut_rows(array, offset, block_width):
    return lax.dynamic_slice_in_dim(array, offset, block_width, 1)


def by_blocks(one_block, carried, total_rows):
    block_width = math.gcd(total_rows, 1024)
    block_count = total_rows // block_width
    if block_count == 1:
        return one_block(carried, 0, block_width)

    def advance(block_no, carry_in):
        return one_block(carry_in, block_no * block_width, block_width)

    return lax.fori_loop(0, block_count, advance, carried)


def body(
    tokens,
    lengths,
    qkv_weight,
    out_weight,
    up_weight,
    down_weight,
    qv_bias,
    out_bias,
    up_bias,
    down_bias,
    gain_one,
    shift_one,
    gain_two,
    shift_two,
    cotangent,
):
    shards = (
        qkv_weight,
        out_weight,
        up_weight,
        down_weight,
        qv_bias,
        out_bias,
        up_bias,
        down_bias,
        gain_one,
        shift_one,
        gain_two,
        shift_two,
    )
    gathered = (
        lax.all_gather(shards[0], "wa", axis=0, tiled=True),
        lax.all_gather(shards[1], "wa", axis=0, tiled=True),
        lax.all_gather(shards[2], "wa", axis=0, tiled=True),
        lax.all_gather(shards[3], "wa", axis=0, tiled=True),
        lax.all_gather(shards[4], "wa", axis=0, tiled=True),
        lax.all_gather(shards[5], "wa", axis=0, tiled=True),
        lax.all_gather(shards[6], "wa", axis=0, tiled=True),
        lax.all_gather(shards[7], "wa", axis=0, tiled=True),
        lax.all_gather(shards[8], "wa", axis=0, tiled=True),
        lax.all_gather(shards[9], "wa", axis=0, tiled=True),
        lax.all_gather(shards[10], "wa", axis=0, tiled=True),
        lax.all_gather(shards[11], "wa", axis=0, tiled=True),
    )
    (
        qkv_full,
        out_full,
        up_full,
        down_full,
        qv_full,
        outb_full,
        upb_full,
        downb_full,
        gone_full,
        sone_full,
        gtwo_full,
        stwo_full,
    ) = gathered
    seq_count, group_len, model_width = tokens.shape
    total_rows = seq_count * group_len
    score_scale = HEAD ** (-0.5)
    group_start = lax.axis_index("ctx") * group_len
    places = group_start + jnp.arange(group_len)
    row_live = places[None, :] < lengths[:, None]
    local_mask = row_live[:, None, None, :]
    flat_rows = tokens.reshape(total_rows, model_width)
    projected = jnp.dot(flat_rows, qkv_full, preferred_element_type=jnp.float32)
    qv_float = qv_full.astype(jnp.float32)
    queries = (
        (projected[:, :model_width] + qv_float[:model_width])
        .astype(jnp.bfloat16)
        .reshape(seq_count, group_len, model_width)
    )
    key_rows = (
        projected[:, model_width : 2 * model_width]
        .astype(jnp.bfloat16)
        .reshape(seq_count, group_len, model_width)
    )
    values = (
        (projected[:, 2 * model_width :] + qv_float[model_width:])
        .astype(jnp.bfloat16)
        .reshape(seq_count, group_len, model_width)
    )
    query_heads = heads_of(queries)
    key_heads_local = heads_of(key_rows)
    value_heads_local = heads_of(values)
    start_state = (
        jnp.full((seq_count, HEADS, group_len), floor_score, jnp.float32),
        jnp.zeros((seq_count, HEADS, group_len), jnp.float32),
        jnp.zeros((seq_count, HEADS, group_len, HEAD), jnp.float32),
    )
    begin_at = jnp.int32(0)
    piece_keys = lax.all_gather(key_rows, "ctx", axis=1, tiled=True)
    piece_values = lax.all_gather(values, "ctx", axis=1, tiled=True)

    def one_block(carry_in, offset, block_width):
        key_places = begin_at + offset + jnp.arange(block_width)
        alive_keys = key_places[None, :] < lengths[:, None]

        def compute(current):
            top_val, totals, summed = current
            key_heads = heads_of(cut_rows(piece_keys, offset, block_width))
            value_heads = heads_of(cut_rows(piece_values, offset, block_width)).astype(jnp.float32)
            scores = (
                jnp.einsum(
                    "sqhe,skhe->shqk", query_heads, key_heads, preferred_element_type=jnp.float32
                )
                * score_scale
            )
            masked = alive_keys[:, None, None, :]
            scores = jnp.where(masked, scores, floor_score)
            new_top = jnp.maximum(top_val, jnp.max(scores, -1))
            attn_prob = jnp.where(masked, jnp.exp(scores - new_top[..., None]), 0.0)
            factor = jnp.exp(top_val - new_top)
            totals = totals * factor + jnp.sum(attn_prob, -1)
            summed = summed * factor[..., None] + jnp.einsum(
                "shqk,skhe->shqe", attn_prob, value_heads, precision=lax.Precision.HIGHEST
            )
            return (new_top, totals, summed)

        return lax.cond(jnp.any(alive_keys), compute, lambda current: current, carry_in)

    top_val, totals, summed = by_blocks(one_block, start_state, piece_keys.shape[1])
    log_sum = top_val + jnp.log(totals)
    attn_float = summed / totals[..., None]
    attn_low = (
        attn_float.transpose(0, 2, 1, 3).reshape(total_rows, model_width).astype(jnp.bfloat16)
    )
    branch = jnp.dot(attn_low, out_full, preferred_element_type=jnp.float32) + outb_full.astype(
        jnp.float32
    )
    resid_one = flat_rows.astype(jnp.float32) + branch
    normed_one, norm_back_one = jax.vjp(
        layer_norm, resid_one, gone_full.astype(jnp.float32), sone_full.astype(jnp.float32)
    )
    normed_low = normed_one.astype(jnp.bfloat16)
    hidden = jnp.dot(normed_low, up_full, preferred_element_type=jnp.float32) + upb_full.astype(
        jnp.float32
    )
    activated, gelu_back = jax.vjp(partial(jax.nn.gelu, approximate=False), hidden)
    act_low = activated.astype(jnp.bfloat16)
    resid_two = (
        normed_one
        + jnp.dot(act_low, down_full, preferred_element_type=jnp.float32)
        + downb_full.astype(jnp.float32)
    )
    normed_two, norm_back_two = jax.vjp(
        layer_norm, resid_two, gtwo_full.astype(jnp.float32), stwo_full.astype(jnp.float32)
    )
    result = normed_two.astype(jnp.bfloat16).reshape(seq_count, group_len, model_width)
    weights_back = (
        lax.all_gather(shards[0], "wa", axis=0, tiled=True),
        lax.all_gather(shards[1], "wa", axis=0, tiled=True),
        lax.all_gather(shards[2], "wa", axis=0, tiled=True),
        lax.all_gather(shards[3], "wa", axis=0, tiled=True),
        lax.all_gather(shards[4], "wa", axis=0, tiled=True),
        lax.all_gather(shards[5], "wa", axis=0, tiled=True),
        lax.all_gather(shards[6], "wa", axis=0, tiled=True),
        lax.all_gather(shards[7], "wa", axis=0, tiled=True),
        lax.all_gather(shards[8], "wa", axis=0, tiled=True),
        lax.all_gather(shards[9], "wa", axis=0, tiled=True),
        lax.all_gather(shards[10], "wa", axis=0, tiled=True),
        lax.all_gather(shards[11], "wa", axis=0, tiled=True),
    )
    qkv_back = weights_back[0]
    out_back = weights_back[1]
    up_back = weights_back[2]
    down_back = weights_back[3]
    grad_out = cotangent.astype(jnp.float32).reshape(total_rows, model_width) * row_live.reshape(
        total_rows
    )[:, None].astype(jnp.float32)
    grad_resid_two, grad_gain_two, grad_shift_two = norm_back_two(grad_out)
    grad_ffn_low = grad_resid_two.astype(jnp.bfloat16)
    grad_down = jnp.dot(act_low.T, grad_ffn_low, preferred_element_type=jnp.float32)
    grad_down_bias = jnp.sum(grad_ffn_low.astype(jnp.float32), 0)
    grad_act = jnp.dot(grad_ffn_low, down_back.T, preferred_element_type=jnp.float32)
    (grad_hidden,) = gelu_back(grad_act)
    grad_hidden_low = grad_hidden.astype(jnp.bfloat16)
    grad_up = jnp.dot(normed_low.T, grad_hidden_low, preferred_element_type=jnp.float32)
    grad_up_bias = jnp.sum(grad_hidden_low.astype(jnp.float32), 0)
    grad_normed = grad_resid_two + jnp.dot(
        grad_hidden_low, up_back.T, preferred_element_type=jnp.float32
    )
    grad_resid_one, grad_gain_one, grad_shift_one = norm_back_one(grad_normed)
    grad_attn_low = grad_resid_one.astype(jnp.bfloat16)
    grad_out_w = jnp.dot(attn_low.T, grad_attn_low, preferred_element_type=jnp.float32)
    grad_out_bias = jnp.sum(grad_attn_low.astype(jnp.float32), 0)
    grad_mix = (
        jnp.dot(grad_attn_low, out_back.T, preferred_element_type=jnp.float32)
        .astype(jnp.bfloat16)
        .reshape(seq_count, group_len, model_width)
    )
    grad_mix_heads = heads_of(grad_mix)
    row_delta = jnp.einsum("sqhe,shqe->shq", grad_mix_heads.astype(jnp.float32), attn_float)
    zero_heads = jnp.zeros((seq_count, group_len, HEADS, HEAD), jnp.float32)
    query_begin_at = jnp.int32(0)
    query_piece_keys = lax.all_gather(key_rows, "ctx", axis=1, tiled=True)
    query_piece_values = lax.all_gather(values, "ctx", axis=1, tiled=True)

    def one_block(carry_in, offset, block_width):
        key_places = query_begin_at + offset + jnp.arange(block_width)
        alive_keys = key_places[None, :] < lengths[:, None]

        def compute(current):
            key_heads = heads_of(cut_rows(query_piece_keys, offset, block_width))
            value_heads = heads_of(cut_rows(query_piece_values, offset, block_width))
            scores = (
                jnp.einsum(
                    "sqhe,skhe->shqk", query_heads, key_heads, preferred_element_type=jnp.float32
                )
                * score_scale
            )
            attn_prob = jnp.where(
                alive_keys[:, None, None, :], jnp.exp(scores - log_sum[..., None]), 0.0
            )
            grad_prob = jnp.einsum(
                "sqhe,skhe->shqk", grad_mix_heads, value_heads, preferred_element_type=jnp.float32
            )
            grad_scores = (attn_prob * (grad_prob - row_delta[..., None])).astype(jnp.bfloat16)
            return current + jnp.einsum(
                "shqk,skhe->sqhe", grad_scores, key_heads, preferred_element_type=jnp.float32
            )

        return lax.cond(jnp.any(alive_keys), compute, lambda current: current, carry_in)

    grad_query = by_blocks(one_block, zero_heads, query_piece_keys.shape[1]) * score_scale
    lse_all, delta_all = (
        lax.all_gather(log_sum, "ctx", axis=2, tiled=True),
        lax.all_gather(row_delta, "ctx", axis=2, tiled=True),
    )
    key_begin_at = jnp.int32(0)
    piece_queries = lax.all_gather(queries, "ctx", axis=1, tiled=True)
    piece_grads = lax.all_gather(grad_mix, "ctx", axis=1, tiled=True)

    def one_block(carry_in, offset, block_width):
        first_row = key_begin_at + offset

        def compute(current):
            grad_keys, grad_values = current
            query_block = heads_of(cut_rows(piece_queries, offset, block_width))
            grad_block = heads_of(cut_rows(piece_grads, offset, block_width))
            lse_block = lax.dynamic_slice_in_dim(lse_all, first_row, block_width, 2)
            delta_block = lax.dynamic_slice_in_dim(delta_all, first_row, block_width, 2)
            scores = (
                jnp.einsum(
                    "sqhe,skhe->shqk",
                    query_block,
                    key_heads_local,
                    preferred_element_type=jnp.float32,
                )
                * score_scale
            )
            attn_prob = jnp.where(local_mask, jnp.exp(scores - lse_block[..., None]), 0.0)
            grad_prob = jnp.einsum(
                "sqhe,skhe->shqk", grad_block, value_heads_local, preferred_element_type=jnp.float32
            )
            grad_scores = (attn_prob * (grad_prob - delta_block[..., None])).astype(jnp.bfloat16)
            grad_keys = grad_keys + jnp.einsum(
                "shqk,sqhe->skhe", grad_scores, query_block, preferred_element_type=jnp.float32
            )
            grad_values = grad_values + jnp.einsum(
                "shqk,sqhe->skhe",
                attn_prob,
                grad_block.astype(jnp.float32),
                precision=lax.Precision.HIGHEST,
            )
            return (grad_keys, grad_values)

        busy = jnp.any(first_row < lengths) & jnp.any(row_live)
        return lax.cond(busy, compute, lambda current: current, carry_in)

    grad_keys, grad_values = by_blocks(one_block, (zero_heads, zero_heads), piece_queries.shape[1])
    grad_q_low = grad_query.astype(jnp.bfloat16).reshape(total_rows, model_width)
    grad_k_low = (grad_keys * score_scale).astype(jnp.bfloat16).reshape(total_rows, model_width)
    grad_v_low = grad_values.astype(jnp.bfloat16).reshape(total_rows, model_width)
    grad_proj = jnp.concatenate([grad_q_low, grad_k_low, grad_v_low], 1)
    grad_qkv = jnp.dot(flat_rows.T, grad_proj, preferred_element_type=jnp.float32)
    grad_qv_bias = jnp.concatenate(
        [jnp.sum(grad_q_low.astype(jnp.float32), 0), jnp.sum(grad_v_low.astype(jnp.float32), 0)]
    )
    grad_input = (
        (grad_resid_one + jnp.dot(grad_proj, qkv_back.T, preferred_element_type=jnp.float32))
        .astype(jnp.bfloat16)
        .reshape(seq_count, group_len, model_width)
    )
    local_grads = (
        grad_qkv,
        grad_out_w,
        grad_up,
        grad_down,
        grad_qv_bias,
        grad_out_bias,
        grad_up_bias,
        grad_down_bias,
        grad_gain_one,
        grad_shift_one,
        grad_gain_two,
        grad_shift_two,
    )
    shares = (
        lax.psum_scatter(local_grads[0], "wa", scatter_dimension=0, tiled=True),
        lax.psum_scatter(local_grads[1], "wa", scatter_dimension=0, tiled=True),
        lax.psum_scatter(local_grads[2], "wa", scatter_dimension=0, tiled=True),
        lax.psum_scatter(local_grads[3], "wa", scatter_dimension=0, tiled=True),
        lax.psum_scatter(local_grads[4], "wa", scatter_dimension=0, tiled=True),
        lax.psum_scatter(local_grads[5], "wa", scatter_dimension=0, tiled=True),
        lax.psum_scatter(local_grads[6], "wa", scatter_dimension=0, tiled=True),
        lax.psum_scatter(local_grads[7], "wa", scatter_dimension=0, tiled=True),
        lax.psum_scatter(local_grads[8], "wa", scatter_dimension=0, tiled=True),
        lax.psum_scatter(local_grads[9], "wa", scatter_dimension=0, tiled=True),
        lax.psum_scatter(local_grads[10], "wa", scatter_dimension=0, tiled=True),
        lax.psum_scatter(local_grads[11], "wa", scatter_dimension=0, tiled=True),
    )
    summed_all = lax.psum(
        (
            shares[0],
            shares[1],
            shares[2],
            shares[3],
            shares[4],
            shares[5],
            shares[6],
            shares[7],
            shares[8],
            shares[9],
            shares[10],
            shares[11],
        ),
        "ctx",
    )
    return (
        result,
        grad_input,
        summed_all[0],
        summed_all[1],
        summed_all[2],
        summed_all[3],
        summed_all[4],
        summed_all[5],
        summed_all[6],
        summed_all[7],
        summed_all[8],
        summed_all[9],
        summed_all[10],
        summed_all[11],
    )


def solution(mesh):
    placed = (
        P("wa", "ctx", None),
        P("wa"),
        P("wa", None),
        P("wa", None),
        P("wa", None),
        P("wa", None),
        P("wa"),
        P("wa"),
        P("wa"),
        P("wa"),
        P("wa"),
        P("wa"),
        P("wa"),
        P("wa"),
        P("wa", "ctx", None),
    )
    return jax.shard_map(
        body,
        mesh=mesh,
        in_specs=placed,
        out_specs=(
            P("wa", "ctx", None),
            P("wa", "ctx", None),
            P("wa", None),
            P("wa", None),
            P("wa", None),
            P("wa", None),
            P("wa"),
            P("wa"),
            P("wa"),
            P("wa"),
            P("wa"),
            P("wa"),
            P("wa"),
            P("wa"),
        ),
        check_vma=False,
    )
```

profile of v0, /device:TPU:0, one launch (start us, length us, event | category | flops | bytes accessed | tf_op | source)
XLA Modules:
  0.0 897.7 jit_solution(13945739045702629561)
XLA Ops:
  8.0 35.1 %all-gather.16.cloned.1.call-done = bf16[768,2304]{1,0:T(8,128)(2,1)} async-done(((bf16[192,2304]{1,0:T(8,128)(2,1)}), bf16[768,2304]{1,0:T(8,128)(2,1)}) %all-gather.16.cloned.1.call-update) | async-done | bytes 3538960 | tf_op jit(solution)/shard_map/all_gather | solution.py:75
  43.1 2.8 fusion.64
  46.6 5.2 all-gather.5
  57.2 10.3 %all-reduce.17 = (bf16[768]{0:T(1024)(128)(2,1)S(1)}, bf16[768]{0:T(1024)(128)(2,1)S(1)}, bf16[768]{0:T(1024)(128)(2,1)S(1)}, bf16[768]{0:T(1024)(128)(2,1)S(1)}...) all-reduce(bf16[768]{0:T(1024)(128)(2,1)S(1)} %dynamic-update-slice, ...), channel_id=1, replica_groups=mesh['ctx'=8,'wa'=4] {'wa'}, use_global_device_ids=true, to_apply=%add | all-reduce | flops 4608 | bytes 18432
  67.4 5.2 all-gather.6
  73.3 1.2 iota_compare_fusion
  76.2 14.8 %all-gather.24.cloned.1.call-done = bf16[1024,768]{1,0:T(8,128)(2,1)} async-done(((bf16[128,768]{1,0:T(8,128)(2,1)}), bf16[1024,768]{1,0:T(8,128)(2,1)}) %all-gather.24.cloned.1.call-update) | async-done | bytes 1572880 | tf_op jit(solution)/shard_map/all_gather | solution.py:136
  91.0 45.8 %all-gather.26.cloned.1.call-done = bf16[1024,768]{1,0:T(8,128)(2,1)} async-done(((bf16[128,768]{1,0:T(8,128)(2,1)}), bf16[1024,768]{1,0:T(8,128)(2,1)}) %all-gather.26.cloned.1.call-update) | async-done | bytes 1572880 | tf_op jit(solution)/shard_map/all_gather | solution.py:137
  136.7 17.3 %conditional.3 = (f32[1,12,128]{2,1,0:T(8,128)S(1)}, f32[1,12,128,64]{2,3,1,0:T(8,128)S(1)}, f32[1,12,128]{2,1,0:T(8,128)S(1)}) conditional(s32[]{:T(128)} %convert_element_type.136, () %tuple.34, (pred[1,1024]{1,0:T(4,128)(4,1)}, bf16[1,128,12,64]{1,3,2,0:T(8,128)(2,1)}, bf16[1,1024,768]{2,1,0:T(8,128)(2,1)}, ...), branch_computations={%region_1.0_spmd.clone, %region_2.5_spmd.clone} | conditional | flops 1428268032 | bytes 60437584 | solution.py:164
  137.5 1.7 copy.72
  139.2 2.0 fusion.24
  141.3 1.8 fusion.26
  143.1 1.1 copy-done
  144.2 1.6 copy.73
  145.8 8.1 fusion.33
  154.5 1.7 fusion.79
  156.4 36.9 %all-gather.20.cloned.1.call-done = bf16[768,3072]{1,0:T(8,128)(2,1)} async-done(((bf16[192,3072]{1,0:T(8,128)(2,1)}), bf16[768,3072]{1,0:T(8,128)(2,1)}) %all-gather.20.cloned.1.call-update) | async-done | bytes 4718608 | tf_op jit(solution)/shard_map/all_gather | solution.py:77
  193.4 8.4 multiply_convert_fusion.8
  201.7 30.5 %all-gather.22.cloned.1.call-done = bf16[3072,768]{1,0:T(8,128)(2,1)} async-done(((bf16[768,768]{1,0:T(8,128)(2,1)}), bf16[3072,768]{1,0:T(8,128)(2,1)}) %all-gather.22.cloned.1.call-update) | async-done | bytes 4718608 | tf_op jit(solution)/shard_map/all_gather | solution.py:78
  232.3 3.4 fusion.80
  236.7 0.9 fusion.76
  238.4 2.4 convert_reduce_fusion.1
  240.9 2.4 multiply_reduce_fusion
  245.6 1.2 convolution_convert_fusion
  248.2 1.7 copy.71
  250.0 1.8 fusion.60
  251.8 16.8 %conditional.4 = (f32[1,128,12,64]{1,3,2,0:T(8,128)S(1)}) conditional(s32[]{:T(128)} %convert_element_type.136, () %tuple.36, (pred[1,1024]{1,0:T(4,128)(4,1)}, bf16[1,128,12,64]{1,3,2,0:T(8,128)(2,1)}, bf16[1,1024,768]{2,1,0:T(8,128)(2,1)S(1)}, f32[1,12,128]{2,1,0:T(8,128)}, bf16[128,768]{1,0:T(8,128)(2,1)}, ...), branch_computations={%region_13.14_spmd, %region_14.15_spmd} | conditional | flops 613416960 | bytes 31890524 | solution.py:267
  251.8 1.6 copy.54
  253.4 5.2 fusion.20
  258.6 1.3 reduce.10
  260.7 1.6 copy.56
  262.3 6.2 fusion.19
  268.5 30.9 %all_gather.75 = f32[1,12,1024]{2,1,0:T(8,128)S(1)} all-gather(f32[1,12,128]{2,1,0:T(8,128)} %copy-done.33), channel_id=1, replica_groups=mesh['ctx'=8,'wa'=4] {'ctx'}, dimensions={2}, use_global_device_ids=true | all-gather | bytes 55296 | tf_op jit(solution)/shard_map/all_gather | solution.py:271
  299.4 30.9 %all-gather.4 = f32[12,1024]{1,0:T(8,128)S(1)} all-gather(f32[12,128]{1,0:T(8,128)} %fusion.60), channel_id=6, replica_groups=mesh['ctx'=8,'wa'=4] {'ctx'}, dimensions={1}, use_global_device_ids=true | all-gather | bytes 55296 | tf_op jit(solution)/shard_map/all_gather | solution.py:272
  330.7 23.4 %conditional.5 = (f32[1,128,12,64]{1,3,2,0:T(8,128)S(1)}, bf16[128,768]{0,1:T(8,128)(2,1)S(1)}, f32[768]{0:T(1024)S(1)}) conditional(s32[]{:T(128)} %convert_element_type.159, () %tuple.38, (s32[]{:T(128)}, s32[1,1,1,128]{3,2,1,0:T(1,128)S(1)}, s32[]{:T(128)}, bf16[1,1024,768]{2,1,0:T(8,128)(2,1)}, bf16[128,768]{1,0:T(8,128)(2,1)}, ...), branch_computations={%region_16.17_spmd, %region_17.0_spmd} | conditional | flops 1826389504 | bytes 34957272 | solution.py:313
  330.9 1.8 copy.57
  332.8 3.7 fusion.81
  337.2 2.6 copy.59
  340.0 7.7 fusion.9
  347.7 6.2 convert_reduce_fusion
  354.1 3.9 convolution_bitcast_fusion
  358.1 8.1 copy.69
  367.2 1.9 fusion.82
  369.1 1.3 copy-done.12
  370.4 6.3 fusion.72
  377.0 0.9 copy-done.7
  377.9 5.1 fusion.83
  383.0 44.2 %reduce-scatter.13.cloned.1.call-done = f32[192,2304]{1,0:T(8,128)} async-done(((f32[768,2304]{1,0:T(8,128)}), f32[192,2304]{1,0:T(8,128)}) %reduce-scatter.13.cloned.1.call-update) | async-done | bytes 1769488
  427.3 2.9 copy.70
  430.2 33.3 %reduce-scatter.7.cloned.1.call-done = f32[192,768]{1,0:T(8,128)} async-done(((f32[768,768]{1,0:T(8,128)}), f32[192,768]{1,0:T(8,128)}) %reduce-scatter.7.cloned.1.call-update) | async-done | bytes 589840 | tf_op jit(solution)/shard_map/reduce_scatter | solution.py:345
  463.5 81.0 %reduce-scatter.9.cloned.1.call-done = f32[192,3072]{1,0:T(8,128)} async-done(((f32[768,3072]{1,0:T(8,128)}), f32[192,3072]{1,0:T(8,128)}) %reduce-scatter.9.cloned.1.call-update) | async-done | bytes 2359312 | tf_op jit(solution)/shard_map/reduce_scatter | solution.py:346
  544.5 80.8 %reduce-scatter.11.cloned.1.call-done = f32[768,768]{1,0:T(8,128)} async-done(((f32[3072,768]{1,0:T(8,128)}), f32[768,768]{1,0:T(8,128)}) %reduce-scatter.11.cloned.1.call-update) | async-done | bytes 2359312 | tf_op jit(solution)/shard_map/reduce_scatter | solution.py:347
  629.0 11.7 %all-reduce.16 = (f32[1536]{0:T(1024)}, f32[768]{0:T(1024)S(1)}, f32[3072]{0:T(1024)}, f32[768]{0:T(1024)}, f32[768]{0:T(1024)}, /*index=5*/f32[768]{0:T(1024)}, f32[768]{0:T(1024)}, f32[768]{0:T(1024)}) all-reduce(f32[1536]{0:T(1024)S(1)} %pad_maximum_fusion.3, ...), channel_id=11, replica_groups=mesh['ctx'=8,'wa'=4] {'wa'}, use_global_device_ids=true, to_apply=%region_28.29.clone | all-reduce | flops 9216 | bytes 73728
  641.5 1.3 dynamic-slice.15
  642.8 1.3 dynamic-slice.17
  644.1 1.3 dynamic-slice.19
  645.4 1.3 dynamic-slice.21
  648.3 40.2 %all-reduce.14 = (f32[384]{0:T(512)}, f32[192]{0:T(256)}, f32[768]{0:T(1024)}, f32[192]{0:T(256)}, f32[192]{0:T(256)}, /*index=5*/f32[192]{0:T(256)}, f32[192]{0:T(256)}, f32[192]{0:T(256)}) all-reduce(f32[384]{0:T(512)S(1)} %dynamic-slice.7, f32[192]{0:T(256)S(1)} %dynamic-slice.9, ...), channel_id=1, replica_groups=mesh['ctx'=8,'wa'=4] {'ctx'}, use_global_device_ids=true, to_apply=%region_29.30 | all-reduce | flops 2304 | bytes 18432 | tf_op jit(solution)/shard_map/psum | solution.py:357
  688.5 3.2 fusion.50
  691.7 191.3 %all-reduce.20.cloned.1.call-done = (f32[192,2304]{0,1:T(8,128)}, f32[192,768]{1,0:T(8,128)}, f32[192,3072]{1,0:T(8,128)}, f32[768,768]{1,0:T(8,128)}) async-done(((f32[192,2304]{0,1:T(8,128)}, f32[192,768]{1,0:T(8,128)}, f32[192,3072]{1,0:T(8,128)}, f32[768,768]{1,0:T(8,128)}), (f32[192,2304]{0,1:T(8,128)}, f32[192,768]{1,0:T(8,128)}, f32[192,3072]{1,0:T(8,128)}, ...) | async-done | bytes 7077904 | tf_op jit(solution)/shard_map/psum | solution.py:357
  883.0 3.1 copy.61
  886.9 1.4 copy.100
  888.3 1.1 copy-done.13
  889.4 1.4 copy.101
  (201 shorter events, 21.4 us)
Async XLA Ops:
  7.2 35.9 %all-gather.16.cloned.1.call-start = ((), (), s32[]{:S(2)}) async-start(), calls=%async_computation.4 | async-start | bytes 4423680 | tf_op jit(solution)/shard_map/all_gather | solution.py:75
  7.9 38.7 %copy-start.41 = (bf16[384]{0:T(512)(128)(2,1)S(1)}, bf16[384]{0:T(512)(128)(2,1)}, u32[]{:S(2)}) copy-start(bf16[384]{0:T(512)(128)(2,1)} %param.27) | copy-start | bytes 2308
  7.9 83.0 %all-gather.24.cloned.1.call-start = ((), (), s32[]{:S(2)}) async-start(), calls=%async_computation.11 | async-start | bytes 1769472 | tf_op jit(solution)/shard_map/all_gather | solution.py:136
  46.6 90.2 %all-gather.26.cloned.1.call-start = ((), (), s32[]{:S(2)}) async-start(), calls=%async_computation.12 | async-start | bytes 1769472 | tf_op jit(solution)/shard_map/all_gather | solution.py:137
  52.6 23.5 %copy-start.19 = (bf16[128,768]{1,0:T(8,128)(2,1)}, bf16[128,768]{1,0:T(8,128)(2,1)S(1)}, u32[]{:S(2)}) copy-start(bf16[128,768]{1,0:T(8,128)(2,1)S(1)} %get-tuple-element.270) | copy-start | bytes 589828
  52.6 1.9 copy-start.39
  52.6 3.2 copy-start.43
  52.6 3.4 copy-start.44
  52.6 3.6 copy-start.45
  52.6 3.9 copy-start.46
  52.6 4.1 copy-start.47
  52.6 4.3 copy-start.48
  52.6 14.8 %copy-start.40 = (bf16[768]{0:T(1024)(128)(2,1)S(1)}, bf16[768]{0:T(1024)(128)(2,1)}, u32[]{:S(2)}) copy-start(bf16[768]{0:T(1024)(128)(2,1)} %param.29) | copy-start | bytes 4612
  52.7 101.8 %all-gather.18.cloned.1.call-start = ((), (), s32[]{:S(2)}) async-start(), calls=%async_computation.5 | async-start | bytes 1474560 | tf_op jit(solution)/shard_map/all_gather | solution.py:76
  53.3 140.1 %all-gather.20.cloned.1.call-start = ((), (), s32[]{:S(2)}) async-start(), calls=%async_computation.6 | async-start | bytes 5898240 | tf_op jit(solution)/shard_map/all_gather | solution.py:77
  53.9 178.4 %all-gather.22.cloned.1.call-start = ((), (), s32[]{:S(2)}) async-start(), calls=%async_computation.7 | async-start | bytes 5898240 | tf_op jit(solution)/shard_map/all_gather | solution.py:78
  54.4 276.2 %all-gather.28.cloned.1.call-start = ((), (), s32[]{:S(2)}) async-start(), calls=%async_computation.13 | async-start | bytes 1769472 | tf_op jit(solution)/shard_map/all_gather | solution.py:275
  76.1 254.5 %all-gather.30.cloned.1.call-start = ((), (), s32[]{:S(2)}) async-start(), calls=%async_computation.14 | async-start | bytes 1769472 | tf_op jit(solution)/shard_map/all_gather | solution.py:276
  136.7 17.7 %copy-start.15 = (bf16[1,128,768]{2,1,0:T(8,128)(2,1)S(1)}, bf16[1,128,768]{2,1,0:T(8,128)(2,1)}, u32[]{:S(2)}) copy-start(bf16[1,128,768]{2,1,0:T(8,128)(2,1)} %param.21) | copy-start | bytes 589828
  141.3 2.9 copy-start
  141.3 2.9 copy-start.3
  154.1 47.6 %copy-start.9 = (f32[1,12,128,64]{2,3,1,0:T(8,128)}, f32[1,12,128,64]{2,3,1,0:T(8,128)S(1)}, u32[]{:S(2)}) copy-start(f32[1,12,128,64]{2,3,1,0:T(8,128)S(1)} %get-tuple-element.93) | copy-start | bytes 1179652
  154.1 47.6 %copy-start.33 = (f32[1,12,128]{2,1,0:T(8,128)}, f32[1,12,128]{2,1,0:T(8,128)S(1)}, u32[]{:S(2)}) copy-start(f32[1,12,128]{2,1,0:T(8,128)S(1)} %get-tuple-element.202) | copy-start | bytes 18436
  154.2 39.2 %copy-start.20 = (bf16[1,12,128,64]{2,3,1,0:T(8,128)(2,1)}, bf16[1,12,128,64]{2,3,1,0:T(8,128)(2,1)S(1)}, u32[]{:S(2)}) copy-start(bf16[1,12,128,64]{2,3,1,0:T(8,128)(2,1)S(1)} %fusion.66) | copy-start | bytes 589828
  156.2 87.1 %copy-start.34 = (f32[128]{0:T(128)}, f32[128]{0:T(128)S(1)}, u32[]{:S(2)}) copy-start(f32[128]{0:T(128)S(1)} %broadcast_multiply_fusion.1) | copy-start | bytes 1540
  156.4 86.9 %copy-start.37 = (f32[128]{0:T(128)}, f32[128]{0:T(128)S(1)}, u32[]{:S(2)}) copy-start(f32[128]{0:T(128)S(1)} %fusion.67) | copy-start | bytes 1540
  201.7 33.9 %copy-start.6 = (bf16[128,3072]{1,0:T(8,128)(2,1)}, bf16[128,3072]{1,0:T(8,128)(2,1)S(1)}, u32[]{:S(2)}) copy-start(bf16[128,3072]{1,0:T(8,128)(2,1)S(1)} %get-tuple-element.261) | copy-start | bytes 2359300
  232.3 6.1 slice-start
  232.3 3.6 copy-start.25
  232.3 6.1 slice-start.1
  232.3 6.1 copy-start.50
  235.7 2.7 copy-start.49
  237.7 3.2 slice-start.2
  238.4 2.5 copy-start.28
  238.4 2.5 slice-start.3
  240.9 2.4 copy-start.11
  243.2 2.4 copy-start.5
  243.5 1.4 copy-start.42
  244.3 7.5 copy-start.1
  244.3 7.5 copy-start.2
  246.9 180.4 %reduce-scatter.13.cloned.1.call-start = ((), (), s32[]{:S(2)}) async-start(), calls=%async_computation.15 | async-start | bytes 8847360
  253.4 6.5 copy-start.10
  260.7 1.6 copy-start.4
  260.7 1.6 copy-start.32
  330.6 23.5 %copy-start.27 = (bf16[1,128,12,64]{1,3,2,0:T(8,128)(2,1)}, bf16[1,128,12,64]{1,3,2,0:T(8,128)(2,1)S(1)}, u32[]{:S(2)}) copy-start(bf16[1,128,12,64]{1,3,2,0:T(8,128)(2,1)S(1)} %get-tuple-element.256) | copy-start | bytes 589828
  330.6 23.5 %copy-start.16 = (bf16[1,128,768]{2,1,0:T(8,128)(2,1)S(1)}, bf16[1,128,768]{2,1,0:T(8,128)(2,1)}, u32[]{:S(2)}) copy-start(bf16[1,128,768]{2,1,0:T(8,128)(2,1)} %param.21) | copy-start | bytes 589828
  330.9 1.8 copy-start.17
  337.2 2.6 copy-start.18
  354.0 4.0 copy-start.26
  354.0 4.0 copy-start.36
  354.1 4.0 copy-start.30
  366.2 97.3 %reduce-scatter.7.cloned.1.call-start = ((), (), s32[]{:S(2)}) async-start(), calls=%async_computation.8 | async-start | bytes 2949120 | tf_op jit(solution)/shard_map/reduce_scatter | solution.py:345
  369.0 1.4 copy-start.12
  369.0 1.4 copy-start.35
  369.0 1.4 copy-start.38
  369.1 175.4 %reduce-scatter.9.cloned.1.call-start = ((), (), s32[]{:S(2)}) async-start(), calls=%async_computation.9 | async-start | bytes 11796480 | tf_op jit(solution)/shard_map/reduce_scatter | solution.py:346
  376.7 1.2 copy-start.7
  376.7 1.2 copy-start.29
  376.7 248.6 %reduce-scatter.11.cloned.1.call-start = ((), (), s32[]{:S(2)}) async-start(), calls=%async_computation.10 | async-start | bytes 11796480 | tf_op jit(solution)/shard_map/reduce_scatter | solution.py:347
  383.0 500.0 %all-reduce.20.cloned.1.call-start = ((), (), s32[]{:S(2)}) async-start(), calls=%async_computation.16 | async-start | bytes 15335424 | tf_op jit(solution)/shard_map/psum | solution.py:357
  625.3 63.2 %copy-start.8 = (bf16[768,2304]{1,0:T(8,128)(2,1)S(1)}, bf16[768,2304]{1,0:T(8,128)(2,1)}, u32[]{:S(2)}) copy-start(bf16[768,2304]{1,0:T(8,128)(2,1)} %all-gather.16.cloned.1.call-done) | copy-start | bytes 10616836
  883.0 3.1 copy-start.31
  883.0 3.9 copy-start.14
  886.8 2.5 copy-start.13
  (4 other events, 3.4 us)
Sparse Core Ops, SparseCore 0:
  9.6 33.4 all-gather.15
  46.7 44.2 all-gather.23
  93.7 42.9 all-gather.25
  138.2 16.2 all-gather.17
  155.9 37.4 all-gather.19
  194.8 37.4 all-gather.21
  234.5 44.0 all-gather.27
  280.7 43.4 all-gather.29
  366.3 60.9 reduce-scatter.12
  430.4 33.0 reduce-scatter.6
  466.1 78.3 reduce-scatter.8
  546.9 78.3 reduce-scatter.10
  630.4 252.5 all-reduce.19
where the time goes:
time: 908 us; the launch traced here: 898 us
  waiting for transfers between devices  597 us (66%)
  blocking collectives  134 us (15%)
  matrix products  81.9 us (9%)
  local copies, waits for them, and re-layouts  50.4 us (6%)
  between operations  19.7 us (2%)
  other arithmetic  13.6 us (1%)
    psum x1, waiting for transfers between devices, body(): lax.psum((shares[0], shares[1], shares[2], shares[3], shares[4], shares[5...  191 us
    reduce_scatter x1, waiting for transfers between devices, body(): lax.psum_scatter(local_grads[2], 'wa', scatter_dimension=0, tiled=True)  81 us
    reduce_scatter x1, waiting for transfers between devices, body(): lax.psum_scatter(local_grads[3], 'wa', scatter_dimension=0, tiled=True)  80.8 us
    unnamed x14, waiting for transfers between devices  46.6 us
    all_gather x1, waiting for transfers between devices, body(): piece_values = lax.all_gather(values, 'ctx', axis=1, tiled=True)  45.8 us
    psum x1, blocking collectives, body(): lax.psum((shares[0], shares[1], shares[2], shares[3], shares[4], shares[5...  40.2 us
    all_gather x1, waiting for transfers between devices, body(): lax.all_gather(shards[2], 'wa', axis=0, tiled=True)  36.9 us
    all_gather x1, waiting for transfers between devices, body(): lax.all_gather(shards[0], 'wa', axis=0, tiled=True)  35.1 us
  transfers between devices with their start and end apart: 13, of which 11 were waited for; matrix products, arithmetic and copies ran while one was open for 10% of the time, Pallas kernels for 0%

commit v1 on v0

v1 whole, which is shorter than its diff:
```python
import functools
import math
from types import SimpleNamespace

import jax
import jax.numpy as jnp
from jax import lax
from jax.experimental import pallas as pl
from jax.experimental.pallas import tpu as pltpu
from jax.sharding import PartitionSpec as P

HEADS = 12
HEAD = 64
EPS = 1e-12
FLOOR = -1e30
MESH = pl.DeviceIdType.MESH
BF = jnp.bfloat16
F32 = jnp.float32

OUTB, DOWNB, GAIN1, SHIFT1, GAIN2, SHIFT2, LEN = range(7)
VROWS = 16
GROWS = 8


def dot(a, b):
    return lax.dot_general(a, b, (((1,), (0,)), ((), ())), preferred_element_type=F32)


def dot_nt(a, b):
    return lax.dot_general(a, b, (((1,), (1,)), ((), ())), preferred_element_type=F32)


def dot_tn(a, b):
    return lax.dot_general(a, b, (((0,), (0,)), ((), ())), preferred_element_type=F32)


def norm_stats(v):
    center = v - jnp.mean(v, -1, keepdims=True)
    rstd = lax.rsqrt(jnp.mean(center * center, -1, keepdims=True) + EPS)
    return center * rstd, rstd


def norm_back(dy, normed, rstd, gain):
    dn = dy * gain
    return rstd * (
        dn - jnp.mean(dn, -1, keepdims=True) - normed * jnp.mean(dn * normed, -1, keepdims=True)
    )


def col_sum(v):
    return jnp.sum(v, 0, keepdims=True)


def make_plan(cfg):
    C, W, B, D, FW, DW, DP, KVW, MW, R = (
        cfg.C, cfg.W, cfg.B, cfg.D, cfg.FW, cfg.DW, cfg.DP, cfg.KVW, cfg.MW, cfg.R)
    V = pltpu.VMEM
    dma = pltpu.SemaphoreType.DMA
    Q = W * B
    plan = dict(
        Xall=V((W, B, D), BF), Wc=V((D, MW), BF), Bb=V((W, 16, MW), BF), Vv=V((W, VROWS, D), F32),
        Vs=V((VROWS, D), F32), Outp=V((W, DP, D), BF), Upc=V((D, FW), BF), Dn=V((FW, D), BF), Cot=V((B, D), BF),
        QKVs=V((W, B, MW), BF), Rq=V((W, B, MW), BF), KV=V((R * Q, KVW), BF),
        Qm=V((cfg.HW, Q, DP), BF), Dm=V((cfg.HW, Q, DP), BF),
        mrow=V((8, Q), F32), lrow=V((8, Q), F32), drow=V((8, Q), F32), OT=V((DP, Q), F32), dQT=V((DP, Q), F32),
        Osend=V((W, B, DP), BF), Mix=V((W, B, DP), BF), MixT=V((W, B, DP), BF),
        N1f=V((B, D), F32), n1=V((B, D), F32), n2=V((B, D), F32), r1=V((B, 1), F32),
        N1all=V((W, B, D), BF), Hp=V((W, B, FW), F32), Gs=V((W, B, FW), BF),
        Fs=V((W, B, D), BF), Fr=V((3, B, D), BF), dR2=V((B, D), F32), dFall=V((W, B, D), BF),
        dHs=V((W, B, FW), BF), dNs=V((W, B, D), BF), dNr=V((3, B, D), BF), dR1=V((B, D), F32),
        dAall=V((W, B, D), BF), dOs=V((W, B, DP), BF), dOr=V((W, B, DP), BF),
        dKVf=V((R * Q, KVW), F32), dKVs=V((R, Q, KVW), BF), dKVr=V((R, Q, KVW), BF),
        dqs=V((W, B, MW), BF), dqr=V((W, B, MW), BF), dxs=V((W, B, D), BF), dxr=V((3, B, D), BF),
        gv=V((GROWS, D), F32),
    )
    sems = dict(
        x=4, wq=4, bb=4, vv=4, ow=4, uw=4, own=8,
        q=W, kv=(R - 1) * W, o=W, mt=4, n=4, f=4, df=4, dn=4, da=4, do=W, dkv=R - 1, dq=W, dx=4,
    )
    recvs = dict(sems, kv=R * W, dkv=R, q=W)
    if cfg.fused:
        NZ = C // 2
        for name, (ch, cols, to_rows) in cfg.grads.items():
            plan["G" + name] = V((NZ, 2, ch, cols), BF)
            plan["X" + name] = V((NZ, ch, cols), BF)
            plan["S" + name] = V((NZ, ch, cols), BF)
            plan["Z" + name] = V((NZ, ch, cols), BF)
            plan["R" + name] = V((ch, cols), BF)
            plan["F" + name] = V((2, W, ch, cols) if to_rows else (NZ, 2, ch, cols), BF)
            for kind in ("gx", "gz", "ga", "gf"):
                sems[kind + name] = NZ + 1
                recvs[kind + name] = NZ + 1
            sems["gw" + name] = 1
            recvs["gw" + name] = W
        plan.update(Vx=V((GROWS, D), F32), Vy=V((GROWS, D), F32), Vz=V((NZ, GROWS, D), F32),
                    Vw=V((W, GROWS, D), F32))
        sems.update(vx=1, vz=NZ, vw=4)
        recvs.update(vx=1, vz=NZ, vw=4)
    for name, n in sems.items():
        plan["s_" + name] = dma((n,))
    for name, n in recvs.items():
        plan["r_" + name] = dma((n,))
    return plan


def layer_kernel(cfg, names, n_in, *refs):
    (x_ref, cot_ref, wq_ref, bias_ref, vec_ref, upb_ref, out_ref, up_ref, down_ref) = refs[:n_in]
    y_ref, gx_ref, gqkv_ref, gout_ref, gup_ref, gdown_ref, gvec_ref = refs[n_in : n_in + 7]
    m = SimpleNamespace(**dict(zip(names, refs[n_in + 7 :])))
    C, W, B, D, DW, DP, KVW, MW, R, HW = (
        cfg.C, cfg.W, cfg.B, cfg.D, cfg.DW, cfg.DP, cfg.KVW, cfg.MW, cfg.R, cfg.HW)
    OFF = DP - DW
    Q = W * B
    c = lax.axis_index("ctx")
    w = lax.axis_index("wa")
    block_part = lax.rem(c, R)
    block_slot = lax.div(c, R)
    s = lax.div(c, R)
    low = lax.rem(c, R)
    g_att = lax.div(w, 2) * 2 + lax.rem(low, 2)
    r_att = lax.div(low, 2) * 2 + lax.rem(w, 2)

    def att_device(t, g, r):
        return (t * R + lax.div(r, 2) * 2 + lax.rem(g, 2), lax.div(g, 2) * 2 + lax.rem(r, 2))

    def is_me(dev):
        return jnp.logical_and(dev[0] == c, dev[1] == w)

    drains = []

    def remote(src, dst, ss, rs, dev):
        return pltpu.make_async_remote_copy(
            src_ref=src, dst_ref=dst, send_sem=ss, recv_sem=rs, device_id=dev, device_id_type=MESH)

    def send(src, dst, ss, rs, dev, pred=None):
        def go():
            remote(src, dst, ss, rs, dev).start()

        def end():
            remote(src, dst, ss, rs, dev).wait_send()

        if pred is None:
            go()
        else:
            pl.when(pred)(go)
        drains.append((pred, end))

    def arrive(dst, rs, pred=None):
        def go():
            remote(dst, dst, rs, rs, (c, w)).wait_recv()

        if pred is None:
            go()
        else:
            pl.when(pred)(go)

    barrier = pltpu.get_barrier_semaphore()

    def greet(i, carry):
        ci, wi = lax.div(i, W), lax.rem(i, W)

        @pl.when(jnp.logical_not(is_me((ci, wi))))
        def _():
            pl.semaphore_signal(barrier, inc=1, device_id=(ci, wi), device_id_type=MESH)

        return carry

    lax.fori_loop(0, C * W, greet, 0)
    pl.semaphore_wait(barrier, C * W - 1)

    def peer(k):
        return (c, jnp.bitwise_xor(w, k))

    def gather_start(buf, ss, rs):
        send(buf.at[w], buf.at[w], ss.at[2], rs.at[2], peer(2))
        send(buf.at[w], buf.at[w], ss.at[1], rs.at[1], peer(1))

    def gather_wait(buf, ss, rs, k):
        if k == 1:
            arrive(buf.at[jnp.bitwise_xor(w, 1)], rs.at[1])
        if k == 2:
            t = jnp.bitwise_xor(w, 2)
            arrive(buf.at[t], rs.at[2])
            send(buf.at[t], buf.at[t], ss.at[3], rs.at[3], peer(1))
        if k == 3:
            arrive(buf.at[jnp.bitwise_xor(w, 3)], rs.at[3])

    def scatter_sum(part, stage, recv, ss, rs):
        t3, t2, t1 = (jnp.bitwise_xor(w, k) for k in (3, 2, 1))
        stage[t3] = part(t3).astype(BF)
        send(stage.at[t3], recv.at[1], ss.at[1], rs.at[1], peer(1))
        mine2 = part(t2)
        arrive(recv.at[1], rs.at[1])
        stage[t2] = (mine2 + recv[1].astype(F32)).astype(BF)
        send(stage.at[t2], recv.at[2], ss.at[2], rs.at[2], peer(2))
        stage[t1] = part(t1).astype(BF)
        send(stage.at[t1], recv.at[0], ss.at[0], rs.at[0], peer(1))
        own = part(w)
        arrive(recv.at[0], rs.at[0])
        own = own + recv[0].astype(F32)
        arrive(recv.at[2], rs.at[2])
        return own + recv[2].astype(F32)

    def local(src, dst, sem):
        cp = pltpu.make_async_copy(src, dst, sem)
        cp.start()
        return cp

    rows_w = pl.ds(w * DW, DW)
    own = [
        local(x_ref, m.Xall.at[w], m.s_own.at[0]),
        local(wq_ref.at[w], m.Wc.at[rows_w], m.s_own.at[1]),
        local(bias_ref.at[w], m.Bb.at[w], m.s_own.at[2]),
        local(vec_ref, m.Vv.at[w], m.s_own.at[3]),
        local(out_ref, m.Outp.at[w, pl.ds(OFF, DW)], m.s_own.at[4]),
        local(up_ref.at[:, pl.ds(pl.multiple_of(w * cfg.FW, cfg.FW), cfg.FW)], m.Upc.at[rows_w], m.s_own.at[5]),
        local(down_ref, m.Dn, m.s_own.at[6]),
        local(cot_ref, m.Cot, m.s_own.at[7]),
    ]
    for k in (2, 3, 1):
        t = jnp.bitwise_xor(w, k)
        send(wq_ref.at[t], m.Wc.at[rows_w], m.s_wq.at[k], m.r_wq.at[k], peer(k))
        send(bias_ref.at[t], m.Bb.at[w], m.s_bb.at[k], m.r_bb.at[k], peer(k))
        send(vec_ref, m.Vv.at[w], m.s_vv.at[k], m.r_vv.at[k], peer(k))
    own[0].wait()
    gather_start(m.Xall, m.s_x, m.r_x)
    for t in range(W):
        m.Outp[t, 0:OFF, :] = jnp.zeros((OFF, D), BF)
    for cp in own[1:]:
        cp.wait()
    for k in (1, 2, 3):
        t = jnp.bitwise_xor(w, k)
        arrive(m.Wc.at[pl.ds(t * DW, DW)], m.r_wq.at[k])
        arrive(m.Bb.at[t], m.r_bb.at[k])
        arrive(m.Vv.at[t], m.r_vv.at[k])
        gather_wait(m.Xall, m.s_x, m.r_x, k)
    for k in (2, 3, 1):
        t = jnp.bitwise_xor(w, k)
        send(out_ref, m.Outp.at[w, pl.ds(OFF, DW)], m.s_ow.at[k], m.r_ow.at[k], peer(k))
    for k in (2, 3, 1):
        t = jnp.bitwise_xor(w, k)
        send(up_ref.at[:, pl.ds(pl.multiple_of(t * cfg.FW, cfg.FW), cfg.FW)], m.Upc.at[rows_w],
             m.s_uw.at[k], m.r_uw.at[k], peer(k))

    vsum = m.Vv[0]
    bias = m.Bb[0, 0:1, :].astype(F32)
    for t in range(1, W):
        vsum = vsum + m.Vv[t]
        bias = bias + m.Bb[t, 0:1, :].astype(F32)
    m.Vs[...] = vsum

    def vec(row):
        return m.Vs[row : row + 1, :]

    for k in range(W):
        t = lax.rem(s + 1 + k, W)
        m.QKVs[t] = (dot(m.Xall[t], m.Wc[...]) + bias).astype(BF)
        dev = att_device(t, w, block_part)
        send(m.QKVs.at[t], m.Rq.at[block_slot], m.s_q.at[k], m.r_q.at[block_slot], dev,
             jnp.logical_not(is_me(dev)))

        @pl.when(is_me(dev))
        def _():
            m.Rq[block_slot] = m.QKVs[t]

    lanes = lax.broadcasted_iota(jnp.int32, (1, DP), 1)

    def q_lane(h):
        return jnp.logical_and(lanes >= h * HEAD, lanes < (h + 1) * HEAD)

    def v_lane(h):
        return jnp.logical_and(lanes >= OFF + h * HEAD, lanes < OFF + (h + 1) * HEAD)

    for j in range(W):
        src = (j * R + r_att, g_att)
        arrive(m.Rq.at[j], m.r_q.at[j], jnp.logical_not(is_me(src)))
        kv_rows = pl.ds(pl.multiple_of(r_att * Q + j * B, B), B)
        for k in range(1, R):
            dev = att_device(s, g_att, lax.rem(r_att + k, R))
            send(m.Rq.at[j, :, pl.ds(0, KVW)], m.KV.at[kv_rows], m.s_kv.at[(k - 1) * W + j],
                 m.r_kv.at[r_att * W + j], dev)
        m.KV[kv_rows, :] = m.Rq[j, :, 0:KVW]
        q = m.Rq[j, :, KVW:MW] * jnp.asarray(HEAD**-0.5, BF)
        for h in range(HW):
            m.Qm[h, j * B : (j + 1) * B, :] = jnp.where(q_lane(h), q, jnp.zeros_like(q))
    for k in range(1, R):
        r = lax.rem(r_att + k, R)
        for j in range(W):
            arrive(m.KV.at[pl.ds(pl.multiple_of(r * Q + j * B, B), B)], m.r_kv.at[r * W + j])

    KC = 2 * B
    PER_SET = Q // KC
    len_s = m.Vs[pl.ds(LEN + s, 1), 0:Q]

    def alive(chunk):
        r, half = lax.div(chunk, PER_SET), lax.rem(chunk, PER_SET)
        row = lax.broadcasted_iota(jnp.int32, (KC, Q), 0)
        later = (row >= B).astype(jnp.int32)
        place = ((2 * half + later) * R + r) * B + row - later * B
        return place.astype(F32) < len_s

    m.mrow[...] = jnp.full(m.mrow.shape, FLOOR, F32)
    m.lrow[...] = jnp.zeros(m.lrow.shape, F32)
    m.OT[...] = jnp.zeros(m.OT.shape, F32)

    def attend(chunk, carry):
        rows = pl.ds(pl.multiple_of(chunk * KC, KC), KC)
        keys = m.KV[rows, 0:DP]
        values_t = m.KV[rows, KVW - DP : KVW].T
        live = alive(chunk)
        for h in range(HW):
            scores = jnp.where(live, dot_nt(keys, m.Qm[h]), FLOOR)
            top = m.mrow[h : h + 1, :]
            new_top = jnp.maximum(top, jnp.max(scores, 0, keepdims=True))
            prob = jnp.exp(scores - new_top)
            factor = jnp.exp(top - new_top)
            m.mrow[h : h + 1, :] = new_top
            m.lrow[h : h + 1, :] = m.lrow[h : h + 1, :] * factor + col_sum(prob)
            a, b = OFF + h * HEAD, OFF + (h + 1) * HEAD
            m.OT[a:b, :] = m.OT[a:b, :] * factor + dot(values_t[a:b, :], prob.astype(BF))
        return carry

    lax.fori_loop(0, R * PER_SET, attend, 0)
    for h in range(HW):
        a, b = OFF + h * HEAD, OFF + (h + 1) * HEAD
        m.OT[a:b, :] = m.OT[a:b, :] / m.lrow[h : h + 1, :]
    m.lrow[0:HW, :] = m.mrow[0:HW, :] + jnp.log(m.lrow[0:HW, :])
    for j in range(W):
        m.Osend[j] = m.OT[:, j * B : (j + 1) * B].T.astype(BF)
        dev = (j * R + r_att, s)
        send(m.Osend.at[j], m.Mix.at[g_att], m.s_o.at[j], m.r_o.at[g_att], dev, jnp.logical_not(is_me(dev)))

        @pl.when(is_me(dev))
        def _():
            m.Mix[g_att] = m.Osend[j]

    for k in (1, 2, 3):
        arrive(m.Outp.at[jnp.bitwise_xor(w, k), pl.ds(OFF, DW)], m.r_ow.at[k])
    resid = m.Xall[w].astype(F32) + vec(OUTB)
    for g in range(W):
        arrive(m.Mix.at[g], m.r_o.at[g], jnp.logical_not(is_me(att_device(w, g, block_part))))
        resid = resid + dot(m.Mix[g], m.Outp[g])
    n1, r1 = norm_stats(resid)
    m.n1[...] = n1
    m.r1[...] = r1
    n1_full = n1 * vec(GAIN1) + vec(SHIFT1)
    m.N1f[...] = n1_full
    m.N1all[w] = n1_full.astype(BF)
    gather_start(m.N1all, m.s_n, m.r_n)

    for k in (1, 2, 3):
        arrive(m.Upc.at[pl.ds(jnp.bitwise_xor(w, k) * DW, DW)], m.r_uw.at[k])
    up_bias = upb_ref[...]

    def expand(t):
        h = dot(m.N1all[t], m.Upc[...]) + up_bias
        phi = 0.5 * (1.0 + lax.erf(h * (2.0**-0.5)))
        m.Gs[t] = (h * phi).astype(BF)
        m.Hp[t] = phi + h * ((2.0 * math.pi) ** -0.5) * jnp.exp(-0.5 * h * h)

    expand(w)
    for k in (1, 2, 3):
        gather_wait(m.N1all, m.s_n, m.r_n, k)
        expand(jnp.bitwise_xor(w, k))

    ffn = scatter_sum(lambda t: dot(m.Gs[t], m.Dn[...]), m.Fs, m.Fr, m.s_f, m.r_f)
    n2, r2 = norm_stats(m.N1f[...] + ffn + vec(DOWNB))
    m.n2[...] = n2
    y_ref[...] = (n2 * vec(GAIN2) + vec(SHIFT2)).astype(BF)

    place = c * B + lax.broadcasted_iota(jnp.int32, (B, D), 0)
    dy = jnp.where(place.astype(F32) < m.Vs[pl.ds(LEN + w, 1), :], m.Cot[...].astype(F32), 0.0)
    d_r2 = norm_back(dy, n2, r2, vec(GAIN2))
    m.dR2[...] = d_r2
    m.dFall[w] = d_r2.astype(BF)
    gather_start(m.dFall, m.s_df, m.r_df)
    m.gv[2:3, :] = col_sum(dy * n2)
    m.gv[3:4, :] = col_sum(dy)
    m.gv[5:6, :] = col_sum(m.dFall[w].astype(F32))

    def shrink(t):
        m.dHs[t] = (dot_nt(m.dFall[t], m.Dn[...]) * m.Hp[t]).astype(BF)

    shrink(w)
    for k in (1, 2, 3):
        gather_wait(m.dFall, m.s_df, m.r_df, k)
        shrink(jnp.bitwise_xor(w, k))
    d_n1 = scatter_sum(lambda t: dot_nt(m.dHs[t], m.Upc[...]), m.dNs, m.dNr, m.s_dn, m.r_dn) + m.dR2[...]
    n1 = m.n1[...]
    d_r1 = norm_back(d_n1, n1, m.r1[...], vec(GAIN1))
    m.dR1[...] = d_r1
    d_a = d_r1.astype(BF)
    m.dAall[w] = d_a
    for g in range(W):
        m.dOs[g] = dot_nt(d_a, m.Outp[g]).astype(BF)
        dev = att_device(w, g, block_part)
        send(m.dOs.at[g], m.dOr.at[block_slot], m.s_do.at[g], m.r_do.at[block_slot], dev,
             jnp.logical_not(is_me(dev)))

        @pl.when(is_me(dev))
        def _():
            m.dOr[block_slot] = m.dOs[g]

    gather_start(m.dAall, m.s_da, m.r_da)
    for k in (2, 3, 1):
        send(m.Mix.at[jnp.bitwise_xor(w, k)], m.MixT.at[w], m.s_mt.at[k], m.r_mt.at[k], peer(k))
    m.MixT[w] = m.Mix[w]
    m.gv[0:1, :] = col_sum(d_n1 * n1)
    m.gv[1:2, :] = col_sum(d_n1)
    m.gv[4:5, :] = col_sum(d_a.astype(F32))

    def flat(ref):
        return ref[...].reshape(Q, ref.shape[-1])

    def put_grad(name, dest, index, lhs, rhs, parts):
        rows = lhs.shape[-1] // parts
        for i in range(parts):
            val = dot_tn(lhs[:, :, i * rows : (i + 1) * rows].reshape(Q, rows), flat(rhs)).astype(BF)
            if cfg.fused:
                ch = cfg.grads[name][0]
                n = rows // (2 * ch)
                dest[i * n : (i + 1) * n] = val.reshape(n, 2, ch, val.shape[-1])
            else:
                dest[i * rows : (i + 1) * rows, :] = val

    put_grad("down", m.Gdown if cfg.fused else gdown_ref, 0, m.Gs, m.dFall, 2)
    put_grad("up", m.Gup if cfg.fused else gup_ref, 1, m.N1all, m.dHs, 2)
    m.gv[6:7, :] = col_sum(flat(m.dHs).astype(F32))

    for j in range(W):
        arrive(m.dOr.at[j], m.r_do.at[j], jnp.logical_not(is_me((j * R + r_att, s))))
        d_o = m.dOr[j]
        cols = slice(j * B, (j + 1) * B)
        for h in range(HW):
            m.Dm[h, cols, :] = jnp.where(v_lane(h), d_o, jnp.zeros_like(d_o))
        prod = m.OT[:, cols] * d_o.astype(F32).T
        for h in range(HW):
            m.drow[h : h + 1, cols] = col_sum(prod[OFF + h * HEAD : OFF + (h + 1) * HEAD, :])
    m.dQT[...] = jnp.zeros(m.dQT.shape, F32)

    def attend_back(step, carry):
        chunk = lax.rem((r_att + 1) * PER_SET + step, R * PER_SET)
        rows = pl.ds(pl.multiple_of(chunk * KC, KC), KC)
        keys = m.KV[rows, 0:DP]
        values = m.KV[rows, KVW - DP : KVW]
        keys_t = keys.T
        live = alive(chunk)
        d_k = jnp.zeros((KC, DP), F32)
        d_v = jnp.zeros((KC, DP), F32)
        for h in range(HW):
            scores = dot_nt(keys, m.Qm[h])
            prob = jnp.where(live, jnp.exp(scores - m.lrow[h : h + 1, :]), 0.0)
            d_prob = dot_nt(values, m.Dm[h])
            d_s = (prob * (d_prob - m.drow[h : h + 1, :])).astype(BF)
            d_k = d_k + dot(d_s, m.Qm[h])
            d_v = d_v + dot(prob.astype(BF), m.Dm[h])
            a, b = h * HEAD, (h + 1) * HEAD
            m.dQT[a:b, :] = m.dQT[a:b, :] + dot(keys_t[a:b, :], d_s)
        lead = KVW - DP
        m.dKVf[rows, 0:lead] = d_k[:, 0:lead]
        m.dKVf[rows, lead:DP] = d_k[:, lead:] + d_v[:, 0 : DP - lead]
        m.dKVf[rows, DP:KVW] = d_v[:, DP - lead :]
        return carry

    lax.fori_loop(0, (R - 1) * PER_SET, attend_back, 0)
    for k in range(1, R):
        r = lax.rem(r_att + k, R)
        m.dKVs[r] = m.dKVf[pl.ds(pl.multiple_of(r * Q, Q), Q), :].astype(BF)
        send(m.dKVs.at[r], m.dKVr.at[r_att], m.s_dkv.at[k - 1], m.r_dkv.at[r_att], att_device(s, g_att, r))
    lax.fori_loop((R - 1) * PER_SET, R * PER_SET, attend_back, 0)
    for k in range(1, R):
        arrive(m.dKVr.at[lax.rem(r_att + k, R)], m.r_dkv.at[lax.rem(r_att + k, R)])
    for j in range(W):
        d_kv = m.dKVf[pl.ds(pl.multiple_of(r_att * Q + j * B, B), B), :]
        for k in range(1, R):
            d_kv = d_kv + m.dKVr[lax.rem(r_att + k, R), j * B : (j + 1) * B, :].astype(F32)
        m.dqs[j, :, 0:KVW] = d_kv.astype(BF)
        d_q = m.dQT[:, j * B : (j + 1) * B].T * (HEAD**-0.5)
        m.dqs[j, :, KVW:MW] = jnp.where(lanes < DW, d_q, 0.0).astype(BF)
        dev = (j * R + r_att, g_att)
        send(m.dqs.at[j], m.dqr.at[s], m.s_dq.at[j], m.r_dq.at[s], dev, jnp.logical_not(is_me(dev)))

        @pl.when(is_me(dev))
        def _():
            m.dqr[s] = m.dqs[j]

    for k in (1, 2, 3):
        gather_wait(m.dAall, m.s_da, m.r_da, k)
        arrive(m.MixT.at[jnp.bitwise_xor(w, k)], m.r_mt.at[k])
    put_grad("out", m.Gout if cfg.fused else gout_ref, 2, m.MixT, m.dAall, 1)

    for t in range(W):
        arrive(m.dqr.at[t], m.r_dq.at[t], jnp.logical_not(is_me(att_device(t, w, block_part))))
    d_x = scatter_sum(lambda t: dot_nt(m.dqr[t], m.Wc[...]), m.dxs, m.dxr, m.s_dx, m.r_dx)
    gx_ref[...] = (m.dR1[...] + d_x).astype(BF)
    put_grad("qkv", m.Gqkv if cfg.fused else gqkv_ref, 3, m.Xall, m.dqr, 2)
    m.gv[7:8, 0:MW] = col_sum(flat(m.dqr).astype(F32))
    m.gv[7:8, MW:D] = jnp.zeros((1, D - MW), F32)

    if not cfg.fused:
        gvec_ref[0] = m.gv[...]
    else:
        NZ = C // 2
        z, x = lax.div(c, 2), lax.rem(c, 2)
        beside = (c + 1 - 2 * x, w)
        G = SimpleNamespace(**{k: getattr(m, k) for k in vars(m)})

        def buf(kind, name):
            return getattr(G, kind + name)

        def zpeer(k):
            return lax.rem(z + k, NZ)

        def halves_start(name):
            for k in list(range(1, NZ)) + [0]:
                zi = zpeer(k)
                send(buf("G", name).at[zi, 1 - x], buf("X", name).at[zi], buf("s_gx", name).at[k],
                     buf("r_gx", name).at[k], beside)

        def planes_start(name):
            for k in range(1, NZ):
                zi = zpeer(k)
                arrive(buf("X", name).at[zi], buf("r_gx", name).at[k])
                buf("S", name)[zi] = (buf("G", name)[zi, x].astype(F32) + buf("X", name)[zi].astype(F32)).astype(BF)
                send(buf("S", name).at[zi], buf("Z", name).at[z], buf("s_gz", name).at[k], buf("r_gz", name).at[k],
                     (zi * 2 + x, w))

        def reduce_end(name):
            to_rows = cfg.grads[name][2]
            arrive(buf("X", name).at[z], buf("r_gx", name).at[0])
            acc = buf("G", name)[z, x].astype(F32) + buf("X", name)[z].astype(F32)
            for k in range(1, NZ):
                zi = lax.rem(z + NZ - k, NZ)
                arrive(buf("Z", name).at[zi], buf("r_gz", name).at[k])
                acc = acc + buf("Z", name)[zi].astype(F32)
            if to_rows:
                buf("R", name)[...] = acc.astype(BF)
                home = block_slot

                @pl.when(home == w)
                def _():
                    buf("F", name)[x, w] = buf("R", name)[...]

                send(buf("R", name), buf("F", name).at[x, w], buf("s_gw", name).at[0], buf("r_gw", name).at[w],
                     (c, home), home != w)
            else:
                buf("F", name)[z, x] = acc.astype(BF)
                fin = buf("F", name)
                for k in range(1, NZ):
                    send(fin.at[z, x], fin.at[z, x], buf("s_ga", name).at[k], buf("r_ga", name).at[k],
                         (zpeer(k) * 2 + x, w))
                send(fin.at[z, x], fin.at[z, x], buf("s_gf", name).at[0], buf("r_gf", name).at[0], beside)

        def spread(name):
            fin = buf("F", name)
            if cfg.grads[name][2]:
                at_home = block_slot == w
                for k in range(1, W):
                    t = jnp.bitwise_xor(w, k)
                    arrive(fin.at[x, t], buf("r_gw", name).at[t], at_home)
                for k in range(1, NZ):
                    send(fin.at[x], fin.at[x], buf("s_ga", name).at[k], buf("r_ga", name).at[0],
                         (zpeer(k) * 2 + x, w), at_home)
                arrive(fin.at[x], buf("r_ga", name).at[0], jnp.logical_not(at_home))
                send(fin.at[x], fin.at[x], buf("s_gf", name).at[0], buf("r_gf", name).at[0], beside)
            else:
                for k in range(1, NZ):
                    zi = lax.rem(z + NZ - k, NZ)
                    arrive(fin.at[zi, x], buf("r_ga", name).at[k])
                    send(fin.at[zi, x], fin.at[zi, x], buf("s_gf", name).at[k], buf("r_gf", name).at[k], beside)

        def finish(name, dest):
            fin = buf("F", name)
            ch, cols, to_rows = cfg.grads[name]
            if to_rows:
                arrive(fin.at[1 - x], buf("r_gf", name).at[0])
                for i in range(2):
                    for t in range(W):
                        dest[i * ch : (i + 1) * ch, t * cols : (t + 1) * cols] = fin[i, t]
            else:
                for k in range(NZ):
                    zi = lax.rem(z + NZ - k, NZ)
                    arrive(fin.at[zi, 1 - x], buf("r_gf", name).at[k])
                dest[...] = fin[...].reshape(dest.shape)

        order = ("up", "down", "qkv", "out")
        send(m.gv, m.Vx, m.s_vx.at[0], m.r_vx.at[0], beside)
        for name in order:
            halves_start(name)
        arrive(m.Vx, m.r_vx.at[0])
        m.Vy[...] = m.gv[...] + m.Vx[...]
        for k in range(1, NZ):
            send(m.Vy, m.Vz.at[z], m.s_vz.at[k], m.r_vz.at[k], (zpeer(k) * 2 + x, w))
        for name in order:
            planes_start(name)
        total = m.Vy[...]
        for k in range(1, NZ):
            zi = lax.rem(z + NZ - k, NZ)
            arrive(m.Vz.at[zi], m.r_vz.at[k])
            total = total + m.Vz[zi]
        m.Vw[w] = total
        for k in (1, 2, 3):
            send(m.Vw.at[w], m.Vw.at[w], m.s_vw.at[k], m.r_vw.at[k], peer(k))
        for name in order:
            reduce_end(name)
        for name in order:
            spread(name)
        for k in (1, 2, 3):
            arrive(m.Vw.at[jnp.bitwise_xor(w, k)], m.r_vw.at[k])
        gvec_ref[...] = m.Vw[...]
        for name, dest in zip(order, (gup_ref, gdown_ref, gqkv_ref, gout_ref)):
            finish(name, dest)

    for pred, end in drains:
        if pred is None:
            end()
        else:
            pl.when(pred)(end)


def body(C, W, tokens, lengths, qkv_weight, out_weight, up_weight, down_weight, qv_bias, out_bias, up_bias,
         down_bias, gain_one, shift_one, gain_two, shift_two, cotangent):
    _, B, D = tokens.shape
    FW = down_weight.shape[0]
    DW = D // W
    DP = -(-DW // 128) * 128
    KVW = 2 * DW
    MW = KVW + DP
    R = C // W
    cfg = SimpleNamespace(C=C, W=W, B=B, D=D, FW=FW, DW=DW, DP=DP, KVW=KVW, MW=MW, R=R, HW=HEADS // W)
    cfg.fused = R == 2 and D % (16 * C) == 0
    cfg.grads = dict(up=(D // C, FW, True), down=(FW // C, D, False), qkv=(D // C, MW, True), out=(DP // C, D, False))
    w = lax.axis_index("wa")

    thirds = qkv_weight.reshape(DW, 3, W, DW)
    pad = jnp.zeros((W, DW, DP - DW), BF)
    wq = jnp.concatenate([thirds[:, i].transpose(1, 0, 2) for i in (1, 2, 0)] + [pad], 2)
    qv = lax.dynamic_update_slice(jnp.zeros((2 * D,), BF), qv_bias, (w * (2 * D // W),)).reshape(2, W, 1, DW)
    bias = jnp.concatenate([jnp.zeros((W, 1, DW), BF), qv[1], qv[0], jnp.zeros((W, 1, DP - DW), BF)], 2)
    bias = jnp.pad(bias, ((0, 0), (0, 15), (0, 0)))
    small = jnp.stack([out_bias, down_bias, gain_one, shift_one, gain_two, shift_two]).astype(F32)
    vec = lax.dynamic_update_slice(jnp.zeros((VROWS, D), F32), small, (0, w * DW))
    vec = lax.dynamic_update_slice(vec, jnp.broadcast_to(lengths.astype(F32)[:, None], (1, D)), (LEN + w, 0))

    plan = make_plan(cfg)
    names = list(plan)
    vm = pl.BlockSpec(memory_space=pltpu.VMEM)
    hbm = pl.BlockSpec(memory_space=pl.ANY)
    shape = jax.ShapeDtypeStruct
    if cfg.fused:
        outs = [shape((DW, W * MW), BF), shape((DP, D), BF), shape((DW, W * FW), BF), shape((FW, D), BF),
                shape((W, GROWS, D), F32)]
    else:
        outs = [shape((D, MW), BF), shape((DP, D), BF), shape((D, FW), BF), shape((FW, D), BF),
                shape((1, GROWS, D), F32)]
    outs = [shape((B, D), BF), shape((B, D), BF)] + outs
    args = (tokens.reshape(B, D), cotangent.reshape(B, D), wq, bias, vec, up_bias.astype(F32).reshape(1, FW),
            out_weight, up_weight, down_weight)
    y, gx, gqkv, gout, gup, gdown, gvec = pl.pallas_call(
        functools.partial(layer_kernel, cfg, names, len(args)),
        out_shape=outs,
        in_specs=[hbm, hbm, hbm, hbm, hbm, vm, hbm, hbm, hbm],
        out_specs=[vm] * len(outs),
        scratch_shapes=[plan[n] for n in names],
        compiler_params=pltpu.CompilerParams(collective_id=0, has_side_effects=True, vmem_limit_bytes=60 << 20),
        name="layer",
    )(*args)
    if not cfg.fused:
        def to_rows(g):
            g = lax.psum(g, "ctx").reshape(W, DW, g.shape[1])
            return lax.all_to_all(g, "wa", 0, 0, tiled=True).transpose(1, 0, 2).reshape(DW, -1)

        gqkv, gup = to_rows(gqkv), to_rows(gup)
        gout, gdown, gvec = lax.psum((gout, gdown, gvec), "ctx")
        gvec = lax.all_gather(gvec, "wa", axis=0, tiled=True)
    gq = gqkv.reshape(DW, W, MW).astype(F32)
    gqkv = jnp.concatenate(
        [gq[:, :, a : a + DW].reshape(DW, D) for a in (KVW, 0, DW)], 1)
    own = lax.dynamic_slice_in_dim(jnp.sum(gvec, 0)[0:6], w * DW, DW, 1)
    g_upb = lax.dynamic_slice_in_dim(gvec, w, 1, 0)[0, 6]
    g_qv = jnp.concatenate([gvec[:, 7, KVW : KVW + DW].reshape(D), gvec[:, 7, DW:KVW].reshape(D)])
    g_qv = lax.dynamic_slice_in_dim(g_qv, w * (2 * D // W), 2 * D // W)
    return (
        y.reshape(1, B, D),
        gx.reshape(1, B, D),
        gqkv,
        gout[DP - DW :].astype(F32),
        gup.astype(F32),
        gdown.astype(F32),
        g_qv,
        own[4],
        g_upb,
        own[5],
        own[0],
        own[1],
        own[2],
        own[3],
    )


def solution(mesh):
    tok, vec, mat = P("wa", "ctx", None), P("wa"), P("wa", None)
    return jax.shard_map(
        functools.partial(body, mesh.shape["ctx"], mesh.shape["wa"]),
        mesh=mesh,
        in_specs=(tok, vec, mat, mat, mat, mat) + (vec,) * 8 + (tok,),
        out_specs=(tok, tok, mat, mat, mat, mat) + (vec,) * 8,
        check_vma=False,
    )
```

time: 908 us -> 285 us (0.31)
  the two profiles are of different devices: /device:TPU:0 before, /device:TPU:25 now
where the time goes in v1:
time: 285 us
  Pallas kernels  254 us (89%)
  local copies, waits for them, and re-layouts  20.6 us (7%)
  other arithmetic  8.87 us (3%)
    pallas_call x1, Pallas kernels, body(): pl.pallas_call(functools.partial(layer_kernel, cfg, names, len(args)), ou...  254 us

profile of v1, /device:TPU:25, one launch (start us, length us, event | category | flops | bytes accessed | tf_op | source)
XLA Modules:
  0.0 284.8 jit_solution(13934006998915809824)
XLA Ops:
  0.7 0.9 dynamic_update_slice.9
  1.5 0.1 squeeze.48
  1.6 0.1 squeeze.49
  1.7 0.1 pad.17.clone
  1.8 0.1 maximum_maximum_fusion.1
  1.9 0.6 pad.4.refs_3_
  2.6 0.7 stack.21
  3.2 0.7 stack.22
  3.9 0.7 stack.23
  4.5 0.7 stack.24
  5.2 0.7 stack.25
  5.9 0.7 stack.26
  6.6 0.8 dynamic_update_slice.10
  8.1 0.1 dynamic_update_slice.11.refs_4_
  8.2 0.0 copy-start.2
  8.2 2.9 %reshape.86 = bf16[192,3,4,192]{3,2,1,0:T(4,128)(2,1)S(1)} reshape(bf16[192,2304]{1,0:T(8,128)(2,1)} %param.17) | data formatting | bytes 1769472 | tf_op jit(solution)/shard_map/reshape | solution.py:635
  11.1 0.4 fusion.2
  11.5 0.0 copy-done.2
  11.5 0.1 copy_bitcast_fusion
  11.6 0.0 copy-start.6
  11.7 1.3 maximum_maximum_fusion.refs_2_
  13.0 0.0 copy-done.6
  13.0 0.6 reshape.95.refs_5_
  13.6 253.9 %layer.1 = (bf16[128,768]{1,0:T(8,128)(2,1)}, bf16[128,768]{1,0:T(8,128)(2,1)}, bf16[192,2560]{1,0:T(8,128)(2,1)}, bf16[256,768]{1,0:T(8,128)(2,1)}, bf16[192,30...) custom-call(bf16[128,768]{1,0:T(8,128)(2,1)} %bitcast.26, bf16[128,768]{1,0:T(8,128)(2,1)} %bitcast.27, ...), custom_call_target="tpu_custom_call" | custom-call | tf_op jit(solution)/shard_map/layer/pallas_call | solution.py:659
  267.5 0.9 slice_reduce_fusion
  268.4 0.1 reshape_squeeze.6
  268.5 0.1 reshape_squeeze.7
  268.6 0.7 fusion
  269.2 1.9 reshape.96
  271.2 1.5 fusion.1
  272.7 1.6 reshape.91
  274.3 0.5 reshape.92
  274.8 0.5 reshape.93
  275.3 0.0 copy-start.5
  275.3 1.3 pad_maximum_fusion
  276.7 0.0 copy-done.5
  276.7 0.7 fusion.3
  277.4 0.6 dynamic-slice_reduce_fusion
  278.0 0.0 copy-start
  278.0 3.0 %convert_element_type.29 = f32[192,3072]{1,0:T(8,128)} convert(bf16[192,3072]{1,0:T(8,128)(2,1)} %get-tuple-element.25) | non-fusion elementwise | flops 589824 | bytes 3538944 | tf_op jit(solution)/shard_map/convert_element_type | solution.py:688
  281.0 0.0 copy-done
  281.0 0.0 copy-start.1
  281.0 0.0 copy-start.4
  281.0 0.0 copy-start.3
  281.0 1.6 convert_element_type.30
  282.6 0.0 copy-done.1
  282.6 0.9 slice_convert_fusion
  283.4 0.0 copy-done.4
  283.4 0.7 copy.47
  284.1 0.0 copy-done.3
  284.1 0.7 copy.48
  (11 shorter events, 0.1 us)
Async XLA Ops:
  8.2 3.3 %copy-start.2 = (f32[16,768]{1,0:T(8,128)}, f32[16,768]{1,0:T(8,128)S(1)}, u32[]{:S(2)}) copy-start(f32[16,768]{1,0:T(8,128)S(1)} %dynamic_update_slice.11.refs_4_) | copy-start | bytes 147460
  11.6 1.4 copy-start.6
  275.3 1.3 copy-start.5
  278.0 3.0 %copy-start = (bf16[768,768]{1,0:T(8,128)(2,1)S(1)}, bf16[768,768]{1,0:T(8,128)(2,1)}, u32[]{:S(2)}) copy-start(bf16[768,768]{1,0:T(8,128)(2,1)} %get-tuple-element.26) | copy-start | bytes 3538948
  281.0 1.6 copy-start.1
  281.0 2.4 copy-start.4
  281.0 3.1 %copy-start.3 = (bf16[128,768]{1,0:T(8,128)(2,1)S(1)}, bf16[128,768]{1,0:T(8,128)(2,1)}, u32[]{:S(2)}) copy-start(bf16[128,768]{1,0:T(8,128)(2,1)} %get-tuple-element.22) | copy-start | bytes 589828

commit v2 on v1

v2 whole, which is shorter than its diff:
```python
import functools
import math
from types import SimpleNamespace

import jax
import jax.numpy as jnp
from jax import lax
from jax.experimental import pallas as pl
from jax.experimental.pallas import tpu as pltpu
from jax.sharding import PartitionSpec as P

HEADS = 12
HEAD = 64
EPS = 1e-12
FLOOR = -1e30
MESH = pl.DeviceIdType.MESH
BF = jnp.bfloat16
F32 = jnp.float32

OUTB, DOWNB, GAIN1, SHIFT1, GAIN2, SHIFT2, QVB = range(7)
UPB, LEN = 8, 12
VROWS = 16
GROWS = 8


def dot(a, b):
    return lax.dot_general(a, b, (((1,), (0,)), ((), ())), preferred_element_type=F32)


def dot_nt(a, b):
    return lax.dot_general(a, b, (((1,), (1,)), ((), ())), preferred_element_type=F32)


def dot_tn(a, b):
    return lax.dot_general(a, b, (((0,), (0,)), ((), ())), preferred_element_type=F32)


def norm_stats(v):
    center = v - jnp.mean(v, -1, keepdims=True)
    rstd = lax.rsqrt(jnp.mean(center * center, -1, keepdims=True) + EPS)
    return center * rstd, rstd


def norm_back(dy, normed, rstd, gain):
    dn = dy * gain
    return rstd * (
        dn - jnp.mean(dn, -1, keepdims=True) - normed * jnp.mean(dn * normed, -1, keepdims=True)
    )


def col_sum(v):
    return jnp.sum(v, 0, keepdims=True)


def make_plan(cfg):
    C, W, B, D, FW, DW, DP, KVW, MW, R = (
        cfg.C, cfg.W, cfg.B, cfg.D, cfg.FW, cfg.DW, cfg.DP, cfg.KVW, cfg.MW, cfg.R)
    V = pltpu.VMEM
    dma = pltpu.SemaphoreType.DMA
    Q = W * B
    plan = dict(
        Xall=V((W, B, D), BF), Wc=V((D, MW), BF), Wq=V((DW, 3 * D), BF), Ws=V((W, DW, MW), BF), Vv=V((W, VROWS, DW), F32),
        Vs=V((8, D), F32), Outp=V((W, DP, D), BF), Upc=V((D, FW), BF), Dn=V((FW, D), BF), Cot=V((B, D), BF),
        QKVs=V((W, B, MW), BF), Rq=V((W, B, MW), BF), KV=V((R * Q, KVW), BF),
        Qm=V((cfg.HW, Q, DP), BF), Dm=V((cfg.HW, Q, DP), BF),
        mrow=V((8, Q), F32), lrow=V((8, Q), F32), bias=V((8, MW), F32), upb=V((8, cfg.FW), F32), drow=V((8, Q), F32), OT=V((DP, Q), F32), dQT=V((DP, Q), F32),
        Osend=V((W, B, DP), BF), Mix=V((W, B, DP), BF), MixT=V((W, B, DP), BF),
        N1f=V((B, D), F32), n1=V((B, D), F32), n2=V((B, D), F32), r1=V((B, 1), F32),
        N1all=V((W, B, D), BF), Hp=V((W, B, FW), F32), Gs=V((W, B, FW), BF),
        Fs=V((W, B, D), BF), Fr=V((3, B, D), BF), dR2=V((B, D), F32), dFall=V((W, B, D), BF),
        dHs=V((W, B, FW), BF), dNs=V((W, B, D), BF), dNr=V((3, B, D), BF), dR1=V((B, D), F32),
        dAall=V((W, B, D), BF), dOs=V((W, B, DP), BF), dOr=V((W, B, DP), BF),
        dKVf=V((Q, KVW), F32), dKVs=V((R - 1, Q, KVW), BF), dKVr=V((R - 1, Q, KVW), BF),
        dqs=V((W, B, MW), BF), dqr=V((W, B, MW), BF), dxs=V((W, B, D), BF), dxr=V((3, B, D), BF),
        gv=V((GROWS, D), F32),
    )
    sems = dict(
        x=4, wq=4, vv=4, ow=4, uw=4, own=7,
        q=W, kv=(R - 1) * W, o=W, mt=4, n=4, f=4, df=4, dn=4, da=4, do=W, dkv=R - 1, dq=W, dx=4,
    )
    recvs = dict(sems, kv=R * W)
    if cfg.fused:
        for name, (pieces, ch, cols, to_rows) in cfg.grads.items():
            plan["G" + name] = V((pieces, 2, 2, ch, cols), BF)
            plan["X" + name] = V((pieces, 2, ch, cols), BF)
            plan["T" + name] = V((pieces, ch, cols), BF)
            plan["Y" + name] = V((pieces, ch, cols), BF)
            plan["U" + name] = V((pieces, ch, cols), BF)
            plan["Z" + name] = V((pieces, ch, cols), BF)
            for kind in ("g1", "g2", "g3", "g4", "g5", "g6"):
                sems[kind + name] = pieces
                recvs[kind + name] = pieces
            if to_rows:
                plan["R" + name] = V((pieces, ch, cols), BF)
        plan.update(Va=V((3, GROWS, D), F32), Vb=V((3, GROWS, D), F32), Vt=V((W, GROWS, DW), F32),
                    Vw=V((W, GROWS, DW), F32))
        sems.update(v1=3, vw=W)
        recvs.update(v1=3, vw=W)
    for name, n in sems.items():
        plan["s_" + name] = dma((n,))
    for name, n in recvs.items():
        plan["r_" + name] = dma((n,))
    return plan


class make_sums:
    def __init__(self, cfg, m, c, w, send, arrive):
        self.cfg, self.m, self.w, self.send, self.arrive = cfg, m, w, send, arrive
        self.c = c
        self.x, self.near = lax.rem(c, 2), lax.rem(lax.div(c, 2), 2)
        self.partners = [(jnp.bitwise_xor(c, k), w) for k in (1, 2, 4)]
        self.waves = []

    def start(self, names):
        if self.cfg.fused:
            for name in names:
                for p in range(self.cfg.grads[name][0]):
                    self.one(name, p)

    def add(self, names, lag):
        if not self.cfg.fused:
            return
        items = [(n, p) for n in names for p in range(self.cfg.grads[n][0])]
        stages = [self.two, self.three, self.four, self.five, self.six, self.seven]
        waves = []
        for wave in range(len(items) + lag * (len(stages) - 1)):
            steps = [functools.partial(stages[k], *items[wave - lag * k])
                     for k in reversed(range(len(stages))) if 0 <= wave - lag * k < len(items)]
            waves.append(steps)
        old, merged = self.waves, []
        for i in range(max(len(old), len(waves))):
            merged.append((old[i] if i < len(old) else []) + (waves[i] if i < len(waves) else []))
        self.waves = merged

    def run(self, n):
        for wave in self.waves[:n]:
            for step in wave:
                step()
        del self.waves[:n]

    def ref(self, kind, name):
        return getattr(self.m, kind + name)

    def go(self, kind, name, p, src, dst, dev, pred=None):
        self.send(src, dst, self.ref("s_" + kind, name).at[p], self.ref("r_" + kind, name).at[p], dev, pred)

    def got(self, kind, name, p, dst, pred=None):
        self.arrive(dst, self.ref("r_" + kind, name).at[p], pred)

    def piece(self, name, k):
        return jnp.bitwise_xor(self.w, k) if self.cfg.grads[name][3] else k

    def one(self, name, k):
        p = self.piece(name, k)
        self.go("g1", name, k, self.ref("G", name).at[p, 1 - self.x], self.ref("X", name).at[k], self.partners[0])

    def two(self, name, k):
        g, other, t = self.ref("G", name), self.ref("X", name), self.ref("T", name)
        self.got("g1", name, k, other.at[k])
        far = 1 - self.near
        mine = g[self.piece(name, k), self.x, far].astype(F32)
        t[k] = (mine + other[k, far].astype(F32)).astype(BF)
        self.go("g2", name, k, t.at[k], self.ref("Y", name).at[k], self.partners[1])

    def three(self, name, k):
        g, other, y, u = (self.ref(kind, name) for kind in "GXYU")
        self.got("g2", name, k, y.at[k])
        n = self.near
        mine = g[self.piece(name, k), self.x, n].astype(F32)
        u[k] = (mine + other[k, n].astype(F32) + y[k].astype(F32)).astype(BF)
        self.go("g3", name, k, u.at[k], self.ref("Z", name).at[k], self.partners[2])

    def four(self, name, k):
        u, z, fin = (self.ref(kind, name) for kind in "UZF")
        self.got("g3", name, k, z.at[k])
        total = (u[k].astype(F32) + z[k].astype(F32)).astype(BF)
        if not self.cfg.grads[name][3] or k == 0:
            fin[self.piece(name, k), self.x, self.near] = total
            return
        done = self.ref("R", name)
        done[k] = total
        self.go("g4", name, k, done.at[k], fin.at[self.w, self.x, self.near], (self.c, jnp.bitwise_xor(self.w, k)))

    def five(self, name, k):
        here = self.ref("F", name).at[self.piece(name, k), self.x, self.near]
        if self.cfg.grads[name][3] and k > 0:
            self.got("g4", name, k, here)
        self.go("g5", name, k, here, here, self.partners[1])

    def six(self, name, k):
        fin, p = self.ref("F", name), self.piece(name, k)
        self.got("g5", name, k, fin.at[p, self.x, 1 - self.near])
        self.go("g6", name, k, fin.at[p, self.x], fin.at[p, self.x], self.partners[0])

    def seven(self, name, k):
        self.got("g6", name, k, self.ref("F", name).at[self.piece(name, k), 1 - self.x])


def layer_kernel(cfg, names, n_in, *refs):
    (x_ref, cot_ref, qkv_ref, vec_ref, out_ref, up_ref, down_ref) = refs[:n_in]
    y_ref, gx_ref, gqkv_ref, gout_ref, gup_ref, gdown_ref, gvec_ref = refs[n_in : n_in + 7]
    m = SimpleNamespace(**dict(zip(names, refs[n_in + 7 :])))
    if cfg.fused:
        m.Fqkv, m.Fout, m.Fup, m.Fdown = gqkv_ref, gout_ref, gup_ref, gdown_ref
    C, W, B, D, DW, DP, KVW, MW, R, HW = (
        cfg.C, cfg.W, cfg.B, cfg.D, cfg.DW, cfg.DP, cfg.KVW, cfg.MW, cfg.R, cfg.HW)
    OFF = DP - DW
    Q = W * B
    c = lax.axis_index("ctx")
    w = lax.axis_index("wa")
    block_part = lax.rem(c, R)
    block_slot = lax.div(c, R)
    s = lax.div(c, R)
    low = lax.rem(c, R)
    g_att = lax.div(w, 2) * 2 + lax.rem(low, 2)
    r_att = lax.div(low, 2) * 2 + lax.rem(w, 2)

    def att_device(t, g, r):
        return (t * R + lax.div(r, 2) * 2 + lax.rem(g, 2), lax.div(g, 2) * 2 + lax.rem(r, 2))

    def is_me(dev):
        return jnp.logical_and(dev[0] == c, dev[1] == w)

    drains = []

    def remote(src, dst, ss, rs, dev):
        return pltpu.make_async_remote_copy(
            src_ref=src, dst_ref=dst, send_sem=ss, recv_sem=rs, device_id=dev, device_id_type=MESH)

    def send(src, dst, ss, rs, dev, pred=None):
        def go():
            remote(src, dst, ss, rs, dev).start()

        def end():
            remote(src, dst, ss, rs, dev).wait_send()

        if pred is None:
            go()
        else:
            pl.when(pred)(go)
        drains.append((pred, end))

    def arrive(dst, rs, pred=None):
        def go():
            remote(dst, dst, rs, rs, (c, w)).wait_recv()

        if pred is None:
            go()
        else:
            pl.when(pred)(go)

    barrier = pltpu.get_barrier_semaphore()

    def greet(i, carry):
        ci, wi = lax.div(i, W), lax.rem(i, W)

        @pl.when(jnp.logical_not(is_me((ci, wi))))
        def _():
            pl.semaphore_signal(barrier, inc=1, device_id=(ci, wi), device_id_type=MESH)

        return carry

    lax.fori_loop(0, C * W, greet, 0)

    def return_barrier():
        pl.semaphore_wait(barrier, C * W - 1)

    def peer(k):
        return (c, jnp.bitwise_xor(w, k))

    def gather_start(buf, ss, rs):
        send(buf.at[w], buf.at[w], ss.at[2], rs.at[2], peer(2))
        send(buf.at[w], buf.at[w], ss.at[1], rs.at[1], peer(1))

    def gather_wait(buf, ss, rs, k):
        if k == 1:
            arrive(buf.at[jnp.bitwise_xor(w, 1)], rs.at[1])
        if k == 2:
            t = jnp.bitwise_xor(w, 2)
            arrive(buf.at[t], rs.at[2])
            send(buf.at[t], buf.at[t], ss.at[3], rs.at[3], peer(1))
        if k == 3:
            arrive(buf.at[jnp.bitwise_xor(w, 3)], rs.at[3])

    def scatter_sum(part, stage, recv, ss, rs, early=None, late=None):
        t3, t2, t1 = (jnp.bitwise_xor(w, k) for k in (3, 2, 1))
        stage[t3] = part(t3).astype(BF)
        send(stage.at[t3], recv.at[1], ss.at[1], rs.at[1], peer(1))
        mine2 = part(t2)
        stage[t1] = part(t1).astype(BF)
        send(stage.at[t1], recv.at[0], ss.at[0], rs.at[0], peer(1))
        if early:
            early()
        arrive(recv.at[1], rs.at[1])
        stage[t2] = (mine2 + recv[1].astype(F32)).astype(BF)
        send(stage.at[t2], recv.at[2], ss.at[2], rs.at[2], peer(2))
        own = part(w)
        if late:
            late()
        arrive(recv.at[0], rs.at[0])
        own = own + recv[0].astype(F32)
        arrive(recv.at[2], rs.at[2])
        return own + recv[2].astype(F32)

    def local(src, dst, sem):
        cp = pltpu.make_async_copy(src, dst, sem)
        cp.start()
        return cp

    rows_w = pl.ds(w * DW, DW)
    own = [
        local(qkv_ref, m.Wq, m.s_own.at[1]),
        local(x_ref, m.Xall.at[w], m.s_own.at[0]),
        local(vec_ref, m.Vv.at[w], m.s_own.at[2]),
        local(out_ref, m.Outp.at[w, pl.ds(OFF, DW)], m.s_own.at[3]),
        local(up_ref.at[:, pl.ds(pl.multiple_of(w * cfg.FW, cfg.FW), cfg.FW)], m.Upc.at[rows_w], m.s_own.at[4]),
        local(down_ref, m.Dn, m.s_own.at[5]),
        local(cot_ref, m.Cot, m.s_own.at[6]),
    ]
    own[0].wait()
    for g in range(W):
        for i, third in enumerate((1, 2, 0)):
            a = third * D + g * DW
            m.Ws[g, :, i * DW : (i + 1) * DW] = m.Wq[:, a : a + DW]
        m.Ws[g, :, 3 * DW : MW] = jnp.zeros((DW, MW - 3 * DW), BF)
    own[1].wait()
    own[2].wait()
    return_barrier()
    for k in (2, 3, 1):
        t = jnp.bitwise_xor(w, k)
        send(m.Ws.at[t], m.Wc.at[rows_w], m.s_wq.at[k], m.r_wq.at[k], peer(k))
        send(m.Vv.at[w], m.Vv.at[w], m.s_vv.at[k], m.r_vv.at[k], peer(k))
    gather_start(m.Xall, m.s_x, m.r_x)
    m.Wc[rows_w, :] = m.Ws[w]
    for t in range(W):
        m.Outp[t, 0:OFF, :] = jnp.zeros((OFF, D), BF)
    m.bias[...] = jnp.zeros(m.bias.shape, F32)
    for cp in own[3:]:
        cp.wait()
    for k in (1, 2, 3):
        t = jnp.bitwise_xor(w, k)
        arrive(m.Wc.at[pl.ds(t * DW, DW)], m.r_wq.at[k])
        arrive(m.Vv.at[t], m.r_vv.at[k])
        gather_wait(m.Xall, m.s_x, m.r_x, k)
    for k in (2, 3, 1):
        t = jnp.bitwise_xor(w, k)
        send(out_ref, m.Outp.at[w, pl.ds(OFF, DW)], m.s_ow.at[k], m.r_ow.at[k], peer(k))
    for k in (2, 3, 1):
        t = jnp.bitwise_xor(w, k)
        send(up_ref.at[:, pl.ds(pl.multiple_of(t * cfg.FW, cfg.FW), cfg.FW)], m.Upc.at[rows_w],
             m.s_uw.at[k], m.r_uw.at[k], peer(k))

    for t in range(W):
        m.Vs[0:6, t * DW : (t + 1) * DW] = m.Vv[t, 0:6, :]
        m.upb[0:1, t * DW : (t + 1) * DW] = m.Vv[w, UPB + t : UPB + t + 1, :]
    half, odd = lax.div(w, 2), lax.rem(w, 2)
    m.bias[0:1, DW : 2 * DW] = m.Vv[W // 2 + half, pl.ds(QVB + odd, 1), :]
    m.bias[0:1, 2 * DW : 3 * DW] = m.Vv[half, pl.ds(QVB + odd, 1), :]
    bias = m.bias[0:1, :]

    def vec(row):
        return m.Vs[row : row + 1, :]

    for k in range(W):
        t = lax.rem(s + 1 + k, W)
        m.QKVs[t] = (dot(m.Xall[t], m.Wc[...]) + bias).astype(BF)
        dev = att_device(t, w, block_part)
        send(m.QKVs.at[t], m.Rq.at[block_slot], m.s_q.at[k], m.r_q.at[block_slot], dev,
             jnp.logical_not(is_me(dev)))

        @pl.when(is_me(dev))
        def _():
            m.Rq[block_slot] = m.QKVs[t]

    lanes = lax.broadcasted_iota(jnp.int32, (1, DP), 1)

    def q_lane(h):
        return jnp.logical_and(lanes >= h * HEAD, lanes < (h + 1) * HEAD)

    def v_lane(h):
        return jnp.logical_and(lanes >= OFF + h * HEAD, lanes < OFF + (h + 1) * HEAD)

    for j in range(W):
        src = (j * R + r_att, g_att)
        arrive(m.Rq.at[j], m.r_q.at[j], jnp.logical_not(is_me(src)))
        kv_rows = pl.ds(pl.multiple_of(r_att * Q + j * B, B), B)
        for k in range(1, R):
            dev = att_device(s, g_att, lax.rem(r_att + k, R))
            send(m.Rq.at[j, :, pl.ds(0, KVW)], m.KV.at[kv_rows], m.s_kv.at[(k - 1) * W + j],
                 m.r_kv.at[r_att * W + j], dev)
        m.KV[kv_rows, :] = m.Rq[j, :, 0:KVW]
        q = m.Rq[j, :, KVW:MW] * jnp.asarray(HEAD**-0.5, BF)
        for h in range(HW):
            m.Qm[h, j * B : (j + 1) * B, :] = jnp.where(q_lane(h), q, jnp.zeros_like(q))
    for k in range(1, R):
        r = lax.rem(r_att + k, R)
        for j in range(W):
            arrive(m.KV.at[pl.ds(pl.multiple_of(r * Q + j * B, B), B)], m.r_kv.at[r * W + j])

    KC = 2 * B
    PER_SET = Q // KC
    len_s = m.Vv[s, LEN : LEN + 1, 0:1]

    def alive(chunk):
        r, half = lax.div(chunk, PER_SET), lax.rem(chunk, PER_SET)
        row = lax.broadcasted_iota(jnp.int32, (KC, Q), 0)
        later = (row >= B).astype(jnp.int32)
        place = ((2 * half + later) * R + r) * B + row - later * B
        return place.astype(F32) < len_s

    m.mrow[...] = jnp.full(m.mrow.shape, FLOOR, F32)
    m.lrow[...] = jnp.zeros(m.lrow.shape, F32)
    m.OT[...] = jnp.zeros(m.OT.shape, F32)

    def attend(chunk, carry):
        rows = pl.ds(pl.multiple_of(chunk * KC, KC), KC)
        keys = m.KV[rows, 0:DP]
        values_t = m.KV[rows, KVW - DP : KVW].T
        live = alive(chunk)
        for h in range(HW):
            scores = jnp.where(live, dot_nt(keys, m.Qm[h]), FLOOR)
            top = m.mrow[h : h + 1, :]
            new_top = jnp.maximum(top, jnp.max(scores, 0, keepdims=True))
            prob = jnp.exp(scores - new_top)
            factor = jnp.exp(top - new_top)
            m.mrow[h : h + 1, :] = new_top
            m.lrow[h : h + 1, :] = m.lrow[h : h + 1, :] * factor + col_sum(prob)
            a, b = OFF + h * HEAD, OFF + (h + 1) * HEAD
            m.OT[a:b, :] = m.OT[a:b, :] * factor + dot(values_t[a:b, :], prob.astype(BF))
        return carry

    lax.fori_loop(0, R * PER_SET, attend, 0)
    for h in range(HW):
        a, b = OFF + h * HEAD, OFF + (h + 1) * HEAD
        m.OT[a:b, :] = m.OT[a:b, :] / m.lrow[h : h + 1, :]
    m.lrow[0:HW, :] = m.mrow[0:HW, :] + jnp.log(m.lrow[0:HW, :])
    for j in range(W):
        m.Osend[j] = m.OT[:, j * B : (j + 1) * B].T.astype(BF)
        dev = (j * R + r_att, s)
        send(m.Osend.at[j], m.Mix.at[g_att], m.s_o.at[j], m.r_o.at[g_att], dev, jnp.logical_not(is_me(dev)))

        @pl.when(is_me(dev))
        def _():
            m.Mix[g_att] = m.Osend[j]

    for k in (1, 2, 3):
        arrive(m.Outp.at[jnp.bitwise_xor(w, k), pl.ds(OFF, DW)], m.r_ow.at[k])
    resid = m.Xall[w].astype(F32) + vec(OUTB)
    for g in range(W):
        arrive(m.Mix.at[g], m.r_o.at[g], jnp.logical_not(is_me(att_device(w, g, block_part))))
        resid = resid + dot(m.Mix[g], m.Outp[g])
    n1, r1 = norm_stats(resid)
    m.n1[...] = n1
    m.r1[...] = r1
    n1_full = n1 * vec(GAIN1) + vec(SHIFT1)
    m.N1f[...] = n1_full
    m.N1all[w] = n1_full.astype(BF)
    gather_start(m.N1all, m.s_n, m.r_n)

    for k in (1, 2, 3):
        arrive(m.Upc.at[pl.ds(jnp.bitwise_xor(w, k) * DW, DW)], m.r_uw.at[k])
    up_bias = m.upb[0:1, :]

    def expand(t):
        h = dot(m.N1all[t], m.Upc[...]) + up_bias
        phi = 0.5 * (1.0 + lax.erf(h * (2.0**-0.5)))
        m.Gs[t] = (h * phi).astype(BF)
        m.Hp[t] = phi + h * ((2.0 * math.pi) ** -0.5) * jnp.exp(-0.5 * h * h)

    expand(w)
    for k in (1, 2, 3):
        gather_wait(m.N1all, m.s_n, m.r_n, k)
        expand(jnp.bitwise_xor(w, k))

    ffn = scatter_sum(lambda t: dot(m.Gs[t], m.Dn[...]), m.Fs, m.Fr, m.s_f, m.r_f)
    n2, r2 = norm_stats(m.N1f[...] + ffn + vec(DOWNB))
    m.n2[...] = n2
    y_ref[...] = (n2 * vec(GAIN2) + vec(SHIFT2)).astype(BF)

    place = c * B + lax.broadcasted_iota(jnp.int32, (B, D), 0)
    dy = jnp.where(place.astype(F32) < m.Vv[w, LEN : LEN + 1, 0:1], m.Cot[...].astype(F32), 0.0)
    d_r2 = norm_back(dy, n2, r2, vec(GAIN2))
    m.dR2[...] = d_r2
    m.dFall[w] = d_r2.astype(BF)
    gather_start(m.dFall, m.s_df, m.r_df)
    m.gv[2:3, :] = col_sum(dy * n2)
    m.gv[3:4, :] = col_sum(dy)
    m.gv[5:6, :] = col_sum(m.dFall[w].astype(F32))

    def shrink(t):
        m.dHs[t] = (dot_nt(m.dFall[t], m.Dn[...]) * m.Hp[t]).astype(BF)

    shrink(w)
    for k in (1, 2, 3):
        gather_wait(m.dFall, m.s_df, m.r_df, k)
        shrink(jnp.bitwise_xor(w, k))

    def flat(ref):
        return ref[...].reshape(Q, ref.shape[-1])

    def put_grad(name, plain, lhs, rhs, parts, lead=0):
        rows = lhs.shape[-1] // parts
        for i in range(parts):
            val = dot_tn(lhs[:, :, i * rows : (i + 1) * rows].reshape(Q, rows), flat(rhs)).astype(BF)
            if cfg.fused:
                _, ch, cols, _ = cfg.grads[name]
                n = (rows - lead) // (4 * ch)
                getattr(m, "G" + name)[i * n : (i + 1) * n] = val[lead:].reshape(n, 2, 2, ch, cols)
            else:
                plain[i * rows : (i + 1) * rows, :] = val

    pump = make_sums(cfg, m, c, w, send, arrive)

    def early():
        put_grad("down", gdown_ref, m.Gs, m.dFall, 2)
        pump.start(("down",))

    def late():
        put_grad("up", gup_ref, m.N1all, m.dHs, 2)
        m.gv[6:7, :] = col_sum(flat(m.dHs).astype(F32))
        pump.add(("down", "up"), 2)
        pump.run(cfg.pump[0])

    d_n1 = scatter_sum(
        lambda t: dot_nt(m.dHs[t], m.Upc[...]), m.dNs, m.dNr, m.s_dn, m.r_dn, early, late) + m.dR2[...]
    n1 = m.n1[...]
    d_r1 = norm_back(d_n1, n1, m.r1[...], vec(GAIN1))
    m.dR1[...] = d_r1
    d_a = d_r1.astype(BF)
    m.dAall[w] = d_a
    for g in range(W):
        m.dOs[g] = dot_nt(d_a, m.Outp[g]).astype(BF)
        dev = att_device(w, g, block_part)
        send(m.dOs.at[g], m.dOr.at[block_slot], m.s_do.at[g], m.r_do.at[block_slot], dev,
             jnp.logical_not(is_me(dev)))

        @pl.when(is_me(dev))
        def _():
            m.dOr[block_slot] = m.dOs[g]

    pump.start(("up",))
    gather_start(m.dAall, m.s_da, m.r_da)
    for k in (2, 3, 1):
        send(m.Mix.at[jnp.bitwise_xor(w, k)], m.MixT.at[w], m.s_mt.at[k], m.r_mt.at[k], peer(k))
    m.MixT[w] = m.Mix[w]
    m.gv[0:1, :] = col_sum(d_n1 * n1)
    m.gv[1:2, :] = col_sum(d_n1)
    m.gv[4:5, :] = col_sum(d_a.astype(F32))

    pump.run(cfg.pump[1])
    for j in range(W):
        arrive(m.dOr.at[j], m.r_do.at[j], jnp.logical_not(is_me((j * R + r_att, s))))
        d_o = m.dOr[j]
        cols = slice(j * B, (j + 1) * B)
        for h in range(HW):
            m.Dm[h, cols, :] = jnp.where(v_lane(h), d_o, jnp.zeros_like(d_o))
        prod = m.OT[:, cols] * d_o.astype(F32).T
        for h in range(HW):
            m.drow[h : h + 1, cols] = col_sum(prod[OFF + h * HEAD : OFF + (h + 1) * HEAD, :])
    m.dQT[...] = jnp.zeros(m.dQT.shape, F32)

    def attend_back(step, carry):
        chunk = lax.rem((r_att + 1) * PER_SET + step, R * PER_SET)
        rows = pl.ds(pl.multiple_of(chunk * KC, KC), KC)
        keys = m.KV[rows, 0:DP]
        values = m.KV[rows, KVW - DP : KVW]
        keys_t = keys.T
        live = alive(chunk)
        d_k = jnp.zeros((KC, DP), F32)
        d_v = jnp.zeros((KC, DP), F32)
        for h in range(HW):
            scores = dot_nt(keys, m.Qm[h])
            prob = jnp.where(live, jnp.exp(scores - m.lrow[h : h + 1, :]), 0.0)
            d_prob = dot_nt(values, m.Dm[h])
            d_s = (prob * (d_prob - m.drow[h : h + 1, :])).astype(BF)
            d_k = d_k + dot(d_s, m.Qm[h])
            d_v = d_v + dot(prob.astype(BF), m.Dm[h])
            a, b = h * HEAD, (h + 1) * HEAD
            m.dQT[a:b, :] = m.dQT[a:b, :] + dot(keys_t[a:b, :], d_s)
        lead = KVW - DP
        d_kv = jnp.concatenate([d_k[:, 0:lead], d_k[:, lead:] + d_v[:, 0 : DP - lead], d_v[:, DP - lead :]], 1)
        place, part = lax.div(step, PER_SET), lax.rem(step, PER_SET)
        rows = pl.ds(pl.multiple_of(part * KC, KC), KC)
        if carry is None:
            m.dKVf[rows, :] = d_kv
        else:
            m.dKVs[place, rows, :] = d_kv.astype(BF)
        return carry

    lax.fori_loop(0, (R - 1) * PER_SET, attend_back, 0)
    for k in range(1, R):
        send(m.dKVs.at[k - 1], m.dKVr.at[R - k - 1], m.s_dkv.at[k - 1], m.r_dkv.at[R - k - 1],
             att_device(s, g_att, lax.rem(r_att + k, R)))
    pump.run(cfg.pump[2])
    lax.fori_loop((R - 1) * PER_SET, R * PER_SET, attend_back, None)
    pump.run(cfg.pump[3])
    for k in range(1, R):
        arrive(m.dKVr.at[k - 1], m.r_dkv.at[k - 1])
    for j in range(W):
        d_kv = m.dKVf[j * B : (j + 1) * B, :]
        for k in range(1, R):
            d_kv = d_kv + m.dKVr[k - 1, j * B : (j + 1) * B, :].astype(F32)
        m.dqs[j, :, 0:KVW] = d_kv.astype(BF)
        d_q = m.dQT[:, j * B : (j + 1) * B].T * (HEAD**-0.5)
        m.dqs[j, :, KVW:MW] = jnp.where(lanes < DW, d_q, 0.0).astype(BF)
        dev = (j * R + r_att, g_att)
        send(m.dqs.at[j], m.dqr.at[s], m.s_dq.at[j], m.r_dq.at[s], dev, jnp.logical_not(is_me(dev)))

        @pl.when(is_me(dev))
        def _():
            m.dqr[s] = m.dqs[j]

    for k in (1, 2, 3):
        gather_wait(m.dAall, m.s_da, m.r_da, k)
        arrive(m.MixT.at[jnp.bitwise_xor(w, k)], m.r_mt.at[k])
    put_grad("out", gout_ref, m.MixT, m.dAall, 1, OFF)
    pump.start(("out",))
    pump.run(cfg.pump[4])

    for t in range(W):
        arrive(m.dqr.at[t], m.r_dq.at[t], jnp.logical_not(is_me(att_device(t, w, block_part))))

    def early():
        put_grad("qkv", gqkv_ref, m.Xall, m.dqr, 2)
        pump.start(("qkv",))

    def late():
        m.gv[7:8, 0:MW] = col_sum(flat(m.dqr).astype(F32))
        m.gv[7:8, MW:D] = jnp.zeros((1, D - MW), F32)
        pump.add(("out", "qkv"), 1)
        pump.run(cfg.pump[5])

    d_x = scatter_sum(
        lambda t: dot_nt(m.dqr[t], m.Wc[...]), m.dxs, m.dxr, m.s_dx, m.r_dx, early, late)
    gx_ref[...] = (m.dR1[...] + d_x).astype(BF)

    if not cfg.fused:
        gvec_ref[0] = m.gv[...]
    else:
        total = m.gv[...]
        for i, dev in enumerate(pump.partners):
            m.Va[i] = total
            send(m.Va.at[i], m.Vb.at[i], m.s_v1.at[i], m.r_v1.at[i], dev)
            pump.run(cfg.pump[6])
            arrive(m.Vb.at[i], m.r_v1.at[i])
            total = total + m.Vb[i]
        for t in range(W):
            m.Vt[t, 0:6, :] = total[0:6, t * DW : (t + 1) * DW]
            m.Vt[t, 6:7, :] = total[7:8, 2 * DW : 3 * DW]
            m.Vt[t, 7:8, :] = total[7:8, DW : 2 * DW]
        m.Vw[w] = m.Vt[w]
        for k in (2, 3, 1):
            send(m.Vt.at[jnp.bitwise_xor(w, k)], m.Vw.at[w], m.s_vw.at[k], m.r_vw.at[k], peer(k))
        m.gv[6:7, :] = total[6:7, :]
        pump.run(cfg.pump[6])
        for k in (1, 2, 3):
            arrive(m.Vw.at[jnp.bitwise_xor(w, k)], m.r_vw.at[k])
        gvec_ref[0:6, 0:DW] = m.Vw[0, 0:6, :] + m.Vw[1, 0:6, :] + m.Vw[2, 0:6, :] + m.Vw[3, 0:6, :]
        for i in range(2):
            gvec_ref[6:7, i * DW : (i + 1) * DW] = m.Vw[2 * odd + i, pl.ds(6 + half, 1), :]
        gvec_ref[7:8, :] = m.gv[6:7, :]
        pump.run(1000)

    for pred, end in drains:
        if pred is None:
            end()
        else:
            pl.when(pred)(end)


def body(C, W, tokens, lengths, qkv_weight, out_weight, up_weight, down_weight, qv_bias, out_bias, up_bias,
         down_bias, gain_one, shift_one, gain_two, shift_two, cotangent):
    _, B, D = tokens.shape
    FW = down_weight.shape[0]
    DW = D // W
    DP = -(-DW // 128) * 128
    KVW = 2 * DW
    MW = KVW + DP
    R = C // W
    cfg = SimpleNamespace(C=C, W=W, B=B, D=D, FW=FW, DW=DW, DP=DP, KVW=KVW, MW=MW, R=R, HW=HEADS // W)
    cfg.fused = R == 2 and C == 8 and DW % 64 == 0 and FW % (64 * W) == 0
    cfg.grads = dict(down=(W, FW // W // 4, D, False), up=(W, DW // 4, FW, True), qkv=(W, DW // 4, MW, True),
                     out=(1, DW // 4, D, False))
    cfg.pump = (2, 2, 1, 1, 2, 2, 1)
    w = lax.axis_index("wa")
    small = [v.astype(F32) for v in (out_bias, down_bias, gain_one, shift_one, gain_two, shift_two, qv_bias, up_bias)]
    small.append(jnp.broadcast_to(lengths.astype(F32), ((VROWS - LEN) * DW,)))
    vec = jnp.concatenate(small).reshape(VROWS, DW)

    plan = make_plan(cfg)
    names = list(plan)
    vm = pl.BlockSpec(memory_space=pltpu.VMEM)
    hbm = pl.BlockSpec(memory_space=pl.ANY)
    shape = jax.ShapeDtypeStruct
    if cfg.fused:
        outs = [shape((n, 2, 2, ch, cols), BF) for n, ch, cols, _ in (cfg.grads[k] for k in ("qkv", "out", "up", "down"))]
        outs.append(shape((GROWS, D), F32))
    else:
        outs = [shape((D, MW), BF), shape((DP, D), BF), shape((D, FW), BF), shape((FW, D), BF),
                shape((1, GROWS, D), F32)]
    outs = [shape((B, D), BF), shape((B, D), BF)] + outs
    args = (tokens.reshape(B, D), cotangent.reshape(B, D), qkv_weight, vec, out_weight, up_weight, down_weight)
    y, gx, gqkv, gout, gup, gdown, gvec = pl.pallas_call(
        functools.partial(layer_kernel, cfg, names, len(args)),
        out_shape=outs,
        in_specs=[hbm] * len(args),
        out_specs=[vm] * len(outs),
        scratch_shapes=[plan[n] for n in names],
        compiler_params=pltpu.CompilerParams(collective_id=0, has_side_effects=True, vmem_limit_bytes=60 << 20),
        name="layer",
    )(*args)
    if cfg.fused:
        return finish(cfg, y, gx, gqkv, gout, gup, gdown, gvec)

    def to_rows(g):
        g = lax.psum(g, "ctx").reshape(W, DW, g.shape[1])
        return lax.all_to_all(g, "wa", 0, 0, tiled=True).transpose(1, 0, 2).reshape(DW, -1)

    gq = to_rows(gqkv).reshape(DW, W, MW).astype(F32)
    gup = to_rows(gup)
    gout, gdown, gvec = lax.psum((gout, gdown, gvec), "ctx")
    gvec = lax.all_gather(gvec, "wa", axis=0, tiled=True)
    gqkv = jnp.concatenate([gq[:, :, a : a + DW].reshape(DW, D) for a in (KVW, 0, DW)], 1)
    own = lax.dynamic_slice_in_dim(jnp.sum(gvec, 0)[0:6], w * DW, DW, 1)
    g_upb = lax.dynamic_slice_in_dim(gvec, w, 1, 0)[0, 6]
    g_qv = jnp.concatenate([gvec[:, 7, KVW : KVW + DW].reshape(D), gvec[:, 7, DW:KVW].reshape(D)])
    g_qv = lax.dynamic_slice_in_dim(g_qv, w * (2 * D // W), 2 * D // W)
    return (y.reshape(1, B, D), gx.reshape(1, B, D), gqkv, gout[DP - DW :].astype(F32), gup.astype(F32),
            gdown.astype(F32), g_qv, own[4], g_upb, own[5], own[0], own[1], own[2], own[3])


def finish_kernel(cfg, y, gx, gqkv, gout, gup, gdown, gvec, o_y, o_gx, o_qkv, o_out, o_up, o_down, o_qv, o_outb, o_upb,
                  o_downb, o_g1, o_s1, o_g2, o_s2):
    W, D, DW, MW, KVW = cfg.W, cfg.D, cfg.DW, cfg.MW, cfg.KVW
    o_y[0] = y[...]
    o_gx[0] = gx[...]
    for g in range(W):
        rows = gqkv[g].reshape(DW, MW).astype(F32)
        for third, a in enumerate((KVW, 0, DW)):
            o_qkv[:, third * D + g * DW : third * D + (g + 1) * DW] = rows[:, a : a + DW]
        o_up[:, g * cfg.FW : (g + 1) * cfg.FW] = gup[g].reshape(DW, cfg.FW).astype(F32)
    o_out[...] = gout[...].reshape(o_out.shape).astype(F32)
    o_down[...] = gdown[...].reshape(o_down.shape).astype(F32)
    o_qv[...] = gvec[6, 0 : 2 * DW]
    o_upb[...] = gvec[7, 0 : cfg.FW]
    for row, ref in enumerate((o_g1, o_s1, o_g2, o_s2, o_outb, o_downb)):
        ref[...] = gvec[row, 0:DW]


def finish(cfg, *arrays):
    B, D, DW, W, FW = cfg.B, cfg.D, cfg.DW, cfg.W, cfg.FW
    shapes = [(1, B, D)] * 2 + [(DW, 3 * D), (DW, D), (DW, W * FW), (FW, D), (2 * DW,), (DW,), (FW,)] + [(DW,)] * 5
    vm = pl.BlockSpec(memory_space=pltpu.VMEM)
    return pl.pallas_call(
        functools.partial(finish_kernel, cfg),
        out_shape=[jax.ShapeDtypeStruct(s, BF if i < 2 else F32) for i, s in enumerate(shapes)],
        in_specs=[vm] * len(arrays),
        out_specs=[vm] * len(shapes),
        name="results",
    )(*arrays)


def solution(mesh):
    tok, vec, mat = P("wa", "ctx", None), P("wa"), P("wa", None)
    return jax.shard_map(
        functools.partial(body, mesh.shape["ctx"], mesh.shape["wa"]),
        mesh=mesh,
        in_specs=(tok, vec, mat, mat, mat, mat) + (vec,) * 8 + (tok,),
        out_specs=(tok, tok, mat, mat, mat, mat) + (vec,) * 8,
        check_vma=False,
    )
```

time: 285 us -> 208 us (0.73)
  the two profiles are of different devices: /device:TPU:25 before, /device:TPU:0 now
where the time goes in v2:
time: 208 us
  Pallas kernels  201 us (97%)
  local copies, waits for them, and re-layouts  6.14 us (3%)
    pallas_call x1, Pallas kernels, body(): pl.pallas_call(functools.partial(layer_kernel, cfg, names, len(args)), ou...  195 us
    concatenate x1, local copies, waits for them, and re-layouts, body(): vec = jnp.concatenate(small).reshape(VROWS, DW)  5.46 us
    pallas_call x1, Pallas kernels, finish(): pl.pallas_call(functools.partial(finish_kernel, cfg), out_shape=[jax.Shap...  5.46 us

profile of v2, /device:TPU:0, one launch (start us, length us, event | category | flops | bytes accessed | tf_op | source)
XLA Modules:
  0.0 208.2 jit_solution(4823860030692726038)
XLA Ops:
  1.3 5.5 %concatenate.3 = f32[3072]{0:T(1024)S(1)} concatenate(bf16[192]{0:T(256)(128)(2,1)} %param.22, bf16[192]{0:T(256)(128)(2,1)} %param.24, bf16[192]{0:T(256)(128)(2,1)} %param.25, bf16[192]{0:T(256)(128)(2,1)} %param.26, bf16[192]{0:T(256)(128)(2,1)} %param.27, bf16[192]{0:T(256)(128)(2,1)} %param.28, bf16[384]{0:T(512)(128)(2,1)} %param.21, bf16[768]{0:T(1024)(128)(2,1)} %param.23, ...), dimensions={0} | concatenate | bytes 19968 | tf_op jit(solution)/shard_map/concatenate | solution.py:688
  6.8 0.7 reshape.39.refs_3_
  7.4 195.2 %layer.1 = (bf16[128,768]{1,0:T(8,128)(2,1)}, bf16[128,768]{1,0:T(8,128)(2,1)}, bf16[4,2,2,48,640]{4,3,2,1,0:T(8,128)(2,1)}, bf16[1,2,2,48,768]{4,3,2,1,0:T(8,12...) custom-call(bf16[128,768]{1,0:T(8,128)(2,1)} %bitcast.3, ...), custom_call_target="tpu_custom_call" | custom-call | tf_op jit(solution)/shard_map/layer/pallas_call | solution.py:703
  202.6 5.5 %results.1 = (bf16[1,128,768]{2,1,0:T(8,128)(2,1)}, bf16[1,128,768]{2,1,0:T(8,128)(2,1)}, f32[192,2304]{1,0:T(8,128)}, f32[192,768]{1,0:T(8,128)}, f32[192,3072]...) custom-call(bf16[128,768]{1,0:T(8,128)(2,1)} %get-tuple-element.21.y, ...), custom_call_target="tpu_custom_call" | custom-call | tf_op jit(solution)/shard_map/results/pallas_call | solution.py:754
  (1 shorter events, 0.0 us)

commit v3 on v2

--- a/solution.py
+++ b/solution.py
@@ -21,6 +21,28 @@
 UPB, LEN = 8, 12
 VROWS = 16
 GROWS = 8
+
+ALL = (0, 1, 2, 3)
+SCHEDULE = dict(
+    norm=((2, "down", (0,)), ),
+    sent0=((3, "down", (0,)), (2, "down", (1,)), ),
+    sent1=(),
+    sent2=((2, "down", (2,)), ),
+    sent3=(),
+    arrived=((3, "down", (1,)), (2, "down", (3,)), (2, "up", (0,)), ),
+    between=((4, "down", (0,)), (3, "down", (2,)), (2, "up", (1,)), ),
+    after=((5, "down", (0,)), (4, "down", (1,)), (3, "down", (3,)), (3, "up", (0,)), (2, "up", (2,)), ),
+    part=(),
+    dq1=(),
+    dq2=(),
+    dq3=(),
+    out=((5, "down", (1,)), (4, "down", (2,)), (3, "up", (1,)), (2, "up", (3,)), ),
+    wait0=((6, "down", (0,)), (5, "down", (2,)), (4, "down", (3,)), (4, "up", (0,)), (3, "up", (2,)), ),
+    wait1=((6, "down", (1,)), (5, "down", (3,)), (4, "up", (1,)), (3, "up", (3,)), ),
+    wait2=(),
+    wait3=((5, "up", (0,)), ),
+    qkv=((6, "down", (2,)), (6, "down", (3,)), (6, "up", (0,)), (4, "up", (2,)), (4, "up", (3,)), ),
+)
 
 
 def dot(a, b):
@@ -61,7 +83,7 @@
     plan = dict(
         Xall=V((W, B, D), BF), Wc=V((D, MW), BF), Wq=V((DW, 3 * D), BF), Ws=V((W, DW, MW), BF), Vv=V((W, VROWS, DW), F32),
         Vs=V((8, D), F32), Outp=V((W, DP, D), BF), Upc=V((D, FW), BF), Dn=V((FW, D), BF), Cot=V((B, D), BF),
-        QKVs=V((W, B, MW), BF), Rq=V((W, B, MW), BF), KV=V((R * Q, KVW), BF),
+        QKVs=V((W, B, MW), BF), Rq=V((W, B, DP), BF), KV=V((R * Q, KVW), BF),
         Qm=V((cfg.HW, Q, DP), BF), Dm=V((cfg.HW, Q, DP), BF),
         mrow=V((8, Q), F32), lrow=V((8, Q), F32), bias=V((8, MW), F32), upb=V((8, cfg.FW), F32), drow=V((8, Q), F32), OT=V((DP, Q), F32), dQT=V((DP, Q), F32),
         Osend=V((W, B, DP), BF), Mix=V((W, B, DP), BF), MixT=V((W, B, DP), BF),
@@ -75,24 +97,24 @@
         gv=V((GROWS, D), F32),
     )
     sems = dict(
-        x=4, wq=4, vv=4, ow=4, uw=4, own=7,
-        q=W, kv=(R - 1) * W, o=W, mt=4, n=4, f=4, df=4, dn=4, da=4, do=W, dkv=R - 1, dq=W, dx=4,
+        x=4, wq=4, wf=12, vv=4, ow=4, uw=4, own=6,
+        q=W, kv=W, kf=(R - 1) * W, o=W, mt=4, n=4, f=4, df=4, dn=4, da=4, do=W, dkv=R - 1, dq=W, dx=4,
     )
-    recvs = dict(sems, kv=R * W)
+    recvs = dict(sems, kf=R * W)
     if cfg.fused:
         for name, (pieces, ch, cols, to_rows) in cfg.grads.items():
             plan["G" + name] = V((pieces, 2, 2, ch, cols), BF)
-            plan["X" + name] = V((pieces, 2, ch, cols), BF)
+            plan["X" + name] = V((pieces, 3, ch, cols), BF)
             plan["T" + name] = V((pieces, ch, cols), BF)
             plan["Y" + name] = V((pieces, ch, cols), BF)
             plan["U" + name] = V((pieces, ch, cols), BF)
             plan["Z" + name] = V((pieces, ch, cols), BF)
             for kind in ("g1", "g2", "g3", "g4", "g5", "g6"):
-                sems[kind + name] = pieces
-                recvs[kind + name] = pieces
+                sems[kind + name] = 3 * pieces
+                recvs[kind + name] = 3 * pieces
             if to_rows:
                 plan["R" + name] = V((pieces, ch, cols), BF)
-        plan.update(Va=V((3, GROWS, D), F32), Vb=V((3, GROWS, D), F32), Vt=V((W, GROWS, DW), F32),
+        plan.update(Va=V((4, GROWS, D), F32), Vb=V((3, GROWS, D), F32), Vt=V((W, GROWS, DW), F32),
                     Vw=V((W, GROWS, DW), F32))
         sems.update(v1=3, vw=W)
         recvs.update(v1=3, vw=W)
@@ -103,60 +125,73 @@
     return plan
 
 
-class make_sums:
+class Sums:
     def __init__(self, cfg, m, c, w, send, arrive):
-        self.cfg, self.m, self.w, self.send, self.arrive = cfg, m, w, send, arrive
-        self.c = c
+        self.cfg, self.m, self.c, self.w, self.send, self.arrive = cfg, m, c, w, send, arrive
         self.x, self.near = lax.rem(c, 2), lax.rem(lax.div(c, 2), 2)
-        self.partners = [(jnp.bitwise_xor(c, k), w) for k in (1, 2, 4)]
-        self.waves = []
+        self.partners = [(jnp.bitwise_xor(c, k), w) for k in (1, 2, 4, 3)]
+        self.done = set()
+        self.long = (self.one, self.two, self.three, self.four, self.five, self.six, self.seven)
+        self.short = (self.quarters, self.quarters_sum, self.four, self.spread, self.spread_end)
+
+    def stages(self, name):
+        return self.long if name in ("up", "down", "out") else self.short
+
+    def step(self, k, name, p):
+        if self.cfg.fused:
+            self.stages(name)[k - 1](name, p)
+            self.done.add((k, name, p))
 
     def start(self, names):
-        if self.cfg.fused:
-            for name in names:
-                for p in range(self.cfg.grads[name][0]):
-                    self.one(name, p)
-
-    def add(self, names, lag):
-        if not self.cfg.fused:
-            return
-        items = [(n, p) for n in names for p in range(self.cfg.grads[n][0])]
-        stages = [self.two, self.three, self.four, self.five, self.six, self.seven]
-        waves = []
-        for wave in range(len(items) + lag * (len(stages) - 1)):
-            steps = [functools.partial(stages[k], *items[wave - lag * k])
-                     for k in reversed(range(len(stages))) if 0 <= wave - lag * k < len(items)]
-            waves.append(steps)
-        old, merged = self.waves, []
-        for i in range(max(len(old), len(waves))):
-            merged.append((old[i] if i < len(old) else []) + (waves[i] if i < len(waves) else []))
-        self.waves = merged
-
-    def run(self, n):
-        for wave in self.waves[:n]:
-            for step in wave:
-                step()
-        del self.waves[:n]
+        for name in names:
+            for p in range(self.cfg.grads[name][0]):
+                self.step(1, name, p)
+
+    def run(self, place):
+        for k, name, pieces in SCHEDULE[place]:
+            for p in pieces:
+                self.step(k, name, p)
+
+    def finish(self, names, others, gap):
+        order, last = [], []
+        for name in names:
+            n = len(self.stages(name))
+            for p in range(self.cfg.grads[name][0]):
+                ahead = 1 + sum((k, name, p) in self.done for k in range(1, n + 1))
+                for k in range(ahead, n):
+                    order.append((p + k - ahead, -k, len(order), (k, name, p)))
+                last.append((n, name, p))
+        others = list(others)
+        for i, step in enumerate(sorted(order)):
+            if others and i % gap == gap - 1:
+                others.pop(0)()
+            self.step(*step[3])
+        for other in others:
+            other()
+        for step in last:
+            if step not in self.done:
+                self.step(*step)
 
     def ref(self, kind, name):
         return getattr(self.m, kind + name)
 
-    def go(self, kind, name, p, src, dst, dev, pred=None):
-        self.send(src, dst, self.ref("s_" + kind, name).at[p], self.ref("r_" + kind, name).at[p], dev, pred)
-
-    def got(self, kind, name, p, dst, pred=None):
-        self.arrive(dst, self.ref("r_" + kind, name).at[p], pred)
+    def go(self, kind, name, p, src, dst, dev):
+        self.send(src, dst, self.ref("s_" + kind, name).at[p], self.ref("r_" + kind, name).at[p], dev)
+
+    def got(self, kind, name, p, dst):
+        self.arrive(dst, self.ref("r_" + kind, name).at[p])
 
     def piece(self, name, k):
         return jnp.bitwise_xor(self.w, k) if self.cfg.grads[name][3] else k
 
     def one(self, name, k):
         p = self.piece(name, k)
-        self.go("g1", name, k, self.ref("G", name).at[p, 1 - self.x], self.ref("X", name).at[k], self.partners[0])
+        self.go("g1", name, k, self.ref("G", name).at[p, 1 - self.x], self.ref("X", name).at[k, pl.ds(0, 2)],
+                self.partners[0])
 
     def two(self, name, k):
         g, other, t = self.ref("G", name), self.ref("X", name), self.ref("T", name)
-        self.got("g1", name, k, other.at[k])
+        self.got("g1", name, k, other.at[k, pl.ds(0, 2)])
         far = 1 - self.near
         mine = g[self.piece(name, k), self.x, far].astype(F32)
         t[k] = (mine + other[k, far].astype(F32)).astype(BF)
@@ -181,10 +216,14 @@
         done[k] = total
         self.go("g4", name, k, done.at[k], fin.at[self.w, self.x, self.near], (self.c, jnp.bitwise_xor(self.w, k)))
 
-    def five(self, name, k):
+    def owned(self, name, k):
         here = self.ref("F", name).at[self.piece(name, k), self.x, self.near]
         if self.cfg.grads[name][3] and k > 0:
             self.got("g4", name, k, here)
+        return here
+
+    def five(self, name, k):
+        here = self.owned(name, k)
         self.go("g5", name, k, here, here, self.partners[1])
 
     def six(self, name, k):
@@ -195,9 +234,38 @@
     def seven(self, name, k):
         self.got("g6", name, k, self.ref("F", name).at[self.piece(name, k), 1 - self.x])
 
+    def three_others(self):
+        x, n = self.x, self.near
+        return ((1 - x, n, self.partners[0]), (x, 1 - n, self.partners[1]), (1 - x, 1 - n, self.partners[3]))
+
+    def quarters(self, name, k):
+        p = self.piece(name, k)
+        for i, (x, n, dev) in enumerate(self.three_others()):
+            self.go("g1", name, 3 * k + i, self.ref("G", name).at[p, x, n], self.ref("X", name).at[k, i], dev)
+
+    def quarters_sum(self, name, k):
+        total = self.ref("G", name)[self.piece(name, k), self.x, self.near].astype(F32)
+        for i in range(3):
+            other = self.ref("X", name).at[k, i]
+            self.got("g1", name, 3 * k + i, other)
+            total = total + other[...].astype(F32)
+        u = self.ref("U", name)
+        u[k] = total.astype(BF)
+        self.go("g3", name, k, u.at[k], self.ref("Z", name).at[k], self.partners[2])
+
+    def spread(self, name, k):
+        here = self.owned(name, k)
+        for i, (_, _, dev) in enumerate(self.three_others()):
+            self.go("g5", name, 3 * k + i, here, here, dev)
+
+    def spread_end(self, name, k):
+        p = self.piece(name, k)
+        for i, (x, n, _) in enumerate(self.three_others()):
+            self.got("g5", name, 3 * k + i, self.ref("F", name).at[p, x, n])
+
 
 def layer_kernel(cfg, names, n_in, *refs):
-    (x_ref, cot_ref, qkv_ref, vec_ref, out_ref, up_ref, down_ref) = refs[:n_in]
+    (x_ref, cot_ref, qkv_ref, out_ref, up_ref, down_ref, len_ref, *vec_refs) = refs[:n_in]
     y_ref, gx_ref, gqkv_ref, gout_ref, gup_ref, gdown_ref, gvec_ref = refs[n_in : n_in + 7]
     m = SimpleNamespace(**dict(zip(names, refs[n_in + 7 :])))
     if cfg.fused:
@@ -262,7 +330,7 @@
 
     lax.fori_loop(0, C * W, greet, 0)
 
-    def return_barrier():
+    def entered():
         pl.semaphore_wait(barrier, C * W - 1)
 
     def peer(k):
@@ -295,12 +363,36 @@
         stage[t2] = (mine2 + recv[1].astype(F32)).astype(BF)
         send(stage.at[t2], recv.at[2], ss.at[2], rs.at[2], peer(2))
         own = part(w)
+        arrive(recv.at[0], rs.at[0])
+        own = own + recv[0].astype(F32)
         if late:
             late()
-        arrive(recv.at[0], rs.at[0])
-        own = own + recv[0].astype(F32)
         arrive(recv.at[2], rs.at[2])
         return own + recv[2].astype(F32)
+
+    def scatter_steps(part, stage, recv, ss, rs):
+        t3, t2, t1 = (jnp.bitwise_xor(w, k) for k in (3, 2, 1))
+
+        def first():
+            stage[t3] = part(t3).astype(BF)
+            send(stage.at[t3], recv.at[1], ss.at[1], rs.at[1], peer(1))
+            stage[t1] = part(t1).astype(BF)
+            send(stage.at[t1], recv.at[0], ss.at[0], rs.at[0], peer(1))
+
+        def second():
+            mine2 = part(t2)
+            arrive(recv.at[1], rs.at[1])
+            stage[t2] = (mine2 + recv[1].astype(F32)).astype(BF)
+            send(stage.at[t2], recv.at[2], ss.at[2], rs.at[2], peer(2))
+
+        def third():
+            own = part(w)
+            arrive(recv.at[0], rs.at[0])
+            own = own + recv[0].astype(F32)
+            arrive(recv.at[2], rs.at[2])
+            return own + recv[2].astype(F32)
+
+        return first, second, third
 
     def local(src, dst, sem):
         cp = pltpu.make_async_copy(src, dst, sem)
@@ -309,13 +401,12 @@
 
     rows_w = pl.ds(w * DW, DW)
     own = [
-        local(qkv_ref, m.Wq, m.s_own.at[1]),
-        local(x_ref, m.Xall.at[w], m.s_own.at[0]),
-        local(vec_ref, m.Vv.at[w], m.s_own.at[2]),
-        local(out_ref, m.Outp.at[w, pl.ds(OFF, DW)], m.s_own.at[3]),
-        local(up_ref.at[:, pl.ds(pl.multiple_of(w * cfg.FW, cfg.FW), cfg.FW)], m.Upc.at[rows_w], m.s_own.at[4]),
-        local(down_ref, m.Dn, m.s_own.at[5]),
-        local(cot_ref, m.Cot, m.s_own.at[6]),
+        local(qkv_ref, m.Wq, m.s_own.at[0]),
+        local(x_ref, m.Xall.at[w], m.s_own.at[1]),
+        local(out_ref, m.Outp.at[w, pl.ds(OFF, DW)], m.s_own.at[2]),
+        local(up_ref.at[:, pl.ds(pl.multiple_of(w * cfg.FW, cfg.FW), cfg.FW)], m.Upc.at[rows_w], m.s_own.at[3]),
+        local(down_ref, m.Dn, m.s_own.at[4]),
+        local(cot_ref, m.Cot, m.s_own.at[5]),
     ]
     own[0].wait()
     for g in range(W):
@@ -323,54 +414,85 @@
             a = third * D + g * DW
             m.Ws[g, :, i * DW : (i + 1) * DW] = m.Wq[:, a : a + DW]
         m.Ws[g, :, 3 * DW : MW] = jnp.zeros((DW, MW - 3 * DW), BF)
+    row = 0
+    for ref in vec_refs:
+        v = ref[...].astype(F32)
+        for i in range(v.shape[0] // DW):
+            m.Vv[w, row : row + 1, :] = v[i * DW : (i + 1) * DW].reshape(1, DW)
+            row += 1
+    m.Vv[w, row:VROWS, :] = jnp.full((VROWS - row, DW), len_ref[0].astype(F32))
     own[1].wait()
-    own[2].wait()
-    return_barrier()
+    entered()
+
+    def part_rows(t, part, parts):
+        return pl.ds(pl.multiple_of(t * DW + part * (DW // parts), 16), DW // parts)
+
+    quarter = lax.rem(c, 4)
+
+    def near_me(k):
+        return (jnp.bitwise_xor(c, k), w)
+
+    for k in (2, 3):
+        send(m.Ws.at[jnp.bitwise_xor(w, k), part_rows(0, quarter, 4)], m.Wc.at[part_rows(w, quarter, 4)],
+             m.s_wq.at[k], m.r_wq.at[k], peer(k))
+    gather_start(m.Xall, m.s_x, m.r_x)
+    send(m.Ws.at[jnp.bitwise_xor(w, 1)], m.Wc.at[rows_w], m.s_wq.at[1], m.r_wq.at[1], peer(1))
     for k in (2, 3, 1):
-        t = jnp.bitwise_xor(w, k)
-        send(m.Ws.at[t], m.Wc.at[rows_w], m.s_wq.at[k], m.r_wq.at[k], peer(k))
         send(m.Vv.at[w], m.Vv.at[w], m.s_vv.at[k], m.r_vv.at[k], peer(k))
-    gather_start(m.Xall, m.s_x, m.r_x)
     m.Wc[rows_w, :] = m.Ws[w]
     for t in range(W):
         m.Outp[t, 0:OFF, :] = jnp.zeros((OFF, D), BF)
     m.bias[...] = jnp.zeros(m.bias.shape, F32)
-    for cp in own[3:]:
+    for cp in own[2:]:
         cp.wait()
+    for k in (2, 3):
+        rows = m.Wc.at[part_rows(jnp.bitwise_xor(w, k), quarter, 4)]
+        arrive(rows, m.r_wq.at[k])
+        for i in (1, 2, 3):
+            e = 3 * (k - 2) + i - 1
+            send(rows, rows, m.s_wf.at[e], m.r_wf.at[e], near_me(i))
     for k in (1, 2, 3):
-        t = jnp.bitwise_xor(w, k)
-        arrive(m.Wc.at[pl.ds(t * DW, DW)], m.r_wq.at[k])
-        arrive(m.Vv.at[t], m.r_vv.at[k])
         gather_wait(m.Xall, m.s_x, m.r_x, k)
+    arrive(m.Wc.at[pl.ds(jnp.bitwise_xor(w, 1) * DW, DW)], m.r_wq.at[1])
+    for k in (1, 2, 3):
+        arrive(m.Vv.at[jnp.bitwise_xor(w, k)], m.r_vv.at[k])
     for k in (2, 3, 1):
-        t = jnp.bitwise_xor(w, k)
         send(out_ref, m.Outp.at[w, pl.ds(OFF, DW)], m.s_ow.at[k], m.r_ow.at[k], peer(k))
     for k in (2, 3, 1):
-        t = jnp.bitwise_xor(w, k)
-        send(up_ref.at[:, pl.ds(pl.multiple_of(t * cfg.FW, cfg.FW), cfg.FW)], m.Upc.at[rows_w],
-             m.s_uw.at[k], m.r_uw.at[k], peer(k))
+        cols = pl.ds(pl.multiple_of(jnp.bitwise_xor(w, k) * cfg.FW, cfg.FW), cfg.FW)
+        send(up_ref.at[:, cols], m.Upc.at[rows_w], m.s_uw.at[k], m.r_uw.at[k], peer(k))
+    for k in (2, 3):
+        for i in (1, 2, 3):
+            e = 3 * (k - 2) + i - 1
+            arrive(m.Wc.at[part_rows(jnp.bitwise_xor(w, k), jnp.bitwise_xor(quarter, i), 4)], m.r_wf.at[e])
 
     for t in range(W):
         m.Vs[0:6, t * DW : (t + 1) * DW] = m.Vv[t, 0:6, :]
         m.upb[0:1, t * DW : (t + 1) * DW] = m.Vv[w, UPB + t : UPB + t + 1, :]
-    half, odd = lax.div(w, 2), lax.rem(w, 2)
-    m.bias[0:1, DW : 2 * DW] = m.Vv[W // 2 + half, pl.ds(QVB + odd, 1), :]
-    m.bias[0:1, 2 * DW : 3 * DW] = m.Vv[half, pl.ds(QVB + odd, 1), :]
+    upper, odd = lax.div(w, 2), lax.rem(w, 2)
+    m.bias[0:1, DW : 2 * DW] = m.Vv[W // 2 + upper, pl.ds(QVB + odd, 1), :]
+    m.bias[0:1, 2 * DW : 3 * DW] = m.Vv[upper, pl.ds(QVB + odd, 1), :]
     bias = m.bias[0:1, :]
 
     def vec(row):
         return m.Vs[row : row + 1, :]
 
-    for k in range(W):
-        t = lax.rem(s + 1 + k, W)
+    kv_rows = pl.ds(pl.multiple_of(block_part * Q + block_slot * B, B), B)
+    order = [lax.rem(s + 1 + k, W) for k in range(W)]
+    for k, t in enumerate(order):
         m.QKVs[t] = (dot(m.Xall[t], m.Wc[...]) + bias).astype(BF)
         dev = att_device(t, w, block_part)
-        send(m.QKVs.at[t], m.Rq.at[block_slot], m.s_q.at[k], m.r_q.at[block_slot], dev,
+        send(m.QKVs.at[t, :, pl.ds(KVW, DP)], m.Rq.at[block_slot], m.s_q.at[k], m.r_q.at[block_slot], dev,
+             jnp.logical_not(is_me(dev)))
+    for k, t in enumerate(order):
+        dev = att_device(t, w, block_part)
+        send(m.QKVs.at[t, :, pl.ds(0, KVW)], m.KV.at[kv_rows], m.s_kv.at[k], m.r_kv.at[block_slot], dev,
              jnp.logical_not(is_me(dev)))
 
         @pl.when(is_me(dev))
         def _():
-            m.Rq[block_slot] = m.QKVs[t]
+            m.Rq[block_slot] = m.QKVs[t, :, KVW:MW]
+            m.KV[kv_rows, :] = m.QKVs[t, :, 0:KVW]
 
     lanes = lax.broadcasted_iota(jnp.int32, (1, DP), 1)
 
@@ -381,21 +503,10 @@
         return jnp.logical_and(lanes >= OFF + h * HEAD, lanes < OFF + (h + 1) * HEAD)
 
     for j in range(W):
-        src = (j * R + r_att, g_att)
-        arrive(m.Rq.at[j], m.r_q.at[j], jnp.logical_not(is_me(src)))
-        kv_rows = pl.ds(pl.multiple_of(r_att * Q + j * B, B), B)
-        for k in range(1, R):
-            dev = att_device(s, g_att, lax.rem(r_att + k, R))
-            send(m.Rq.at[j, :, pl.ds(0, KVW)], m.KV.at[kv_rows], m.s_kv.at[(k - 1) * W + j],
-                 m.r_kv.at[r_att * W + j], dev)
-        m.KV[kv_rows, :] = m.Rq[j, :, 0:KVW]
-        q = m.Rq[j, :, KVW:MW] * jnp.asarray(HEAD**-0.5, BF)
+        arrive(m.Rq.at[j], m.r_q.at[j], jnp.logical_not(is_me((j * R + r_att, g_att))))
+        q = m.Rq[j] * jnp.asarray(HEAD**-0.5, BF)
         for h in range(HW):
             m.Qm[h, j * B : (j + 1) * B, :] = jnp.where(q_lane(h), q, jnp.zeros_like(q))
-    for k in range(1, R):
-        r = lax.rem(r_att + k, R)
-        for j in range(W):
-            arrive(m.KV.at[pl.ds(pl.multiple_of(r * Q + j * B, B), B)], m.r_kv.at[r * W + j])
 
     KC = 2 * B
     PER_SET = Q // KC
@@ -429,7 +540,25 @@
             m.OT[a:b, :] = m.OT[a:b, :] * factor + dot(values_t[a:b, :], prob.astype(BF))
         return carry
 
-    lax.fori_loop(0, R * PER_SET, attend, 0)
+    for i in range(PER_SET):
+        pair = jnp.bitwise_xor(lax.div(s, 2), i)
+        for e in range(2):
+            j = 2 * pair + e
+            rows = m.KV.at[pl.ds(pl.multiple_of(r_att * Q + j * B, B), B)]
+            arrive(rows, m.r_kv.at[j], jnp.logical_not(is_me((j * R + r_att, g_att))))
+            for k in range(1, R):
+                send(rows, rows, m.s_kf.at[(k - 1) * W + 2 * i + e], m.r_kf.at[r_att * W + j],
+                     att_device(s, g_att, lax.rem(r_att + k, R)))
+        attend(r_att * PER_SET + pair, 0)
+
+        def others(k, carry):
+            r = lax.rem(r_att + k, R)
+            for e in range(2):
+                j = 2 * pair + e
+                arrive(m.KV.at[pl.ds(pl.multiple_of(r * Q + j * B, B), B)], m.r_kf.at[r * W + j])
+            return attend(r * PER_SET + pair, carry)
+
+        lax.fori_loop(1, R, others, 0)
     for h in range(HW):
         a, b = OFF + h * HEAD, OFF + (h + 1) * HEAD
         m.OT[a:b, :] = m.OT[a:b, :] / m.lrow[h : h + 1, :]
@@ -509,7 +638,7 @@
             else:
                 plain[i * rows : (i + 1) * rows, :] = val
 
-    pump = make_sums(cfg, m, c, w, send, arrive)
+    pump = Sums(cfg, m, c, w, send, arrive)
 
     def early():
         put_grad("down", gdown_ref, m.Gs, m.dFall, 2)
@@ -518,8 +647,7 @@
     def late():
         put_grad("up", gup_ref, m.N1all, m.dHs, 2)
         m.gv[6:7, :] = col_sum(flat(m.dHs).astype(F32))
-        pump.add(("down", "up"), 2)
-        pump.run(cfg.pump[0])
+        pump.run("norm")
 
     d_n1 = scatter_sum(
         lambda t: dot_nt(m.dHs[t], m.Upc[...]), m.dNs, m.dNr, m.s_dn, m.r_dn, early, late) + m.dR2[...]
@@ -547,8 +675,8 @@
     m.gv[1:2, :] = col_sum(d_n1)
     m.gv[4:5, :] = col_sum(d_a.astype(F32))
 
-    pump.run(cfg.pump[1])
     for j in range(W):
+        pump.run("sent%d" % j)
         arrive(m.dOr.at[j], m.r_do.at[j], jnp.logical_not(is_me((j * R + r_att, s))))
         d_o = m.dOr[j]
         cols = slice(j * B, (j + 1) * B)
@@ -558,6 +686,7 @@
         for h in range(HW):
             m.drow[h : h + 1, cols] = col_sum(prod[OFF + h * HEAD : OFF + (h + 1) * HEAD, :])
     m.dQT[...] = jnp.zeros(m.dQT.shape, F32)
+    pump.run("arrived")
 
     def attend_back(step, carry):
         chunk = lax.rem((r_att + 1) * PER_SET + step, R * PER_SET)
@@ -591,9 +720,10 @@
     for k in range(1, R):
         send(m.dKVs.at[k - 1], m.dKVr.at[R - k - 1], m.s_dkv.at[k - 1], m.r_dkv.at[R - k - 1],
              att_device(s, g_att, lax.rem(r_att + k, R)))
-    pump.run(cfg.pump[2])
+    pump.run("between")
     lax.fori_loop((R - 1) * PER_SET, R * PER_SET, attend_back, None)
-    pump.run(cfg.pump[3])
+    pump.run("after")
+    pump.run("part")
     for k in range(1, R):
         arrive(m.dKVr.at[k - 1], m.r_dkv.at[k - 1])
     for j in range(W):
@@ -611,39 +741,41 @@
             m.dqr[s] = m.dqs[j]
 
     for k in (1, 2, 3):
+        pump.run("dq%d" % k)
         gather_wait(m.dAall, m.s_da, m.r_da, k)
         arrive(m.MixT.at[jnp.bitwise_xor(w, k)], m.r_mt.at[k])
     put_grad("out", gout_ref, m.MixT, m.dAall, 1, OFF)
     pump.start(("out",))
-    pump.run(cfg.pump[4])
+    pump.run("out")
 
     for t in range(W):
+        pump.run("wait%d" % t)
         arrive(m.dqr.at[t], m.r_dq.at[t], jnp.logical_not(is_me(att_device(t, w, block_part))))
 
-    def early():
-        put_grad("qkv", gqkv_ref, m.Xall, m.dqr, 2)
-        pump.start(("qkv",))
-
-    def late():
-        m.gv[7:8, 0:MW] = col_sum(flat(m.dqr).astype(F32))
-        m.gv[7:8, MW:D] = jnp.zeros((1, D - MW), F32)
-        pump.add(("out", "qkv"), 1)
-        pump.run(cfg.pump[5])
-
-    d_x = scatter_sum(
-        lambda t: dot_nt(m.dqr[t], m.Wc[...]), m.dxs, m.dxr, m.s_dx, m.r_dx, early, late)
-    gx_ref[...] = (m.dR1[...] + d_x).astype(BF)
-
-    if not cfg.fused:
-        gvec_ref[0] = m.gv[...]
-    else:
-        total = m.gv[...]
-        for i, dev in enumerate(pump.partners):
-            m.Va[i] = total
-            send(m.Va.at[i], m.Vb.at[i], m.s_v1.at[i], m.r_v1.at[i], dev)
-            pump.run(cfg.pump[6])
-            arrive(m.Vb.at[i], m.r_v1.at[i])
-            total = total + m.Vb[i]
+    put_grad("qkv", gqkv_ref, m.Xall, m.dqr, 2)
+    pump.start(("qkv",))
+    pump.run("qkv")
+
+    m.gv[7:8, 0:MW] = col_sum(flat(m.dqr).astype(F32))
+    m.gv[7:8, MW:D] = jnp.zeros((1, D - MW), F32)
+
+    def d_x(t):
+        return dot_nt(m.dqr[t], m.Wc[...])
+
+    token_steps = scatter_steps(d_x, m.dxs, m.dxr, m.s_dx, m.r_dx)
+
+    def vectors(i):
+        if i:
+            arrive(m.Vb.at[i - 1], m.r_v1.at[i - 1])
+            m.Va[i] = m.Va[i - 1] + m.Vb[i - 1]
+        else:
+            m.Va[0] = m.gv[...]
+        if i < 3:
+            send(m.Va.at[i], m.Vb.at[i], m.s_v1.at[i], m.r_v1.at[i], pump.partners[i])
+
+    def vectors_to_rows():
+        vectors(3)
+        total = m.Va[3]
         for t in range(W):
             m.Vt[t, 0:6, :] = total[0:6, t * DW : (t + 1) * DW]
             m.Vt[t, 6:7, :] = total[7:8, 2 * DW : 3 * DW]
@@ -651,15 +783,27 @@
         m.Vw[w] = m.Vt[w]
         for k in (2, 3, 1):
             send(m.Vt.at[jnp.bitwise_xor(w, k)], m.Vw.at[w], m.s_vw.at[k], m.r_vw.at[k], peer(k))
-        m.gv[6:7, :] = total[6:7, :]
-        pump.run(cfg.pump[6])
+        gvec_ref[7:8, :] = total[6:7, :]
+
+    def vectors_end():
         for k in (1, 2, 3):
             arrive(m.Vw.at[jnp.bitwise_xor(w, k)], m.r_vw.at[k])
         gvec_ref[0:6, 0:DW] = m.Vw[0, 0:6, :] + m.Vw[1, 0:6, :] + m.Vw[2, 0:6, :] + m.Vw[3, 0:6, :]
         for i in range(2):
-            gvec_ref[6:7, i * DW : (i + 1) * DW] = m.Vw[2 * odd + i, pl.ds(6 + half, 1), :]
-        gvec_ref[7:8, :] = m.gv[6:7, :]
-        pump.run(1000)
+            gvec_ref[6:7, i * DW : (i + 1) * DW] = m.Vw[2 * odd + i, pl.ds(6 + upper, 1), :]
+
+    steps = [functools.partial(vectors, i) for i in range(3)] + [vectors_to_rows, vectors_end]
+
+    if not cfg.fused:
+        for step in token_steps[:-1]:
+            step()
+        d_x_sum = token_steps[-1]()
+        gvec_ref[0] = m.gv[...]
+    else:
+        vector_steps = [functools.partial(vectors, i) for i in range(3)] + [vectors_to_rows, vectors_end]
+        pump.finish(("qkv", "out", "up", "down"), [token_steps[0], vector_steps[0], token_steps[1]] + vector_steps[1:], 3)
+        d_x_sum = token_steps[2]()
+    gx_ref[...] = (m.dR1[...] + d_x_sum).astype(BF)
 
     for pred, end in drains:
         if pred is None:
@@ -681,32 +825,28 @@
     cfg.fused = R == 2 and C == 8 and DW % 64 == 0 and FW % (64 * W) == 0
     cfg.grads = dict(down=(W, FW // W // 4, D, False), up=(W, DW // 4, FW, True), qkv=(W, DW // 4, MW, True),
                      out=(1, DW // 4, D, False))
-    cfg.pump = (2, 2, 1, 1, 2, 2, 1)
     w = lax.axis_index("wa")
-    small = [v.astype(F32) for v in (out_bias, down_bias, gain_one, shift_one, gain_two, shift_two, qv_bias, up_bias)]
-    small.append(jnp.broadcast_to(lengths.astype(F32), ((VROWS - LEN) * DW,)))
-    vec = jnp.concatenate(small).reshape(VROWS, DW)
+    small = (out_bias, down_bias, gain_one, shift_one, gain_two, shift_two, qv_bias, up_bias)
 
     plan = make_plan(cfg)
     names = list(plan)
     vm = pl.BlockSpec(memory_space=pltpu.VMEM)
     hbm = pl.BlockSpec(memory_space=pl.ANY)
-    shape = jax.ShapeDtypeStruct
     if cfg.fused:
-        outs = [shape((n, 2, 2, ch, cols), BF) for n, ch, cols, _ in (cfg.grads[k] for k in ("qkv", "out", "up", "down"))]
-        outs.append(shape((GROWS, D), F32))
+        outs = [(n, 2, 2, ch, cols) for n, ch, cols, _ in (cfg.grads[k] for k in ("qkv", "out", "up", "down"))]
+        place = pltpu.VMEM
     else:
-        outs = [shape((D, MW), BF), shape((DP, D), BF), shape((D, FW), BF), shape((FW, D), BF),
-                shape((1, GROWS, D), F32)]
-    outs = [shape((B, D), BF), shape((B, D), BF)] + outs
-    args = (tokens.reshape(B, D), cotangent.reshape(B, D), qkv_weight, vec, out_weight, up_weight, down_weight)
+        outs = [(D, MW), (DP, D), (D, FW), (FW, D)]
+        place = jax.ShapeDtypeStruct
+    outs = [place(a, BF) for a in [(B, D), (B, D)] + outs] + [place((GROWS, D) if cfg.fused else (1, GROWS, D), F32)]
+    args = (tokens.reshape(B, D), cotangent.reshape(B, D), qkv_weight, out_weight, up_weight, down_weight, lengths, *small)
     y, gx, gqkv, gout, gup, gdown, gvec = pl.pallas_call(
         functools.partial(layer_kernel, cfg, names, len(args)),
         out_shape=outs,
-        in_specs=[hbm] * len(args),
+        in_specs=[hbm] * 6 + [pl.BlockSpec(memory_space=pltpu.SMEM)] + [vm] * len(small),
         out_specs=[vm] * len(outs),
         scratch_shapes=[plan[n] for n in names],
-        compiler_params=pltpu.CompilerParams(collective_id=0, has_side_effects=True, vmem_limit_bytes=60 << 20),
+        compiler_params=pltpu.CompilerParams(collective_id=0, has_side_effects=True, vmem_limit_bytes=(52 if cfg.fused else 60) << 20),
         name="layer",
     )(*args)
     if cfg.fused:
@@ -751,11 +891,13 @@
     B, D, DW, W, FW = cfg.B, cfg.D, cfg.DW, cfg.W, cfg.FW
     shapes = [(1, B, D)] * 2 + [(DW, 3 * D), (DW, D), (DW, W * FW), (FW, D), (2 * DW,), (DW,), (FW,)] + [(DW,)] * 5
     vm = pl.BlockSpec(memory_space=pltpu.VMEM)
+    arrays = [pltpu.with_memory_space_constraint(a, pltpu.VMEM) for a in arrays]
     return pl.pallas_call(
         functools.partial(finish_kernel, cfg),
         out_shape=[jax.ShapeDtypeStruct(s, BF if i < 2 else F32) for i, s in enumerate(shapes)],
         in_specs=[vm] * len(arrays),
         out_specs=[vm] * len(shapes),
+        compiler_params=pltpu.CompilerParams(vmem_limit_bytes=32 << 20),
         name="results",
     )(*arrays)
 

time: 208 us -> 185 us (0.89)
  Pallas kernels: 201 us -> 183 us
  local copies, waits for them, and re-layouts: 6.14 us -> 0 us
    pallas_call x1, Pallas kernels: 195 us -> 180 us  [body(): pl.pallas_call(functools.partial(layer_kernel, cfg, names, len(args)), ou...]
    concatenate x1 -> x0, local copies, waits for them, and re-layouts: 5.46 us -> none  [body(): vec = jnp.concatenate(small).reshape(VROWS, DW)]
    pallas_call x1, Pallas kernels: 5.46 us -> 3.31 us  [finish(): pl.pallas_call(functools.partial(finish_kernel, cfg), out_shape=[jax.Shap...]
where the time goes in v3:
time: 185 us; the launch traced here: 184 us
  Pallas kernels  183 us (99%)
    pallas_call x1, Pallas kernels, body(): pl.pallas_call(functools.partial(layer_kernel, cfg, names, len(args)), ou...  180 us

profile of v3, /device:TPU:0, one launch (start us, length us, event | category | flops | bytes accessed | tf_op | source)
XLA Modules:
  0.0 184.4 jit_solution(8852937790500378718)
XLA Ops:
  1.3 179.6 %layer.1 = (bf16[128,768]{1,0:T(8,128)(2,1)S(1)}, bf16[128,768]{1,0:T(8,128)(2,1)S(1)}, bf16[4,2,2,48,640]{4,3,2,1,0:T(8,128)(2,1)S(1)}, bf16[1,2,2,48,768]{4,3,...) custom-call(bf16[128,768]{1,0:T(8,128)(2,1)} %bitcast.2, ...), custom_call_target="tpu_custom_call" | custom-call | tf_op jit(solution)/shard_map/layer/pallas_call | solution.py:843
  180.9 3.3 %results.1 = (bf16[1,128,768]{2,1,0:T(8,128)(2,1)}, bf16[1,128,768]{2,1,0:T(8,128)(2,1)}, f32[192,2304]{1,0:T(8,128)}, f32[192,768]{1,0:T(8,128)}, f32[192,3072]...) custom-call(bf16[128,768]{1,0:T(8,128)(2,1)S(1)} %get-tuple-element., ...), custom_call_target="tpu_custom_call" | custom-call | tf_op jit(solution)/shard_map/results/pallas_call | solution.py:895

commit v4 on v3

--- a/solution.py
+++ b/solution.py
@@ -24,24 +24,64 @@
 
 ALL = (0, 1, 2, 3)
 SCHEDULE = dict(
-    norm=((2, "down", (0,)), ),
-    sent0=((3, "down", (0,)), (2, "down", (1,)), ),
-    sent1=(),
-    sent2=((2, "down", (2,)), ),
-    sent3=(),
-    arrived=((3, "down", (1,)), (2, "down", (3,)), (2, "up", (0,)), ),
-    between=((4, "down", (0,)), (3, "down", (2,)), (2, "up", (1,)), ),
-    after=((5, "down", (0,)), (4, "down", (1,)), (3, "down", (3,)), (3, "up", (0,)), (2, "up", (2,)), ),
+    early=(),
+    norm=(
+        (1, "up", 0), (1, "up", 1), (1, "up", 2), (1, "up", 3),
+    ),
+    sent=(),
+    down=(
+        (1, "down", 0), (1, "down", 1), (1, "down", 2), (1, "down", 3), (2, "down", 0), (2, "down", 1),
+        (2, "down", 2), (2, "down", 3),
+    ),
+    sent0=(
+        (3, "down", 0),
+    ),
+    sent1=(
+        (3, "down", 1),
+    ),
+    sent2=(
+        (3, "down", 2),
+    ),
+    sent3=(
+        (3, "down", 3),
+    ),
+    arrived=(
+        (2, "up", 0), (4, "down", 0), (5, "down", 0),
+    ),
+    between=(
+        (4, "down", 1), (5, "down", 1), (2, "up", 1),
+    ),
+    after=(
+        (4, "down", 2), (5, "down", 2), (3, "up", 0), (2, "up", 2),
+    ),
     part=(),
     dq1=(),
     dq2=(),
     dq3=(),
-    out=((5, "down", (1,)), (4, "down", (2,)), (3, "up", (1,)), (2, "up", (3,)), ),
-    wait0=((6, "down", (0,)), (5, "down", (2,)), (4, "down", (3,)), (4, "up", (0,)), (3, "up", (2,)), ),
-    wait1=((6, "down", (1,)), (5, "down", (3,)), (4, "up", (1,)), (3, "up", (3,)), ),
+    out=(
+        (1, "out", 0), (6, "down", 0), (3, "up", 1), (2, "up", 3),
+    ),
+    wait0=(
+        (4, "down", 3), (4, "up", 0), (3, "up", 2),
+    ),
+    wait1=(
+        (6, "down", 1), (5, "down", 3), (4, "up", 1), (3, "up", 3),
+    ),
     wait2=(),
-    wait3=((5, "up", (0,)), ),
-    qkv=((6, "down", (2,)), (6, "down", (3,)), (6, "up", (0,)), (4, "up", (2,)), (4, "up", (3,)), ),
+    wait3=(
+        (5, "up", 0),
+    ),
+    qkv=(
+        (1, "qkv", 0), (1, "qkv", 1), (1, "qkv", 2), (1, "qkv", 3), (6, "down", 2), (6, "down", 3),
+        (6, "up", 0), (4, "up", 2), (4, "up", 3), (2, "qkv", 0), (2, "out", 0),
+    ),
+    tail=(
+        (5, "up", 1), (3, "qkv", 0), (0, "tokens", 0), (3, "out", 0), (2, "qkv", 1), (6, "up", 1),
+        (0, "vectors", 0), (5, "up", 2), (4, "qkv", 0), (4, "out", 0), (1, "tokens", 0), (3, "qkv", 1),
+        (2, "qkv", 2), (6, "up", 2), (1, "vectors", 0), (5, "out", 0), (5, "up", 3), (4, "qkv", 1),
+        (2, "vectors", 0), (3, "qkv", 2), (2, "qkv", 3), (6, "out", 0), (3, "vectors", 0), (6, "up", 3),
+        (4, "qkv", 2), (3, "qkv", 3), (4, "vectors", 0), (4, "qkv", 3),
+    ),
 )
 
 
@@ -79,31 +119,38 @@
         cfg.C, cfg.W, cfg.B, cfg.D, cfg.FW, cfg.DW, cfg.DP, cfg.KVW, cfg.MW, cfg.R)
     V = pltpu.VMEM
     dma = pltpu.SemaphoreType.DMA
-    Q = W * B
+    Q, HB = W * B, B // 2
     plan = dict(
         Xall=V((W, B, D), BF), Wc=V((D, MW), BF), Wq=V((DW, 3 * D), BF), Ws=V((W, DW, MW), BF), Vv=V((W, VROWS, DW), F32),
-        Vs=V((8, D), F32), Outp=V((W, DP, D), BF), Upc=V((D, FW), BF), Dn=V((FW, D), BF), Cot=V((B, D), BF),
-        QKVs=V((W, B, MW), BF), Rq=V((W, B, DP), BF), KV=V((R * Q, KVW), BF),
+        Vs=V((8, D), F32), Out=V((W, DW, D), BF), Upc=V((D, FW), BF), Dn=V((FW, D), BF), UpT=V((FW, D), BF), DnT=V((D, FW), BF),
+        OutT=V((D, D), BF), WcT=V((MW, D), BF), Cot=V((B, D), BF),
+        KVs=V((W, B, KVW), BF), Qs=V((W, HB, KVW), BF), Rq=V((W, HB, KVW), BF), wide=V((B, DP), BF), KV=V((R * Q, KVW), BF),
         Qm=V((cfg.HW, Q, DP), BF), Dm=V((cfg.HW, Q, DP), BF),
-        mrow=V((8, Q), F32), lrow=V((8, Q), F32), bias=V((8, MW), F32), upb=V((8, cfg.FW), F32), drow=V((8, Q), F32), OT=V((DP, Q), F32), dQT=V((DP, Q), F32),
-        Osend=V((W, B, DP), BF), Mix=V((W, B, DP), BF), MixT=V((W, B, DP), BF),
+        mrow=V((8, Q), F32), lrow=V((8, Q), F32), bias=V((8, MW), F32), upb=V((8, cfg.FW), F32), drow=V((8, Q), F32), OT=V((DW, Q), F32), dQT=V((DW, Q), F32),
+        Os=V((W, HB, KVW), BF), Mix=V((W, HB, KVW), BF), MixT=V((W, HB, KVW), BF), mixed=V((B, D), BF),
+        Mt=V((W, B, DW), BF),
         N1f=V((B, D), F32), n1=V((B, D), F32), n2=V((B, D), F32), r1=V((B, 1), F32),
         N1all=V((W, B, D), BF), Hp=V((W, B, FW), F32), Gs=V((W, B, FW), BF),
         Fs=V((W, B, D), BF), Fr=V((3, B, D), BF), dR2=V((B, D), F32), dFall=V((W, B, D), BF),
         dHs=V((W, B, FW), BF), dNs=V((W, B, D), BF), dNr=V((3, B, D), BF), dR1=V((B, D), F32),
-        dAall=V((W, B, D), BF), dOs=V((W, B, DP), BF), dOr=V((W, B, DP), BF),
+        dAall=V((W, B, D), BF), dOs=V((W, HB, KVW), BF), dOr=V((W, HB, KVW), BF),
         dKVf=V((Q, KVW), F32), dKVs=V((R - 1, Q, KVW), BF), dKVr=V((R - 1, Q, KVW), BF),
-        dqs=V((W, B, MW), BF), dqr=V((W, B, MW), BF), dxs=V((W, B, D), BF), dxr=V((3, B, D), BF),
+        dKVo=V((W, B, KVW), BF), dQs=V((W, HB, KVW), BF), dQr=V((W, HB, KVW), BF), dqr=V((W, B, MW), BF), dxs=V((W, B, D), BF), dxr=V((3, B, D), BF),
         gv=V((GROWS, D), F32),
     )
     sems = dict(
         x=4, wq=4, wf=12, vv=4, ow=4, uw=4, own=6,
-        q=W, kv=W, kf=(R - 1) * W, o=W, mt=4, n=4, f=4, df=4, dn=4, da=4, do=W, dkv=R - 1, dq=W, dx=4,
+        q=W, kv=W, kf=(R - 1) * W, o=W, mt=4, n=8, f=6, df=8, dn=6, da=4, do=W, dkv=R - 1, dq=W, dk=W, dx=4,
     )
     recvs = dict(sems, kf=R * W)
+    if cfg.keep:
+        plan["Pm"] = V((cfg.HW, R * Q, Q), F32)
     if cfg.fused:
+        plan.update(GX=V((W, B, FW), BF), DX=V((W, B, D // 2), BF))
+        sems.update(gx=6, fx=4)
+        recvs.update(gx=6, fx=4)
         for name, (pieces, ch, cols, to_rows) in cfg.grads.items():
-            plan["G" + name] = V((pieces, 2, 2, ch, cols), BF)
+            plan["G" + name] = V((pieces, 2, ch, cols) if name == "down" else (pieces, 2, 2, ch, cols), BF)
             plan["X" + name] = V((pieces, 3, ch, cols), BF)
             plan["T" + name] = V((pieces, ch, cols), BF)
             plan["Y" + name] = V((pieces, ch, cols), BF)
@@ -130,47 +177,32 @@
         self.cfg, self.m, self.c, self.w, self.send, self.arrive = cfg, m, c, w, send, arrive
         self.x, self.near = lax.rem(c, 2), lax.rem(lax.div(c, 2), 2)
         self.partners = [(jnp.bitwise_xor(c, k), w) for k in (1, 2, 4, 3)]
-        self.done = set()
         self.long = (self.one, self.two, self.three, self.four, self.five, self.six, self.seven)
+        self.halved = (self.nothing, self.pass_on, self.join) + self.long[3:]
         self.short = (self.quarters, self.quarters_sum, self.four, self.spread, self.spread_end)
 
     def stages(self, name):
+        if name == "down":
+            return self.halved
         return self.long if name in ("up", "down", "out") else self.short
 
     def step(self, k, name, p):
         if self.cfg.fused:
             self.stages(name)[k - 1](name, p)
-            self.done.add((k, name, p))
-
-    def start(self, names):
-        for name in names:
+
+    def run(self, place, others=None):
+        if not self.cfg.fused:
+            return
+        for k, name, p in SCHEDULE[place]:
+            if name in self.cfg.grads:
+                self.step(k, name, p)
+            else:
+                others[name][k]()
+
+    def finish(self):
+        for name in ("down", "up", "out", "qkv"):
             for p in range(self.cfg.grads[name][0]):
-                self.step(1, name, p)
-
-    def run(self, place):
-        for k, name, pieces in SCHEDULE[place]:
-            for p in pieces:
-                self.step(k, name, p)
-
-    def finish(self, names, others, gap):
-        order, last = [], []
-        for name in names:
-            n = len(self.stages(name))
-            for p in range(self.cfg.grads[name][0]):
-                ahead = 1 + sum((k, name, p) in self.done for k in range(1, n + 1))
-                for k in range(ahead, n):
-                    order.append((p + k - ahead, -k, len(order), (k, name, p)))
-                last.append((n, name, p))
-        others = list(others)
-        for i, step in enumerate(sorted(order)):
-            if others and i % gap == gap - 1:
-                others.pop(0)()
-            self.step(*step[3])
-        for other in others:
-            other()
-        for step in last:
-            if step not in self.done:
-                self.step(*step)
+                self.step(len(self.stages(name)), name, p)
 
     def ref(self, kind, name):
         return getattr(self.m, kind + name)
@@ -183,6 +215,19 @@
 
     def piece(self, name, k):
         return jnp.bitwise_xor(self.w, k) if self.cfg.grads[name][3] else k
+
+    def nothing(self, name, k):
+        pass
+
+    def pass_on(self, name, k):
+        g = self.ref("G", name).at[k, 1 - self.near]
+        self.go("g2", name, k, g, self.ref("Y", name).at[k], self.partners[1])
+
+    def join(self, name, k):
+        y, u = self.ref("Y", name), self.ref("U", name)
+        self.got("g2", name, k, y.at[k])
+        u[k] = (self.ref("G", name)[k, self.near].astype(F32) + y[k].astype(F32)).astype(BF)
+        self.go("g3", name, k, u.at[k], self.ref("Z", name).at[k], self.partners[2])
 
     def one(self, name, k):
         p = self.piece(name, k)
@@ -273,7 +318,7 @@
     C, W, B, D, DW, DP, KVW, MW, R, HW = (
         cfg.C, cfg.W, cfg.B, cfg.D, cfg.DW, cfg.DP, cfg.KVW, cfg.MW, cfg.R, cfg.HW)
     OFF = DP - DW
-    Q = W * B
+    Q, HB = W * B, B // 2
     c = lax.axis_index("ctx")
     w = lax.axis_index("wa")
     block_part = lax.rem(c, R)
@@ -336,38 +381,73 @@
     def peer(k):
         return (c, jnp.bitwise_xor(w, k))
 
-    def gather_start(buf, ss, rs):
-        send(buf.at[w], buf.at[w], ss.at[2], rs.at[2], peer(2))
+    def gather_start(buf, ss, rs, parts=1):
+        n = buf.shape[1] // parts
+        for h in range(parts):
+            rows = buf.at[w, pl.ds(h * n, n)]
+            send(rows, rows, ss.at[2 * parts + h], rs.at[2 * parts + h], peer(2))
         send(buf.at[w], buf.at[w], ss.at[1], rs.at[1], peer(1))
 
-    def gather_wait(buf, ss, rs, k):
+    def gather_wait(buf, ss, rs, k, h=0, parts=1):
+        n = buf.shape[1] // parts
+        t = jnp.bitwise_xor(w, k)
         if k == 1:
-            arrive(buf.at[jnp.bitwise_xor(w, 1)], rs.at[1])
+            arrive(buf.at[t], rs.at[1])
+            return
+        rows = buf.at[t, pl.ds(h * n, n)]
+        arrive(rows, rs.at[k * parts + h])
         if k == 2:
-            t = jnp.bitwise_xor(w, 2)
-            arrive(buf.at[t], rs.at[2])
-            send(buf.at[t], buf.at[t], ss.at[3], rs.at[3], peer(1))
-        if k == 3:
-            arrive(buf.at[jnp.bitwise_xor(w, 3)], rs.at[3])
-
-    def scatter_sum(part, stage, recv, ss, rs, early=None, late=None):
+            send(rows, rows, ss.at[3 * parts + h], rs.at[3 * parts + h], peer(1))
+
+    def take(ref, blocks):
+        parts = [ref[t, rows, :] for t, rows in blocks]
+        return jnp.concatenate(parts, 0) if len(parts) > 1 else parts[0]
+
+    def put(ref, blocks, value):
+        n = value.shape[0] // len(blocks)
+        for i, (t, rows) in enumerate(blocks):
+            ref[t, rows, :] = value[i * n : (i + 1) * n].astype(ref.dtype)
+
+    def feed(buf, sems, work, part, stage, recv, sum_sems, idle, early=None, late=None):
+        (ss, rs), (ss2, rs2) = sems, sum_sems
         t3, t2, t1 = (jnp.bitwise_xor(w, k) for k in (3, 2, 1))
-        stage[t3] = part(t3).astype(BF)
-        send(stage.at[t3], recv.at[1], ss.at[1], rs.at[1], peer(1))
-        mine2 = part(t2)
-        stage[t1] = part(t1).astype(BF)
-        send(stage.at[t1], recv.at[0], ss.at[0], rs.at[0], peer(1))
+        every = pl.ds(0, B)
+        halves = [pl.ds(h * HB, HB) for h in range(2)]
+        mine = [None, None]
+
+        def across(h):
+            rows = halves[h]
+            arrive(recv.at[1, rows], rs2.at[2 + h])
+            stage[t2, rows, :] = (mine[h] + recv[1, rows, :].astype(F32)).astype(BF)
+            send(stage.at[t2, rows], recv.at[2, rows], ss2.at[4 + h], rs2.at[4 + h], peer(2))
+
+        gather_start(buf, ss, rs, 2)
+        work([(w, every)])
+        gather_wait(buf, ss, rs, 1, 0, 2)
+        work([(t1, every)])
+        idle()
+        for h, rows in enumerate(halves):
+            gather_wait(buf, ss, rs, 2, h, 2)
+            if h:
+                across(0)
+            gather_wait(buf, ss, rs, 3, h, 2)
+            work([(t3, rows), (t2, rows)])
+            both = part([(t3, rows), (t2, rows)])
+            stage[t3, rows, :] = both[0:HB].astype(BF)
+            send(stage.at[t3, rows], recv.at[1, rows], ss2.at[2 + h], rs2.at[2 + h], peer(1))
+            mine[h] = both[HB:]
+        stage[t1] = part([(t1, every)]).astype(BF)
+        send(stage.at[t1], recv.at[0], ss2.at[0], rs2.at[0], peer(1))
         if early:
             early()
-        arrive(recv.at[1], rs.at[1])
-        stage[t2] = (mine2 + recv[1].astype(F32)).astype(BF)
-        send(stage.at[t2], recv.at[2], ss.at[2], rs.at[2], peer(2))
-        own = part(w)
-        arrive(recv.at[0], rs.at[0])
+        across(1)
+        own = part([(w, every)])
+        arrive(recv.at[0], rs2.at[0])
         own = own + recv[0].astype(F32)
         if late:
             late()
-        arrive(recv.at[2], rs.at[2])
+        for h, rows in enumerate(halves):
+            arrive(recv.at[2, rows], rs2.at[4 + h])
         return own + recv[2].astype(F32)
 
     def scatter_steps(part, stage, recv, ss, rs):
@@ -394,6 +474,14 @@
 
         return first, second, third
 
+    def pack(ref, value):
+        ref[:, 0:DW] = value[0:HB].astype(BF)
+        ref[:, DW:KVW] = value[HB:B].astype(BF)
+
+    def unpack(ref, lane, packed):
+        ref[0:HB, lane : lane + DW] = packed[:, 0:DW]
+        ref[HB:B, lane : lane + DW] = packed[:, DW:KVW]
+
     def local(src, dst, sem):
         cp = pltpu.make_async_copy(src, dst, sem)
         cp.start()
@@ -403,7 +491,7 @@
     own = [
         local(qkv_ref, m.Wq, m.s_own.at[0]),
         local(x_ref, m.Xall.at[w], m.s_own.at[1]),
-        local(out_ref, m.Outp.at[w, pl.ds(OFF, DW)], m.s_own.at[2]),
+        local(out_ref, m.Out.at[w], m.s_own.at[2]),
         local(up_ref.at[:, pl.ds(pl.multiple_of(w * cfg.FW, cfg.FW), cfg.FW)], m.Upc.at[rows_w], m.s_own.at[3]),
         local(down_ref, m.Dn, m.s_own.at[4]),
         local(cot_ref, m.Cot, m.s_own.at[5]),
@@ -440,11 +528,11 @@
     for k in (2, 3, 1):
         send(m.Vv.at[w], m.Vv.at[w], m.s_vv.at[k], m.r_vv.at[k], peer(k))
     m.Wc[rows_w, :] = m.Ws[w]
-    for t in range(W):
-        m.Outp[t, 0:OFF, :] = jnp.zeros((OFF, D), BF)
+    m.wide[...] = jnp.zeros(m.wide.shape, BF)
     m.bias[...] = jnp.zeros(m.bias.shape, F32)
     for cp in own[2:]:
         cp.wait()
+    m.DnT[...] = m.Dn[...].T
     for k in (2, 3):
         rows = m.Wc.at[part_rows(jnp.bitwise_xor(w, k), quarter, 4)]
         arrive(rows, m.r_wq.at[k])
@@ -456,8 +544,7 @@
     arrive(m.Wc.at[pl.ds(jnp.bitwise_xor(w, 1) * DW, DW)], m.r_wq.at[1])
     for k in (1, 2, 3):
         arrive(m.Vv.at[jnp.bitwise_xor(w, k)], m.r_vv.at[k])
-    for k in (2, 3, 1):
-        send(out_ref, m.Outp.at[w, pl.ds(OFF, DW)], m.s_ow.at[k], m.r_ow.at[k], peer(k))
+    gather_start(m.Out, m.s_ow, m.r_ow)
     for k in (2, 3, 1):
         cols = pl.ds(pl.multiple_of(jnp.bitwise_xor(w, k) * cfg.FW, cfg.FW), cfg.FW)
         send(up_ref.at[:, cols], m.Upc.at[rows_w], m.s_uw.at[k], m.r_uw.at[k], peer(k))
@@ -480,19 +567,19 @@
     kv_rows = pl.ds(pl.multiple_of(block_part * Q + block_slot * B, B), B)
     order = [lax.rem(s + 1 + k, W) for k in range(W)]
     for k, t in enumerate(order):
-        m.QKVs[t] = (dot(m.Xall[t], m.Wc[...]) + bias).astype(BF)
+        qkv = dot(m.Xall[t], m.Wc[...]) + bias
+        m.KVs[t] = qkv[:, 0:KVW].astype(BF)
+        pack(m.Qs.at[t], qkv[:, KVW : KVW + DW])
         dev = att_device(t, w, block_part)
-        send(m.QKVs.at[t, :, pl.ds(KVW, DP)], m.Rq.at[block_slot], m.s_q.at[k], m.r_q.at[block_slot], dev,
-             jnp.logical_not(is_me(dev)))
+        send(m.Qs.at[t], m.Rq.at[block_slot], m.s_q.at[k], m.r_q.at[block_slot], dev, jnp.logical_not(is_me(dev)))
     for k, t in enumerate(order):
         dev = att_device(t, w, block_part)
-        send(m.QKVs.at[t, :, pl.ds(0, KVW)], m.KV.at[kv_rows], m.s_kv.at[k], m.r_kv.at[block_slot], dev,
-             jnp.logical_not(is_me(dev)))
+        send(m.KVs.at[t], m.KV.at[kv_rows], m.s_kv.at[k], m.r_kv.at[block_slot], dev, jnp.logical_not(is_me(dev)))
 
         @pl.when(is_me(dev))
         def _():
-            m.Rq[block_slot] = m.QKVs[t, :, KVW:MW]
-            m.KV[kv_rows, :] = m.QKVs[t, :, 0:KVW]
+            m.Rq[block_slot] = m.Qs[t]
+            m.KV[kv_rows, :] = m.KVs[t]
 
     lanes = lax.broadcasted_iota(jnp.int32, (1, DP), 1)
 
@@ -504,7 +591,8 @@
 
     for j in range(W):
         arrive(m.Rq.at[j], m.r_q.at[j], jnp.logical_not(is_me((j * R + r_att, g_att))))
-        q = m.Rq[j] * jnp.asarray(HEAD**-0.5, BF)
+        unpack(m.wide, 0, m.Rq.at[j])
+        q = m.wide[...] * jnp.asarray(HEAD**-0.5, BF)
         for h in range(HW):
             m.Qm[h, j * B : (j + 1) * B, :] = jnp.where(q_lane(h), q, jnp.zeros_like(q))
 
@@ -536,8 +624,8 @@
             factor = jnp.exp(top - new_top)
             m.mrow[h : h + 1, :] = new_top
             m.lrow[h : h + 1, :] = m.lrow[h : h + 1, :] * factor + col_sum(prob)
-            a, b = OFF + h * HEAD, OFF + (h + 1) * HEAD
-            m.OT[a:b, :] = m.OT[a:b, :] * factor + dot(values_t[a:b, :], prob.astype(BF))
+            a, b = h * HEAD, (h + 1) * HEAD
+            m.OT[a:b, :] = m.OT[a:b, :] * factor + dot(values_t[OFF + a : OFF + b, :], prob.astype(BF))
         return carry
 
     for i in range(PER_SET):
@@ -550,6 +638,8 @@
                 send(rows, rows, m.s_kf.at[(k - 1) * W + 2 * i + e], m.r_kf.at[r_att * W + j],
                      att_device(s, g_att, lax.rem(r_att + k, R)))
         attend(r_att * PER_SET + pair, 0)
+        if i == 0:
+            gather_wait(m.Out, m.s_ow, m.r_ow, 2)
 
         def others(k, carry):
             r = lax.rem(r_att + k, R)
@@ -560,48 +650,56 @@
 
         lax.fori_loop(1, R, others, 0)
     for h in range(HW):
-        a, b = OFF + h * HEAD, OFF + (h + 1) * HEAD
+        a, b = h * HEAD, (h + 1) * HEAD
         m.OT[a:b, :] = m.OT[a:b, :] / m.lrow[h : h + 1, :]
     m.lrow[0:HW, :] = m.mrow[0:HW, :] + jnp.log(m.lrow[0:HW, :])
     for j in range(W):
-        m.Osend[j] = m.OT[:, j * B : (j + 1) * B].T.astype(BF)
+        pack(m.Os.at[j], m.OT[:, j * B : (j + 1) * B].T)
         dev = (j * R + r_att, s)
-        send(m.Osend.at[j], m.Mix.at[g_att], m.s_o.at[j], m.r_o.at[g_att], dev, jnp.logical_not(is_me(dev)))
+        send(m.Os.at[j], m.Mix.at[g_att], m.s_o.at[j], m.r_o.at[g_att], dev, jnp.logical_not(is_me(dev)))
 
         @pl.when(is_me(dev))
         def _():
-            m.Mix[g_att] = m.Osend[j]
-
-    for k in (1, 2, 3):
-        arrive(m.Outp.at[jnp.bitwise_xor(w, k), pl.ds(OFF, DW)], m.r_ow.at[k])
+            m.Mix[g_att] = m.Os[j]
+
+    for k in (1, 3):
+        gather_wait(m.Out, m.s_ow, m.r_ow, k)
+    out_weight = m.Out[...].reshape(D, D)
     resid = m.Xall[w].astype(F32) + vec(OUTB)
     for g in range(W):
         arrive(m.Mix.at[g], m.r_o.at[g], jnp.logical_not(is_me(att_device(w, g, block_part))))
-        resid = resid + dot(m.Mix[g], m.Outp[g])
+        unpack(m.mixed, g * DW, m.Mix.at[g])
+    resid = resid + dot(m.mixed[...], out_weight)
     n1, r1 = norm_stats(resid)
     m.n1[...] = n1
     m.r1[...] = r1
     n1_full = n1 * vec(GAIN1) + vec(SHIFT1)
     m.N1f[...] = n1_full
     m.N1all[w] = n1_full.astype(BF)
-    gather_start(m.N1all, m.s_n, m.r_n)
 
     for k in (1, 2, 3):
         arrive(m.Upc.at[pl.ds(jnp.bitwise_xor(w, k) * DW, DW)], m.r_uw.at[k])
     up_bias = m.upb[0:1, :]
 
-    def expand(t):
-        h = dot(m.N1all[t], m.Upc[...]) + up_bias
+    activated = []
+
+    def expand(blocks):
+        h = dot(take(m.N1all, blocks), m.Upc[...]) + up_bias
         phi = 0.5 * (1.0 + lax.erf(h * (2.0**-0.5)))
-        m.Gs[t] = (h * phi).astype(BF)
-        m.Hp[t] = phi + h * ((2.0 * math.pi) ** -0.5) * jnp.exp(-0.5 * h * h)
-
-    expand(w)
-    for k in (1, 2, 3):
-        gather_wait(m.N1all, m.s_n, m.r_n, k)
-        expand(jnp.bitwise_xor(w, k))
-
-    ffn = scatter_sum(lambda t: dot(m.Gs[t], m.Dn[...]), m.Fs, m.Fr, m.s_f, m.r_f)
+        put(m.Gs, blocks, h * phi)
+        put(m.Hp, blocks, phi + h * ((2.0 * math.pi) ** -0.5) * jnp.exp(-0.5 * h * h))
+        if cfg.fused:
+            for t, rows in blocks:
+                i = len(activated)
+                activated.append((t, rows))
+                send(m.Gs.at[t, rows], m.GX.at[t, rows], m.s_gx.at[i], m.r_gx.at[i], near_me(1))
+
+    def turn_weights():
+        m.UpT[...] = m.Upc[...].T
+        m.OutT[...] = m.Out[...].reshape(D, D).T
+
+    ffn = feed(m.N1all, (m.s_n, m.r_n), expand, lambda blocks: dot(take(m.Gs, blocks), m.Dn[...]), m.Fs, m.Fr,
+               (m.s_f, m.r_f), turn_weights)
     n2, r2 = norm_stats(m.N1f[...] + ffn + vec(DOWNB))
     m.n2[...] = n2
     y_ref[...] = (n2 * vec(GAIN2) + vec(SHIFT2)).astype(BF)
@@ -611,53 +709,79 @@
     d_r2 = norm_back(dy, n2, r2, vec(GAIN2))
     m.dR2[...] = d_r2
     m.dFall[w] = d_r2.astype(BF)
-    gather_start(m.dFall, m.s_df, m.r_df)
-    m.gv[2:3, :] = col_sum(dy * n2)
-    m.gv[3:4, :] = col_sum(dy)
-    m.gv[5:6, :] = col_sum(m.dFall[w].astype(F32))
-
-    def shrink(t):
-        m.dHs[t] = (dot_nt(m.dFall[t], m.Dn[...]) * m.Hp[t]).astype(BF)
-
-    shrink(w)
-    for k in (1, 2, 3):
-        gather_wait(m.dFall, m.s_df, m.r_df, k)
-        shrink(jnp.bitwise_xor(w, k))
+
+    def shrink(blocks):
+        put(m.dHs, blocks, dot(take(m.dFall, blocks), m.DnT[...]) * take(m.Hp, blocks))
 
     def flat(ref):
         return ref[...].reshape(Q, ref.shape[-1])
 
-    def put_grad(name, plain, lhs, rhs, parts, lead=0):
+    def put_grad(name, plain, lhs, rhs, parts):
         rows = lhs.shape[-1] // parts
         for i in range(parts):
             val = dot_tn(lhs[:, :, i * rows : (i + 1) * rows].reshape(Q, rows), flat(rhs)).astype(BF)
             if cfg.fused:
                 _, ch, cols, _ = cfg.grads[name]
-                n = (rows - lead) // (4 * ch)
-                getattr(m, "G" + name)[i * n : (i + 1) * n] = val[lead:].reshape(n, 2, 2, ch, cols)
+                n = rows // (4 * ch)
+                getattr(m, "G" + name)[i * n : (i + 1) * n] = val.reshape(n, 2, 2, ch, cols)
             else:
                 plain[i * rows : (i + 1) * rows, :] = val
 
     pump = Sums(cfg, m, c, w, send, arrive)
 
+    side = lax.rem(c, 2)
+
+    def half_cols(side):
+        return pl.ds(pl.multiple_of(side * (D // 2), 128), D // 2)
+
+    def down_half():
+        for i, k in enumerate((0, 2)):
+            rows = m.DX.at[jnp.bitwise_xor(w, k)]
+            arrive(rows, m.r_fx.at[i])
+            send(rows, rows, m.s_fx.at[2 + i], m.r_fx.at[2 + i], peer(1))
+        for i, (t, rows) in enumerate(activated):
+            arrive(m.GX.at[t, rows], m.r_gx.at[i])
+        for i, k in enumerate((1, 3)):
+            arrive(m.DX.at[jnp.bitwise_xor(w, k)], m.r_fx.at[2 + i])
+        pieces, ch, cols, _ = cfg.grads["down"]
+        n = cfg.FW // 2
+        here = m.dFall[:, :, half_cols(side)].reshape(Q, cols)
+        there = flat(m.DX)
+        for i in range(2):
+            at = slice(i * n, (i + 1) * n)
+            val = dot_tn(m.Gs[:, :, at].reshape(Q, n), here) + dot_tn(m.GX[:, :, at].reshape(Q, n), there)
+            m.Gdown[i * (pieces // 2) : (i + 1) * (pieces // 2)] = val.astype(BF).reshape(pieces // 2, 2, ch, cols)
+
     def early():
-        put_grad("down", gdown_ref, m.Gs, m.dFall, 2)
-        pump.start(("down",))
+        if cfg.fused:
+            for i, k in enumerate((0, 2)):
+                t = jnp.bitwise_xor(w, k)
+                send(m.dFall.at[t, :, half_cols(1 - side)], m.DX.at[t], m.s_fx.at[i], m.r_fx.at[i], near_me(1))
+        else:
+            put_grad("down", gdown_ref, m.Gs, m.dFall, 2)
+        pump.run("early")
 
     def late():
+        m.gv[2:3, :] = col_sum(dy * n2)
+        m.gv[3:4, :] = col_sum(dy)
+        m.gv[5:6, :] = col_sum(m.dFall[w].astype(F32))
         put_grad("up", gup_ref, m.N1all, m.dHs, 2)
         m.gv[6:7, :] = col_sum(flat(m.dHs).astype(F32))
         pump.run("norm")
 
-    d_n1 = scatter_sum(
-        lambda t: dot_nt(m.dHs[t], m.Upc[...]), m.dNs, m.dNr, m.s_dn, m.r_dn, early, late) + m.dR2[...]
+    def turn_projection():
+        m.WcT[...] = m.Wc[...].T
+
+    d_n1 = feed(m.dFall, (m.s_df, m.r_df), shrink, lambda blocks: dot(take(m.dHs, blocks), m.UpT[...]), m.dNs, m.dNr,
+                (m.s_dn, m.r_dn), turn_projection, early, late) + m.dR2[...]
     n1 = m.n1[...]
     d_r1 = norm_back(d_n1, n1, m.r1[...], vec(GAIN1))
     m.dR1[...] = d_r1
     d_a = d_r1.astype(BF)
     m.dAall[w] = d_a
+    d_mixed = dot(d_a, m.OutT[...])
     for g in range(W):
-        m.dOs[g] = dot_nt(d_a, m.Outp[g]).astype(BF)
+        pack(m.dOs.at[g], d_mixed[:, g * DW : (g + 1) * DW])
         dev = att_device(w, g, block_part)
         send(m.dOs.at[g], m.dOr.at[block_slot], m.s_do.at[g], m.r_do.at[block_slot], dev,
              jnp.logical_not(is_me(dev)))
@@ -666,25 +790,44 @@
         def _():
             m.dOr[block_slot] = m.dOs[g]
 
-    pump.start(("up",))
+    pump.run("sent")
     gather_start(m.dAall, m.s_da, m.r_da)
     for k in (2, 3, 1):
         send(m.Mix.at[jnp.bitwise_xor(w, k)], m.MixT.at[w], m.s_mt.at[k], m.r_mt.at[k], peer(k))
+    if cfg.fused:
+        down_half()
+    pump.run("down")
     m.MixT[w] = m.Mix[w]
     m.gv[0:1, :] = col_sum(d_n1 * n1)
     m.gv[1:2, :] = col_sum(d_n1)
     m.gv[4:5, :] = col_sum(d_a.astype(F32))
 
+    m.wide[...] = jnp.zeros(m.wide.shape, BF)
+
+    def weights_again(chunk, h):
+        rows = pl.ds(pl.multiple_of(chunk * KC, KC), KC)
+        scores = dot_nt(m.KV[rows, 0:DP], m.Qm[h])
+        return jnp.where(alive(chunk), jnp.exp(scores - m.lrow[h : h + 1, :]), 0.0)
+
+    if cfg.keep:
+
+        def keep(chunk, carry):
+            for h in range(HW):
+                m.Pm[h, pl.ds(pl.multiple_of(chunk * KC, KC), KC), :] = weights_again(chunk, h)
+            return carry
+
+        lax.fori_loop(0, R * PER_SET, keep, 0)
     for j in range(W):
         pump.run("sent%d" % j)
         arrive(m.dOr.at[j], m.r_do.at[j], jnp.logical_not(is_me((j * R + r_att, s))))
-        d_o = m.dOr[j]
+        unpack(m.wide, OFF, m.dOr.at[j])
+        d_o = m.wide[...]
         cols = slice(j * B, (j + 1) * B)
         for h in range(HW):
             m.Dm[h, cols, :] = jnp.where(v_lane(h), d_o, jnp.zeros_like(d_o))
-        prod = m.OT[:, cols] * d_o.astype(F32).T
+        prod = m.OT[:, cols] * d_o.astype(F32).T[OFF:DP, :]
         for h in range(HW):
-            m.drow[h : h + 1, cols] = col_sum(prod[OFF + h * HEAD : OFF + (h + 1) * HEAD, :])
+            m.drow[h : h + 1, cols] = col_sum(prod[h * HEAD : (h + 1) * HEAD, :])
     m.dQT[...] = jnp.zeros(m.dQT.shape, F32)
     pump.run("arrived")
 
@@ -694,12 +837,10 @@
         keys = m.KV[rows, 0:DP]
         values = m.KV[rows, KVW - DP : KVW]
         keys_t = keys.T
-        live = alive(chunk)
         d_k = jnp.zeros((KC, DP), F32)
         d_v = jnp.zeros((KC, DP), F32)
         for h in range(HW):
-            scores = dot_nt(keys, m.Qm[h])
-            prob = jnp.where(live, jnp.exp(scores - m.lrow[h : h + 1, :]), 0.0)
+            prob = m.Pm[h, rows, :] if cfg.keep else weights_again(chunk, h)
             d_prob = dot_nt(values, m.Dm[h])
             d_s = (prob * (d_prob - m.drow[h : h + 1, :])).astype(BF)
             d_k = d_k + dot(d_s, m.Qm[h])
@@ -730,37 +871,42 @@
         d_kv = m.dKVf[j * B : (j + 1) * B, :]
         for k in range(1, R):
             d_kv = d_kv + m.dKVr[k - 1, j * B : (j + 1) * B, :].astype(F32)
-        m.dqs[j, :, 0:KVW] = d_kv.astype(BF)
-        d_q = m.dQT[:, j * B : (j + 1) * B].T * (HEAD**-0.5)
-        m.dqs[j, :, KVW:MW] = jnp.where(lanes < DW, d_q, 0.0).astype(BF)
+        m.dKVo[j] = d_kv.astype(BF)
+        pack(m.dQs.at[j], m.dQT[:, j * B : (j + 1) * B].T * (HEAD**-0.5))
         dev = (j * R + r_att, g_att)
-        send(m.dqs.at[j], m.dqr.at[s], m.s_dq.at[j], m.r_dq.at[s], dev, jnp.logical_not(is_me(dev)))
+        away = jnp.logical_not(is_me(dev))
+        send(m.dKVo.at[j], m.dqr.at[s, :, pl.ds(0, KVW)], m.s_dk.at[j], m.r_dk.at[s], dev, away)
+        send(m.dQs.at[j], m.dQr.at[s], m.s_dq.at[j], m.r_dq.at[s], dev, away)
 
         @pl.when(is_me(dev))
         def _():
-            m.dqr[s] = m.dqs[j]
+            m.dqr[s, :, 0:KVW] = m.dKVo[j]
+            m.dQr[s] = m.dQs[j]
 
     for k in (1, 2, 3):
         pump.run("dq%d" % k)
         gather_wait(m.dAall, m.s_da, m.r_da, k)
         arrive(m.MixT.at[jnp.bitwise_xor(w, k)], m.r_mt.at[k])
-    put_grad("out", gout_ref, m.MixT, m.dAall, 1, OFF)
-    pump.start(("out",))
+    for t in range(W):
+        unpack(m.Mt.at[t], 0, m.MixT.at[t])
+        m.dqr[t, :, KVW + DW : MW] = jnp.zeros((B, MW - KVW - DW), BF)
+    put_grad("out", gout_ref, m.Mt, m.dAall, 1)
     pump.run("out")
 
     for t in range(W):
         pump.run("wait%d" % t)
-        arrive(m.dqr.at[t], m.r_dq.at[t], jnp.logical_not(is_me(att_device(t, w, block_part))))
-
+        away = jnp.logical_not(is_me(att_device(t, w, block_part)))
+        arrive(m.dqr.at[t, :, pl.ds(0, KVW)], m.r_dk.at[t], away)
+        arrive(m.dQr.at[t], m.r_dq.at[t], away)
+        unpack(m.dqr.at[t], KVW, m.dQr.at[t])
     put_grad("qkv", gqkv_ref, m.Xall, m.dqr, 2)
-    pump.start(("qkv",))
     pump.run("qkv")
 
     m.gv[7:8, 0:MW] = col_sum(flat(m.dqr).astype(F32))
     m.gv[7:8, MW:D] = jnp.zeros((1, D - MW), F32)
 
     def d_x(t):
-        return dot_nt(m.dqr[t], m.Wc[...])
+        return dot(m.dqr[t], m.WcT[...])
 
     token_steps = scatter_steps(d_x, m.dxs, m.dxr, m.s_dx, m.r_dx)
 
@@ -801,7 +947,8 @@
         gvec_ref[0] = m.gv[...]
     else:
         vector_steps = [functools.partial(vectors, i) for i in range(3)] + [vectors_to_rows, vectors_end]
-        pump.finish(("qkv", "out", "up", "down"), [token_steps[0], vector_steps[0], token_steps[1]] + vector_steps[1:], 3)
+        pump.run("tail", dict(tokens=token_steps, vectors=vector_steps))
+        pump.finish()
         d_x_sum = token_steps[2]()
     gx_ref[...] = (m.dR1[...] + d_x_sum).astype(BF)
 
@@ -823,7 +970,8 @@
     R = C // W
     cfg = SimpleNamespace(C=C, W=W, B=B, D=D, FW=FW, DW=DW, DP=DP, KVW=KVW, MW=MW, R=R, HW=HEADS // W)
     cfg.fused = R == 2 and C == 8 and DW % 64 == 0 and FW % (64 * W) == 0
-    cfg.grads = dict(down=(W, FW // W // 4, D, False), up=(W, DW // 4, FW, True), qkv=(W, DW // 4, MW, True),
+    cfg.keep = R == 2
+    cfg.grads = dict(down=(W, FW // W // 2, D // 2, False), up=(W, DW // 4, FW, True), qkv=(W, DW // 4, MW, True),
                      out=(1, DW // 4, D, False))
     w = lax.axis_index("wa")
     small = (out_bias, down_bias, gain_one, shift_one, gain_two, shift_two, qv_bias, up_bias)
@@ -836,7 +984,7 @@
         outs = [(n, 2, 2, ch, cols) for n, ch, cols, _ in (cfg.grads[k] for k in ("qkv", "out", "up", "down"))]
         place = pltpu.VMEM
     else:
-        outs = [(D, MW), (DP, D), (D, FW), (FW, D)]
+        outs = [(D, MW), (DW, D), (D, FW), (FW, D)]
         place = jax.ShapeDtypeStruct
     outs = [place(a, BF) for a in [(B, D), (B, D)] + outs] + [place((GROWS, D) if cfg.fused else (1, GROWS, D), F32)]
     args = (tokens.reshape(B, D), cotangent.reshape(B, D), qkv_weight, out_weight, up_weight, down_weight, lengths, *small)
@@ -865,7 +1013,7 @@
     g_upb = lax.dynamic_slice_in_dim(gvec, w, 1, 0)[0, 6]
     g_qv = jnp.concatenate([gvec[:, 7, KVW : KVW + DW].reshape(D), gvec[:, 7, DW:KVW].reshape(D)])
     g_qv = lax.dynamic_slice_in_dim(g_qv, w * (2 * D // W), 2 * D // W)
-    return (y.reshape(1, B, D), gx.reshape(1, B, D), gqkv, gout[DP - DW :].astype(F32), gup.astype(F32),
+    return (y.reshape(1, B, D), gx.reshape(1, B, D), gqkv, gout.astype(F32), gup.astype(F32),
             gdown.astype(F32), g_qv, own[4], g_upb, own[5], own[0], own[1], own[2], own[3])
 
 
@@ -880,7 +1028,8 @@
             o_qkv[:, third * D + g * DW : third * D + (g + 1) * DW] = rows[:, a : a + DW]
         o_up[:, g * cfg.FW : (g + 1) * cfg.FW] = gup[g].reshape(DW, cfg.FW).astype(F32)
     o_out[...] = gout[...].reshape(o_out.shape).astype(F32)
-    o_down[...] = gdown[...].reshape(o_down.shape).astype(F32)
+    for x in range(2):
+        o_down[:, x * (D // 2) : (x + 1) * (D // 2)] = gdown[:, x].reshape(cfg.FW, D // 2).astype(F32)
     o_qv[...] = gvec[6, 0 : 2 * DW]
     o_upb[...] = gvec[7, 0 : cfg.FW]
     for row, ref in enumerate((o_g1, o_s1, o_g2, o_s2, o_outb, o_downb)):

time: 185 us -> 174 us (0.941)
  Pallas kernels: 183 us -> 172 us
    pallas_call x1, Pallas kernels: 180 us -> 168 us  [body(): pl.pallas_call(functools.partial(layer_kernel, cfg, names, len(args)), ou...]
where the time goes in v4:
time: 174 us; the launch traced here: 173 us
  Pallas kernels  172 us (99%)
    pallas_call x1, Pallas kernels, body(): pl.pallas_call(functools.partial(layer_kernel, cfg, names, len(args)), ou...  168 us

profile of v4, /device:TPU:0, one launch (start us, length us, event | category | flops | bytes accessed | tf_op | source)
XLA Modules:
  0.0 173.0 jit_solution(1233964792856359744)
XLA Ops:
  1.3 168.2 %layer.1 = (bf16[128,768]{1,0:T(8,128)(2,1)S(1)}, bf16[128,768]{1,0:T(8,128)(2,1)S(1)}, bf16[4,2,2,48,640]{4,3,2,1,0:T(8,128)(2,1)S(1)}, bf16[1,2,2,48,768]{4,3,...) custom-call(bf16[128,768]{1,0:T(8,128)(2,1)} %bitcast.2, ...), custom_call_target="tpu_custom_call" | custom-call | tf_op jit(solution)/shard_map/layer/pallas_call | solution.py:991
  169.5 3.3 %results.1 = (bf16[1,128,768]{2,1,0:T(8,128)(2,1)}, bf16[1,128,768]{2,1,0:T(8,128)(2,1)}, f32[192,2304]{1,0:T(8,128)}, f32[192,768]{1,0:T(8,128)}, f32[192,3072]...) custom-call(bf16[128,768]{1,0:T(8,128)(2,1)S(1)} %get-tuple-element., ...), custom_call_target="tpu_custom_call" | custom-call | tf_op jit(solution)/shard_map/results/pallas_call | solution.py:1044

commit v5 on v4

--- a/solution.py
+++ b/solution.py
@@ -25,10 +25,10 @@
 ALL = (0, 1, 2, 3)
 SCHEDULE = dict(
     early=(),
-    norm=(
+    norm=(),
+    sent=(
         (1, "up", 0), (1, "up", 1), (1, "up", 2), (1, "up", 3),
     ),
-    sent=(),
     down=(
         (1, "down", 0), (1, "down", 1), (1, "down", 2), (1, "down", 3), (2, "down", 0), (2, "down", 1),
         (2, "down", 2), (2, "down", 3),
@@ -36,33 +36,31 @@
     sent0=(
         (3, "down", 0),
     ),
-    sent1=(
-        (3, "down", 1),
-    ),
-    sent2=(
-        (3, "down", 2),
-    ),
+    sent1=(),
+    sent2=(),
     sent3=(
-        (3, "down", 3),
+        (4, "down", 0),
     ),
     arrived=(
-        (2, "up", 0), (4, "down", 0), (5, "down", 0),
+        (5, "down", 0), (3, "down", 1), (2, "up", 0),
     ),
     between=(
-        (4, "down", 1), (5, "down", 1), (2, "up", 1),
+        (3, "down", 2), (2, "up", 1),
     ),
     after=(
-        (4, "down", 2), (5, "down", 2), (3, "up", 0), (2, "up", 2),
+        (4, "down", 1), (3, "down", 3), (3, "up", 0), (2, "up", 2),
     ),
     part=(),
     dq1=(),
     dq2=(),
-    dq3=(),
+    dq3=(
+        (6, "down", 0),
+    ),
     out=(
-        (1, "out", 0), (6, "down", 0), (3, "up", 1), (2, "up", 3),
+        (1, "out", 0), (5, "down", 1), (4, "down", 2), (3, "up", 1), (2, "up", 3),
     ),
     wait0=(
-        (4, "down", 3), (4, "up", 0), (3, "up", 2),
+        (5, "down", 2), (4, "down", 3), (4, "up", 0), (3, "up", 2),
     ),
     wait1=(
         (6, "down", 1), (5, "down", 3), (4, "up", 1), (3, "up", 3),
@@ -72,15 +70,15 @@
         (5, "up", 0),
     ),
     qkv=(
-        (1, "qkv", 0), (1, "qkv", 1), (1, "qkv", 2), (1, "qkv", 3), (6, "down", 2), (6, "down", 3),
-        (6, "up", 0), (4, "up", 2), (4, "up", 3), (2, "qkv", 0), (2, "out", 0),
+        (1, "qkv", 0), (1, "qkv", 1), (1, "qkv", 2), (1, "qkv", 3), (6, "down", 2), (6, "up", 0),
+        (4, "up", 2), (4, "up", 3), (2, "qkv", 0), (2, "out", 0),
     ),
     tail=(
-        (5, "up", 1), (3, "qkv", 0), (0, "tokens", 0), (3, "out", 0), (2, "qkv", 1), (6, "up", 1),
-        (0, "vectors", 0), (5, "up", 2), (4, "qkv", 0), (4, "out", 0), (1, "tokens", 0), (3, "qkv", 1),
-        (2, "qkv", 2), (6, "up", 2), (1, "vectors", 0), (5, "out", 0), (5, "up", 3), (4, "qkv", 1),
-        (2, "vectors", 0), (3, "qkv", 2), (2, "qkv", 3), (6, "out", 0), (3, "vectors", 0), (6, "up", 3),
-        (4, "qkv", 2), (3, "qkv", 3), (4, "vectors", 0), (4, "qkv", 3),
+        (6, "down", 3), (5, "up", 1), (3, "qkv", 0), (0, "tokens", 0), (3, "out", 0), (2, "qkv", 1),
+        (6, "up", 1), (0, "vectors", 0), (5, "up", 2), (4, "qkv", 0), (4, "out", 0), (1, "tokens", 0),
+        (3, "qkv", 1), (2, "qkv", 2), (6, "up", 2), (1, "vectors", 0), (5, "out", 0), (5, "up", 3),
+        (4, "qkv", 1), (2, "vectors", 0), (3, "qkv", 2), (2, "qkv", 3), (6, "out", 0), (3, "vectors", 0),
+        (6, "up", 3), (4, "qkv", 2), (3, "qkv", 3), (4, "vectors", 0), (4, "qkv", 3),
     ),
 )
 
@@ -152,15 +150,15 @@
         for name, (pieces, ch, cols, to_rows) in cfg.grads.items():
             plan["G" + name] = V((pieces, 2, ch, cols) if name == "down" else (pieces, 2, 2, ch, cols), BF)
             plan["X" + name] = V((pieces, 3, ch, cols), BF)
-            plan["T" + name] = V((pieces, ch, cols), BF)
-            plan["Y" + name] = V((pieces, ch, cols), BF)
-            plan["U" + name] = V((pieces, ch, cols), BF)
-            plan["Z" + name] = V((pieces, ch, cols), BF)
+            plan["T" + name] = V((pieces, 2, ch, cols), BF)
+            plan["Y" + name] = V((pieces, 2, ch, cols), BF)
+            plan["U" + name] = V((pieces, 2, ch, cols), BF)
+            plan["Z" + name] = V((pieces, 2, ch, cols), BF)
             for kind in ("g1", "g2", "g3", "g4", "g5", "g6"):
                 sems[kind + name] = 3 * pieces
                 recvs[kind + name] = 3 * pieces
             if to_rows:
-                plan["R" + name] = V((pieces, ch, cols), BF)
+                plan["R" + name] = V((pieces, 2, ch, cols), BF)
         plan.update(Va=V((4, GROWS, D), F32), Vb=V((3, GROWS, D), F32), Vt=V((W, GROWS, DW), F32),
                     Vw=V((W, GROWS, DW), F32))
         sems.update(v1=3, vw=W)
@@ -177,9 +175,12 @@
         self.cfg, self.m, self.c, self.w, self.send, self.arrive = cfg, m, c, w, send, arrive
         self.x, self.near = lax.rem(c, 2), lax.rem(lax.div(c, 2), 2)
         self.partners = [(jnp.bitwise_xor(c, k), w) for k in (1, 2, 4, 3)]
+        self.other_middle = (jnp.bitwise_xor(c, 6), w)
+        self.middle = self.near != lax.div(c, 4)
+        self.end = jnp.logical_not(self.middle)
         self.long = (self.one, self.two, self.three, self.four, self.five, self.six, self.seven)
-        self.halved = (self.nothing, self.pass_on, self.join) + self.long[3:]
-        self.short = (self.quarters, self.quarters_sum, self.four, self.spread, self.spread_end)
+        self.halved = (self.nothing,) + self.long[1:]
+        self.short = (self.quarters, self.quarters_sum, self.quarters_total, self.spread, self.spread_end)
 
     def stages(self, name):
         if name == "down":
@@ -207,11 +208,11 @@
     def ref(self, kind, name):
         return getattr(self.m, kind + name)
 
-    def go(self, kind, name, p, src, dst, dev):
-        self.send(src, dst, self.ref("s_" + kind, name).at[p], self.ref("r_" + kind, name).at[p], dev)
-
-    def got(self, kind, name, p, dst):
-        self.arrive(dst, self.ref("r_" + kind, name).at[p])
+    def go(self, kind, name, p, src, dst, dev, pred=None):
+        self.send(src, dst, self.ref("s_" + kind, name).at[p], self.ref("r_" + kind, name).at[p], dev, pred)
+
+    def got(self, kind, name, p, dst, pred=None):
+        self.arrive(dst, self.ref("r_" + kind, name).at[p], pred)
 
     def piece(self, name, k):
         return jnp.bitwise_xor(self.w, k) if self.cfg.grads[name][3] else k
@@ -219,15 +220,12 @@
     def nothing(self, name, k):
         pass
 
-    def pass_on(self, name, k):
-        g = self.ref("G", name).at[k, 1 - self.near]
-        self.go("g2", name, k, g, self.ref("Y", name).at[k], self.partners[1])
-
-    def join(self, name, k):
-        y, u = self.ref("Y", name), self.ref("U", name)
-        self.got("g2", name, k, y.at[k])
-        u[k] = (self.ref("G", name)[k, self.near].astype(F32) + y[k].astype(F32)).astype(BF)
-        self.go("g3", name, k, u.at[k], self.ref("Z", name).at[k], self.partners[2])
+    def half(self, name, k):
+        if name == "down":
+            return self.ref("G", name)[k].astype(F32)
+        other = self.ref("X", name).at[k, pl.ds(0, 2)]
+        self.got("g1", name, k, other)
+        return self.ref("G", name)[self.piece(name, k), self.x].astype(F32) + other[...].astype(F32)
 
     def one(self, name, k):
         p = self.piece(name, k)
@@ -235,49 +233,73 @@
                 self.partners[0])
 
     def two(self, name, k):
-        g, other, t = self.ref("G", name), self.ref("X", name), self.ref("T", name)
-        self.got("g1", name, k, other.at[k, pl.ds(0, 2)])
-        far = 1 - self.near
-        mine = g[self.piece(name, k), self.x, far].astype(F32)
-        t[k] = (mine + other[k, far].astype(F32)).astype(BF)
-        self.go("g2", name, k, t.at[k], self.ref("Y", name).at[k], self.partners[1])
+        t = self.ref("T", name)
+
+        @pl.when(self.end)
+        def _():
+            t[k] = self.half(name, k).astype(BF)
+
+        self.go("g2", name, k, t.at[k], self.ref("Y", name).at[k], self.partners[1], self.end)
 
     def three(self, name, k):
-        g, other, y, u = (self.ref(kind, name) for kind in "GXYU")
-        self.got("g2", name, k, y.at[k])
-        n = self.near
-        mine = g[self.piece(name, k), self.x, n].astype(F32)
-        u[k] = (mine + other[k, n].astype(F32) + y[k].astype(F32)).astype(BF)
-        self.go("g3", name, k, u.at[k], self.ref("Z", name).at[k], self.partners[2])
+        y, u = self.ref("Y", name), self.ref("U", name)
+
+        @pl.when(self.middle)
+        def _():
+            mine = self.half(name, k)
+            self.got("g2", name, k, y.at[k])
+            u[k] = (mine + y[k].astype(F32)).astype(BF)
+
+        self.go("g3", name, k, u.at[k], self.ref("Z", name).at[k], self.other_middle, self.middle)
 
     def four(self, name, k):
         u, z, fin = (self.ref(kind, name) for kind in "UZF")
-        self.got("g3", name, k, z.at[k])
-        total = (u[k].astype(F32) + z[k].astype(F32)).astype(BF)
+        away = self.cfg.grads[name][3] and k > 0
+
+        @pl.when(self.middle)
+        def _():
+            self.got("g3", name, k, z.at[k])
+            total = (u[k].astype(F32) + z[k].astype(F32)).astype(BF)
+            if away:
+                self.ref("R", name)[k] = total
+            else:
+                fin[self.piece(name, k), self.x] = total
+
+        if away:
+            self.go("g4", name, k, self.ref("R", name).at[k], fin.at[self.w, self.x],
+                    (self.c, jnp.bitwise_xor(self.w, k)), self.middle)
+
+    def five(self, name, k):
+        here = self.ref("F", name).at[self.piece(name, k), self.x]
+        if self.cfg.grads[name][3] and k > 0:
+            self.got("g4", name, k, here, self.middle)
+        self.go("g5", name, k, here, here, self.partners[1], self.middle)
+        self.go("g6", name, k, here, here, self.partners[0], self.middle)
+
+    def six(self, name, k):
+        here = self.ref("F", name).at[self.piece(name, k), self.x]
+        self.got("g5", name, k, here, self.end)
+        self.go("g6", name, k, here, here, self.partners[0], self.end)
+
+    def seven(self, name, k):
+        self.got("g6", name, k, self.ref("F", name).at[self.piece(name, k), 1 - self.x])
+
+    def quarters_total(self, name, k):
+        u, z, fin = (self.ref(kind, name) for kind in "UZF")
+        self.got("g3", name, k, z.at[k, 0])
+        total = (u[k, 0].astype(F32) + z[k, 0].astype(F32)).astype(BF)
         if not self.cfg.grads[name][3] or k == 0:
             fin[self.piece(name, k), self.x, self.near] = total
             return
         done = self.ref("R", name)
-        done[k] = total
-        self.go("g4", name, k, done.at[k], fin.at[self.w, self.x, self.near], (self.c, jnp.bitwise_xor(self.w, k)))
+        done[k, 0] = total
+        self.go("g4", name, k, done.at[k, 0], fin.at[self.w, self.x, self.near], (self.c, jnp.bitwise_xor(self.w, k)))
 
     def owned(self, name, k):
         here = self.ref("F", name).at[self.piece(name, k), self.x, self.near]
         if self.cfg.grads[name][3] and k > 0:
             self.got("g4", name, k, here)
         return here
-
-    def five(self, name, k):
-        here = self.owned(name, k)
-        self.go("g5", name, k, here, here, self.partners[1])
-
-    def six(self, name, k):
-        fin, p = self.ref("F", name), self.piece(name, k)
-        self.got("g5", name, k, fin.at[p, self.x, 1 - self.near])
-        self.go("g6", name, k, fin.at[p, self.x], fin.at[p, self.x], self.partners[0])
-
-    def seven(self, name, k):
-        self.got("g6", name, k, self.ref("F", name).at[self.piece(name, k), 1 - self.x])
 
     def three_others(self):
         x, n = self.x, self.near
@@ -295,8 +317,8 @@
             self.got("g1", name, 3 * k + i, other)
             total = total + other[...].astype(F32)
         u = self.ref("U", name)
-        u[k] = total.astype(BF)
-        self.go("g3", name, k, u.at[k], self.ref("Z", name).at[k], self.partners[2])
+        u[k, 0] = total.astype(BF)
+        self.go("g3", name, k, u.at[k, 0], self.ref("Z", name).at[k, 0], self.partners[2])
 
     def spread(self, name, k):
         here = self.owned(name, k)

time: 174 us -> 171 us (0.983)
  Pallas kernels: 172 us -> 169 us
    pallas_call x1, Pallas kernels: 168 us -> 166 us  [body(): pl.pallas_call(functools.partial(layer_kernel, cfg, names, len(args)), ou...]
where the time goes in v5:
time: 171 us
  Pallas kernels  169 us (99%)
    pallas_call x1, Pallas kernels, body(): pl.pallas_call(functools.partial(layer_kernel, cfg, names, len(args)), ou...  166 us

profile of v5, /device:TPU:0, one launch (start us, length us, event | category | flops | bytes accessed | tf_op | source)
XLA Modules:
  0.0 170.8 jit_solution(2233710953950506015)
XLA Ops:
  1.3 166.0 %layer.1 = (bf16[128,768]{1,0:T(8,128)(2,1)S(1)}, bf16[128,768]{1,0:T(8,128)(2,1)S(1)}, bf16[4,2,2,48,640]{4,3,2,1,0:T(8,128)(2,1)S(1)}, bf16[1,2,2,48,768]{4,3,...) custom-call(bf16[128,768]{1,0:T(8,128)(2,1)} %bitcast.2, ...), custom_call_target="tpu_custom_call" | custom-call | tf_op jit(solution)/shard_map/layer/pallas_call | solution.py:1013
  167.3 3.3 %results.1 = (bf16[1,128,768]{2,1,0:T(8,128)(2,1)}, bf16[1,128,768]{2,1,0:T(8,128)(2,1)}, f32[192,2304]{1,0:T(8,128)}, f32[192,768]{1,0:T(8,128)}, f32[192,3072]...) custom-call(bf16[128,768]{1,0:T(8,128)(2,1)S(1)} %get-tuple-element., ...), custom_call_target="tpu_custom_call" | custom-call | tf_op jit(solution)/shard_map/results/pallas_call | solution.py:1066

commit v6 on v5

--- a/solution.py
+++ b/solution.py
@@ -1040,22 +1040,31 @@
 
 
 def finish_kernel(cfg, y, gx, gqkv, gout, gup, gdown, gvec, o_y, o_gx, o_qkv, o_out, o_up, o_down, o_qv, o_outb, o_upb,
-                  o_downb, o_g1, o_s1, o_g2, o_s2):
+                  o_downb, o_g1, o_s1, o_g2, o_s2, f_qkv, f_out, f_up, f_down, sems):
     W, D, DW, MW, KVW = cfg.W, cfg.D, cfg.DW, cfg.MW, cfg.KVW
-    o_y[0] = y[...]
-    o_gx[0] = gx[...]
+    copies = [pltpu.make_async_copy(a, b, sems.at[i]) for i, (a, b) in enumerate(
+        ((f_down, o_down), (f_up, o_up), (f_qkv, o_qkv), (f_out, o_out)))]
+    for x in range(2):
+        f_down[:, x * (D // 2) : (x + 1) * (D // 2)] = gdown[:, x].reshape(cfg.FW, D // 2).astype(F32)
+    copies[0].start()
+    for g in range(W):
+        f_up[:, g * cfg.FW : (g + 1) * cfg.FW] = gup[g].reshape(DW, cfg.FW).astype(F32)
+    copies[1].start()
     for g in range(W):
         rows = gqkv[g].reshape(DW, MW).astype(F32)
         for third, a in enumerate((KVW, 0, DW)):
-            o_qkv[:, third * D + g * DW : third * D + (g + 1) * DW] = rows[:, a : a + DW]
-        o_up[:, g * cfg.FW : (g + 1) * cfg.FW] = gup[g].reshape(DW, cfg.FW).astype(F32)
-    o_out[...] = gout[...].reshape(o_out.shape).astype(F32)
-    for x in range(2):
-        o_down[:, x * (D // 2) : (x + 1) * (D // 2)] = gdown[:, x].reshape(cfg.FW, D // 2).astype(F32)
+            f_qkv[:, third * D + g * DW : third * D + (g + 1) * DW] = rows[:, a : a + DW]
+    copies[2].start()
+    f_out[...] = gout[...].reshape(f_out.shape).astype(F32)
+    copies[3].start()
+    o_y[0] = y[...]
+    o_gx[0] = gx[...]
     o_qv[...] = gvec[6, 0 : 2 * DW]
     o_upb[...] = gvec[7, 0 : cfg.FW]
     for row, ref in enumerate((o_g1, o_s1, o_g2, o_s2, o_outb, o_downb)):
         ref[...] = gvec[row, 0:DW]
+    for cp in copies:
+        cp.wait()
 
 
 def finish(cfg, *arrays):
@@ -1067,7 +1076,8 @@
         functools.partial(finish_kernel, cfg),
         out_shape=[jax.ShapeDtypeStruct(s, BF if i < 2 else F32) for i, s in enumerate(shapes)],
         in_specs=[vm] * len(arrays),
-        out_specs=[vm] * len(shapes),
+        out_specs=[vm] * 2 + [pl.BlockSpec(memory_space=pl.ANY)] * 4 + [vm] * 8,
+        scratch_shapes=[pltpu.VMEM(s, F32) for s in shapes[2:6]] + [pltpu.SemaphoreType.DMA((4,))],
         compiler_params=pltpu.CompilerParams(vmem_limit_bytes=32 << 20),
         name="results",
     )(*arrays)

time: 171 us -> 172 us (level)
  no operation moved by 1% of the time
where the time goes in v6:
time: 172 us
  Pallas kernels  170 us (99%)
    pallas_call x1, Pallas kernels, body(): pl.pallas_call(functools.partial(layer_kernel, cfg, names, len(args)), ou...  166 us
    pallas_call x1, Pallas kernels, finish(): pl.pallas_call(functools.partial(finish_kernel, cfg), out_shape=[jax.Shap...  4.05 us

profile of v6, /device:TPU:0, one launch (start us, length us, event | category | flops | bytes accessed | tf_op | source)
XLA Modules:
  0.0 171.5 jit_solution(6475693831234781271)
XLA Ops:
  1.3 166.0 %layer.1 = (bf16[128,768]{1,0:T(8,128)(2,1)S(1)}, bf16[128,768]{1,0:T(8,128)(2,1)S(1)}, bf16[4,2,2,48,640]{4,3,2,1,0:T(8,128)(2,1)S(1)}, bf16[1,2,2,48,768]{4,3,...) custom-call(bf16[128,768]{1,0:T(8,128)(2,1)} %bitcast.2, ...), custom_call_target="tpu_custom_call" | custom-call | tf_op jit(solution)/shard_map/layer/pallas_call | solution.py:1013
  167.3 4.1 %results.1 = (bf16[1,128,768]{2,1,0:T(8,128)(2,1)}, bf16[1,128,768]{2,1,0:T(8,128)(2,1)}, f32[192,2304]{1,0:T(8,128)}, f32[192,768]{1,0:T(8,128)}, f32[192,3072]...) custom-call(bf16[128,768]{1,0:T(8,128)(2,1)S(1)} %get-tuple-element., ...), custom_call_target="tpu_custom_call" | custom-call | tf_op jit(solution)/shard_map/results/pallas_call | solution.py:1075
